TPU v7x, 256 devices: a whole 4x4x8 slice. The times are simulated.
256 devices in a mesh: tm: 16 (over z_hi, y), gx: 4 (over z_lo, core), gy: 4 (over x).
Axes of the slice: x: 4, y: 4, z: 8 (z_hi: 4, z_lo: 2; z = z_hi * 2 + z_lo), core: 2. Of those that a mesh axis runs over, the one named last changes fastest.
Arguments:
- provisional: float32 [16, 3, 3, 16, 64, 1024], P('tm', None, None, None, 'gx', 'gy'), may hold values from -1.5 to 1.5
Outputs:
- corrected: float32 [16, 3, 3, 16, 64, 1024], P('tm', None, None, None, 'gx', 'gy')
All inputs are finite; a program needn't handle non-finite values.
Results may differ from a plain program's by a relative error of at most 0.00002.
Values sent between devices are 32-bit elements; how exact they have to be, the bound alone decides.
No kernel may reach another device: no remote copies, remote signals or barrier semaphores. Data moves between devices by JAX's collectives and lax.ppermute only.
A program may use at most 64 MiB of HBM per device.

v0:
```python
import jax
import jax.numpy as jnp
from jax import lax
from jax.sharding import PartitionSpec as P

viscosity = 0.1
slice_step = 0.25
half_step = 0.125
first_row = (5.0 / 24.0, 1.0 / 3.0, -1.0 / 24.0)
second_row = (-1.0 / 24.0, 1.0 / 3.0, 5.0 / 24.0)


def padded_2(block, sides, width):
    for axis, dim in sides:
        count = lax.axis_size(axis)
        forward = [(i, i + 1) for i in range(count - 1)]
        backward = [(target, source) for source, target in forward]
        low = lax.ppermute(
            lax.slice_in_dim(block, block.shape[dim] - width, None, axis=dim), axis, forward
        )
        high = lax.ppermute(lax.slice_in_dim(block, 0, width, axis=dim), axis, backward)
        block = jnp.concatenate([low, block, high], axis=dim)
    return block


def passed_along(block, axis, distance):
    devices = range(lax.axis_size(axis))
    route = [(i - distance, i) for i in devices if i - distance in devices]
    return lax.ppermute(block, axis, route)


def tendency(padded, spacing):
    centre = padded[:, :, 1:-1, 1:-1]
    east_side = padded[:, :, 2:, 1:-1]
    west_side = padded[:, :, :-2, 1:-1]
    north_side = padded[:, :, 1:-1, 2:]
    south_side = padded[:, :, 1:-1, :-2]
    upper_side = jnp.roll(centre, -1, axis=1)
    lower_side = jnp.roll(centre, 1, axis=1)
    change_first = 0.5 * (east_side - west_side)
    change_second = 0.5 / spacing * (north_side - south_side)
    change_third = 0.5 * (upper_side - lower_side)
    laplace = (
        east_side
        + west_side
        - 2.0 * centre
        + (north_side + south_side - 2.0 * centre) / (spacing * spacing)
        + (upper_side + lower_side - 2.0 * centre)
    )
    transport = (
        centre[0:1] * change_first + centre[1:2] * change_second + centre[2:3] * change_third
    )
    return viscosity * laplace - transport


def quadrature(values, weights):
    return slice_step * (weights[0] * values[0] + weights[1] * values[1] + weights[2] * values[2])


def restrict(field):
    return 0.5 * (field[..., 0::2] + field[..., 1::2])


def prolong(field):
    return jnp.repeat(field, 2, axis=-1)


def per_device(provisional):
    states = provisional[0]
    start_node = states[0]
    middle_node = states[1]
    final_node = states[2]
    padded_start, padded_middle, padded_final = (
        padded_2(start_node, (("gx", 2), ("gy", 3)), 1),
        padded_2(middle_node, (("gx", 2), ("gy", 3)), 1),
        padded_2(final_node, (("gx", 2), ("gy", 3)), 1),
    )
    old_fluxes = (
        tendency(padded_start, 1.0),
        tendency(padded_middle, 1.0),
        tendency(padded_final, 1.0),
    )
    new_middle = start_node + quadrature(old_fluxes, first_row)
    slope_middle = tendency(padded_2(new_middle, (("gx", 2), ("gy", 3)), 1), 1.0)
    new_final = (
        new_middle + half_step * (slope_middle - old_fluxes[1]) + quadrature(old_fluxes, second_row)
    )
    slope_final = tendency(padded_2(new_final, (("gx", 2), ("gy", 3)), 1), 1.0)
    coarse_start = restrict(start_node)
    coarse_middle = restrict(new_middle)
    coarse_final = restrict(new_final)
    new_fluxes = (old_fluxes[0], slope_middle, slope_final)
    integral_first = restrict(quadrature(new_fluxes, first_row))
    integral_second = restrict(quadrature(new_fluxes, second_row))
    leader = lax.axis_index("tm") == 0
    around_start, around_middle = (
        padded_2(coarse_start, (("gx", 2), ("gy", 3)), 1),
        padded_2(coarse_middle, (("gx", 2), ("gy", 3)), 1),
    )
    base_start = tendency(around_start, 2.0)
    base_middle = tendency(around_middle, 2.0)

    def coarse_sweep(chain_start):
        chain_middle = (
            chain_start
            + half_step
            * (tendency(padded_2(chain_start, (("gx", 2), ("gy", 3)), 1), 2.0) - base_start)
            + integral_first
        )
        chain_final = (
            chain_middle
            + half_step
            * (tendency(padded_2(chain_middle, (("gx", 2), ("gy", 3)), 1), 2.0) - base_middle)
            + integral_second
        )
        return (chain_middle, chain_final)

    def advance(rounds, chain_start):
        chain_middle, chain_final = coarse_sweep(chain_start)
        arrived = passed_along(chain_final, "tm", 1)
        return jnp.where(leader, coarse_start, arrived)

    chain_start = lax.fori_loop(0, lax.axis_size("tm") - 1, advance, coarse_start)
    chain_middle, chain_final = coarse_sweep(chain_start)
    out_middle = new_middle + prolong(chain_middle - coarse_middle)
    out_final = new_final + prolong(chain_final - coarse_final)
    out_start = jnp.where(leader, start_node, passed_along(out_final, "tm", 1))
    return jnp.stack([out_start, out_middle, out_final])[None]


def solution(mesh):
    in_specs = (P("tm", None, None, None, "gx", "gy"),)
    out_specs = P("tm", None, None, None, "gx", "gy")
    return jax.shard_map(
        per_device, mesh=mesh, in_specs=in_specs, out_specs=out_specs, check_vma=False
    )
```

profile of v0, /device:TPU:130, one launch (start us, length us, event | category | flops | bytes accessed | tf_op | source)
XLA Modules:
  0.0 1379.7 jit_solution(8977352889845136328)
XLA Ops:
  7.7 13.4 slice.670
  21.1 14.0 %slice.671 = f32[3,16,16,128]{3,2,1,0:T(8,128)} slice(f32[3,16,16,256]{3,2,1,0:T(8,128)S(1)} %get-tuple-element.136), slice={[0:3:1], [0:16:1], [0:16:1], [1:256:2]} | slice | bytes 786432 | tf_op jit(solution)/shard_map/slice | solution.py:61
  114.2 7.5 multiply_add_fusion.1
  121.7 13.4 slice.704
  135.1 13.4 slice.705
  180.6 7.1 collective-permute-done.23
  204.4 12.4 collective-permute-start.32
  216.9 14.0 %slice.753 = f32[3,16,16,128]{3,2,1,0:T(8,128)} slice(f32[3,16,16,256]{3,2,1,0:T(8,128)S(1)} %get-tuple-element.104), slice={[0:3:1], [0:16:1], [0:16:1], [0:256:2]} | slice | bytes 786432 | tf_op jit(solution)/shard_map/slice | solution.py:61
  230.9 14.0 %slice.754 = f32[3,16,16,128]{3,2,1,0:T(8,128)} slice(f32[3,16,16,256]{3,2,1,0:T(8,128)S(1)} %get-tuple-element.104), slice={[0:3:1], [0:16:1], [0:16:1], [1:256:2]} | slice | bytes 786432 | tf_op jit(solution)/shard_map/slice | solution.py:61
  251.2 14.2 %slice.702 = f32[3,16,16,128]{3,2,1,0:T(8,128)S(1)} slice(f32[3,16,16,256]{3,2,1,0:T(8,128)} %get-tuple-element.102), slice={[0:3:1], [0:16:1], [0:16:1], [0:256:2]} | slice | bytes 786432 | tf_op jit(solution)/shard_map/slice | solution.py:61
  265.5 14.8 %slice.703 = f32[3,16,16,128]{3,2,1,0:T(8,128)} slice(f32[3,16,16,256]{3,2,1,0:T(8,128)} %get-tuple-element.102), slice={[0:3:1], [0:16:1], [0:16:1], [1:256:2]} | slice | bytes 786432 | tf_op jit(solution)/shard_map/slice | solution.py:61
  281.9 13.4 slice.721
  295.4 13.6 slice.722
  313.3 966.2 %while.10 = (s32[]{:T(128)}, f32[3,16,16,128]{3,2,1,0:T(8,128)S(1)}, pred[]{:T(512)}, f32[3,16,16,128]{3,1,2,0:T(8,128)}, f32[3,16,16,128]{3,1,2,0:T(8,128)}, /*...) while((s32[]{:T(128)}, ...), condition=%wide.region_1.2_spmd, body=%wide.region_0.1_spmd.sunk | while | flops 6807554 | bytes 20943924 | solution.py:123
  357.4 21.9 %collective-permute-done.8 = f32[3,16,16,128]{3,2,1,0:T(8,128)S(1)} collective-permute-done((f32[3,16,16,128]{3,2,1,0:T(8,128)S(1)}, f32[3,16,16,128]{3,2,1,0:T(8,128)S(1)}, u32[]{:S(2)}, u32[]{:S(2)}) %collective-permute-start.8) | collective-permute-done | bytes 393248 | tf_op jit(solution)/shard_map/while/body/eval_jaxpr/ppermute | solution.py:29
  420.2 23.4 %collective-permute-done.8 = f32[3,16,16,128]{3,2,1,0:T(8,128)S(1)} collective-permute-done((f32[3,16,16,128]{3,2,1,0:T(8,128)S(1)}, f32[3,16,16,128]{3,2,1,0:T(8,128)S(1)}, u32[]{:S(2)}, u32[]{:S(2)}) %collective-permute-start.8) | collective-permute-done | bytes 393248 | tf_op jit(solution)/shard_map/while/body/eval_jaxpr/ppermute | solution.py:29
  484.5 23.4 %collective-permute-done.8 = f32[3,16,16,128]{3,2,1,0:T(8,128)S(1)} collective-permute-done((f32[3,16,16,128]{3,2,1,0:T(8,128)S(1)}, f32[3,16,16,128]{3,2,1,0:T(8,128)S(1)}, u32[]{:S(2)}, u32[]{:S(2)}) %collective-permute-start.8) | collective-permute-done | bytes 393248 | tf_op jit(solution)/shard_map/while/body/eval_jaxpr/ppermute | solution.py:29
  548.8 23.4 %collective-permute-done.8 = f32[3,16,16,128]{3,2,1,0:T(8,128)S(1)} collective-permute-done((f32[3,16,16,128]{3,2,1,0:T(8,128)S(1)}, f32[3,16,16,128]{3,2,1,0:T(8,128)S(1)}, u32[]{:S(2)}, u32[]{:S(2)}) %collective-permute-start.8) | collective-permute-done | bytes 393248 | tf_op jit(solution)/shard_map/while/body/eval_jaxpr/ppermute | solution.py:29
  613.1 23.4 %collective-permute-done.8 = f32[3,16,16,128]{3,2,1,0:T(8,128)S(1)} collective-permute-done((f32[3,16,16,128]{3,2,1,0:T(8,128)S(1)}, f32[3,16,16,128]{3,2,1,0:T(8,128)S(1)}, u32[]{:S(2)}, u32[]{:S(2)}) %collective-permute-start.8) | collective-permute-done | bytes 393248 | tf_op jit(solution)/shard_map/while/body/eval_jaxpr/ppermute | solution.py:29
  677.4 23.4 %collective-permute-done.8 = f32[3,16,16,128]{3,2,1,0:T(8,128)S(1)} collective-permute-done((f32[3,16,16,128]{3,2,1,0:T(8,128)S(1)}, f32[3,16,16,128]{3,2,1,0:T(8,128)S(1)}, u32[]{:S(2)}, u32[]{:S(2)}) %collective-permute-start.8) | collective-permute-done | bytes 393248 | tf_op jit(solution)/shard_map/while/body/eval_jaxpr/ppermute | solution.py:29
  741.7 23.4 %collective-permute-done.8 = f32[3,16,16,128]{3,2,1,0:T(8,128)S(1)} collective-permute-done((f32[3,16,16,128]{3,2,1,0:T(8,128)S(1)}, f32[3,16,16,128]{3,2,1,0:T(8,128)S(1)}, u32[]{:S(2)}, u32[]{:S(2)}) %collective-permute-start.8) | collective-permute-done | bytes 393248 | tf_op jit(solution)/shard_map/while/body/eval_jaxpr/ppermute | solution.py:29
  806.0 23.4 %collective-permute-done.8 = f32[3,16,16,128]{3,2,1,0:T(8,128)S(1)} collective-permute-done((f32[3,16,16,128]{3,2,1,0:T(8,128)S(1)}, f32[3,16,16,128]{3,2,1,0:T(8,128)S(1)}, u32[]{:S(2)}, u32[]{:S(2)}) %collective-permute-start.8) | collective-permute-done | bytes 393248 | tf_op jit(solution)/shard_map/while/body/eval_jaxpr/ppermute | solution.py:29
  870.3 23.4 %collective-permute-done.8 = f32[3,16,16,128]{3,2,1,0:T(8,128)S(1)} collective-permute-done((f32[3,16,16,128]{3,2,1,0:T(8,128)S(1)}, f32[3,16,16,128]{3,2,1,0:T(8,128)S(1)}, u32[]{:S(2)}, u32[]{:S(2)}) %collective-permute-start.8) | collective-permute-done | bytes 393248 | tf_op jit(solution)/shard_map/while/body/eval_jaxpr/ppermute | solution.py:29
  934.6 23.4 %collective-permute-done.8 = f32[3,16,16,128]{3,2,1,0:T(8,128)S(1)} collective-permute-done((f32[3,16,16,128]{3,2,1,0:T(8,128)S(1)}, f32[3,16,16,128]{3,2,1,0:T(8,128)S(1)}, u32[]{:S(2)}, u32[]{:S(2)}) %collective-permute-start.8) | collective-permute-done | bytes 393248 | tf_op jit(solution)/shard_map/while/body/eval_jaxpr/ppermute | solution.py:29
  998.9 23.4 %collective-permute-done.8 = f32[3,16,16,128]{3,2,1,0:T(8,128)S(1)} collective-permute-done((f32[3,16,16,128]{3,2,1,0:T(8,128)S(1)}, f32[3,16,16,128]{3,2,1,0:T(8,128)S(1)}, u32[]{:S(2)}, u32[]{:S(2)}) %collective-permute-start.8) | collective-permute-done | bytes 393248 | tf_op jit(solution)/shard_map/while/body/eval_jaxpr/ppermute | solution.py:29
  1063.2 23.4 %collective-permute-done.8 = f32[3,16,16,128]{3,2,1,0:T(8,128)S(1)} collective-permute-done((f32[3,16,16,128]{3,2,1,0:T(8,128)S(1)}, f32[3,16,16,128]{3,2,1,0:T(8,128)S(1)}, u32[]{:S(2)}, u32[]{:S(2)}) %collective-permute-start.8) | collective-permute-done | bytes 393248 | tf_op jit(solution)/shard_map/while/body/eval_jaxpr/ppermute | solution.py:29
  1127.5 23.4 %collective-permute-done.8 = f32[3,16,16,128]{3,2,1,0:T(8,128)S(1)} collective-permute-done((f32[3,16,16,128]{3,2,1,0:T(8,128)S(1)}, f32[3,16,16,128]{3,2,1,0:T(8,128)S(1)}, u32[]{:S(2)}, u32[]{:S(2)}) %collective-permute-start.8) | collective-permute-done | bytes 393248 | tf_op jit(solution)/shard_map/while/body/eval_jaxpr/ppermute | solution.py:29
  1191.8 23.4 %collective-permute-done.8 = f32[3,16,16,128]{3,2,1,0:T(8,128)S(1)} collective-permute-done((f32[3,16,16,128]{3,2,1,0:T(8,128)S(1)}, f32[3,16,16,128]{3,2,1,0:T(8,128)S(1)}, u32[]{:S(2)}, u32[]{:S(2)}) %collective-permute-start.8) | collective-permute-done | bytes 393248 | tf_op jit(solution)/shard_map/while/body/eval_jaxpr/ppermute | solution.py:29
  1256.1 23.4 %collective-permute-done.8 = f32[3,16,16,128]{3,2,1,0:T(8,128)S(1)} collective-permute-done((f32[3,16,16,128]{3,2,1,0:T(8,128)S(1)}, f32[3,16,16,128]{3,2,1,0:T(8,128)S(1)}, u32[]{:S(2)}, u32[]{:S(2)}) %collective-permute-start.8) | collective-permute-done | bytes 393248 | tf_op jit(solution)/shard_map/while/body/eval_jaxpr/ppermute | solution.py:29
  1291.1 7.4 collective-permute-done.39
  1314.9 8.0 collective-permute-done.43
  1353.1 23.2 %collective-permute-done.45 = f32[3,16,16,256]{3,2,1,0:T(8,128)S(1)} collective-permute-done((f32[3,16,16,256]{3,2,1,0:T(8,128)S(1)}, f32[3,16,16,256]{3,2,1,0:T(8,128)S(1)}, u32[]{:S(2)}, u32[]{:S(2)}) %collective-permute-start.45) | collective-permute-done | bytes 786464 | tf_op jit(solution)/shard_map/ppermute | solution.py:29
  (1103 shorter events, 821.5 us)
Async XLA Ops:
  3.5 70.2 %collective-permute-start.18 = (f32[3,16,1,256]{3,1,2,0:T(8,128)}, f32[3,16,1,256]{3,1,2,0:T(8,128)}, u32[]{:S(2)}, u32[]{:S(2)}) collective-permute-start(f32[3,16,1,256]{3,1,2,0:T(8,128)} %copy.596), channel_id=1, source_target_pairs={{0,4},{4,8},{8,12},{1,5},{5,9},{9,13},{2,6},{6,10},{10,14},{3,7},{... | collective-permute-start | bytes 147464 | tf_op jit(solution)/shard_map/ppermute | solution.py:18
  6.4 69.8 %collective-permute-start.17 = (f32[3,16,1,256]{3,1,2,0:T(8,128)}, f32[3,16,1,256]{3,1,2,0:T(8,128)}, u32[]{:S(2)}, u32[]{:S(2)}) collective-permute-start(f32[3,16,1,256]{3,1,2,0:T(8,128)} %copy.594), channel_id=1, source_target_pairs={{4,0},{8,4},{12,8},{5,1},{9,5},{13,9},{6,2},{10,6},{14,10},{7,3},{... | collective-permute-start | bytes 147464 | tf_op jit(solution)/shard_map/ppermute | solution.py:21
  58.9 21.1 %collective-permute-start.14 = (f32[3,16,1,256]{3,1,2,0:T(8,128)}, f32[3,16,1,256]{3,1,2,0:T(8,128)S(1)}, u32[]{:S(2)}, u32[]{:S(2)}) collective-permute-start(f32[3,16,1,256]{3,1,2,0:T(8,128)} %copy.589), channel_id=1, source_target_pairs={{0,4},{4,8},{8,12},{1,5},{5,9},{9,13},{2,6},{6,10},{10,14},{3,7},{... | collective-permute-start | bytes 147464 | tf_op jit(solution)/shard_map/ppermute | solution.py:18
  63.7 19.9 %collective-permute-start.13 = (f32[3,16,1,256]{3,1,2,0:T(8,128)}, f32[3,16,1,256]{3,1,2,0:T(8,128)S(1)}, u32[]{:S(2)}, u32[]{:S(2)}) collective-permute-start(f32[3,16,1,256]{3,1,2,0:T(8,128)} %copy.587), channel_id=1, source_target_pairs={{4,0},{8,4},{12,8},{5,1},{9,5},{13,9},{6,2},{10,6},{14,10},{7,3},{... | collective-permute-start | bytes 147464 | tf_op jit(solution)/shard_map/ppermute | solution.py:21
  70.8 15.9 %collective-permute-start.10 = (f32[3,16,1,256]{3,1,2,0:T(8,128)S(1)}, f32[3,16,1,256]{3,1,2,0:T(8,128)S(1)}, u32[]{:S(2)}, u32[]{:S(2)}) collective-permute-start(f32[3,16,1,256]{3,1,2,0:T(8,128)S(1)} %copy-done.60), channel_id=1, source_target_pairs={{0,4},{4,8},{8,12},{1,5},{5,9},{9,13},{2,6},{6,10},{10,14},{3,7},{... | collective-permute-start | bytes 147464 | tf_op jit(solution)/shard_map/ppermute | solution.py:18
  74.9 15.2 %collective-permute-start.9 = (f32[3,16,1,256]{3,1,2,0:T(8,128)S(1)}, f32[3,16,1,256]{3,1,2,0:T(8,128)S(1)}, u32[]{:S(2)}, u32[]{:S(2)}) collective-permute-start(f32[3,16,1,256]{3,1,2,0:T(8,128)S(1)} %copy-done.59), channel_id=1, source_target_pairs={{4,0},{8,4},{12,8},{5,1},{9,5},{13,9},{6,2},{10,6},{14,10},{7,3},{... | collective-permute-start | bytes 147464 | tf_op jit(solution)/shard_map/ppermute | solution.py:21
  77.2 18.0 %collective-permute-start.19 = (f32[3,16,18,1]{3,1,2,0:T(8,128)S(1)}, f32[3,16,18,1]{3,1,2,0:T(8,128)S(1)}, u32[]{:S(2)}, u32[]{:S(2)}) collective-permute-start(f32[3,16,18,1]{3,1,2,0:T(8,128)S(1)} %get-tuple-element.156), channel_id=1, source_target_pairs={{1,0},{2,1},{3,2},{5,4},{6,5},{7,6},{9,8},{10,9},{11,10},{13,12},{... | collective-permute-start | bytes 10376 | tf_op jit(solution)/shard_map/ppermute | solution.py:21
  80.6 17.8 %collective-permute-start.20 = (f32[3,16,18,1]{3,1,2,0:T(8,128)S(1)}, f32[3,16,18,1]{3,1,2,0:T(8,128)S(1)}, u32[]{:S(2)}, u32[]{:S(2)}) collective-permute-start(f32[3,16,18,1]{3,1,2,0:T(8,128)S(1)} %get-tuple-element.157), channel_id=1, source_target_pairs={{0,1},{1,2},{2,3},{4,5},{5,6},{6,7},{8,9},{9,10},{10,11},{12,13},{... | collective-permute-start | bytes 10376 | tf_op jit(solution)/shard_map/ppermute | solution.py:18
  83.8 16.3 %collective-permute-start.15 = (f32[3,16,18,1]{3,1,2,0:T(8,128)S(1)}, f32[3,16,18,1]{3,1,2,0:T(8,128)S(1)}, u32[]{:S(2)}, u32[]{:S(2)}) collective-permute-start(f32[3,16,18,1]{3,1,2,0:T(8,128)S(1)} %get-tuple-element.160), channel_id=1, source_target_pairs={{1,0},{2,1},{3,2},{5,4},{6,5},{7,6},{9,8},{10,9},{11,10},{13,12},{... | collective-permute-start | bytes 10376 | tf_op jit(solution)/shard_map/ppermute | solution.py:21
  87.2 16.7 %collective-permute-start.16 = (f32[3,16,18,1]{3,1,2,0:T(8,128)S(1)}, f32[3,16,18,1]{3,1,2,0:T(8,128)S(1)}, u32[]{:S(2)}, u32[]{:S(2)}) collective-permute-start(f32[3,16,18,1]{3,1,2,0:T(8,128)S(1)} %get-tuple-element.161), channel_id=1, source_target_pairs={{0,1},{1,2},{2,3},{4,5},{5,6},{6,7},{8,9},{9,10},{10,11},{12,13},{... | collective-permute-start | bytes 10376 | tf_op jit(solution)/shard_map/ppermute | solution.py:18
  92.3 17.3 %collective-permute-start.11 = (f32[3,16,18,1]{3,1,2,0:T(8,128)S(1)}, f32[3,16,18,1]{3,1,2,0:T(8,128)S(1)}, u32[]{:S(2)}, u32[]{:S(2)}) collective-permute-start(f32[3,16,18,1]{3,1,2,0:T(8,128)S(1)} %get-tuple-element.164), channel_id=1, source_target_pairs={{1,0},{2,1},{3,2},{5,4},{6,5},{7,6},{9,8},{10,9},{11,10},{13,12},{... | collective-permute-start | bytes 10376 | tf_op jit(solution)/shard_map/ppermute | solution.py:21
  95.2 18.2 %collective-permute-start.12 = (f32[3,16,18,1]{3,1,2,0:T(8,128)S(1)}, f32[3,16,18,1]{3,1,2,0:T(8,128)S(1)}, u32[]{:S(2)}, u32[]{:S(2)}) collective-permute-start(f32[3,16,18,1]{3,1,2,0:T(8,128)S(1)} %get-tuple-element.165), channel_id=1, source_target_pairs={{0,1},{1,2},{2,3},{4,5},{5,6},{6,7},{8,9},{9,10},{10,11},{12,13},{... | collective-permute-start | bytes 10376 | tf_op jit(solution)/shard_map/ppermute | solution.py:18
  172.9 14.8 %collective-permute-start.23 = (f32[3,16,18,1]{3,1,2,0:T(8,128)S(1)}, f32[3,16,18,1]{3,1,2,0:T(8,128)S(1)}, u32[]{:S(2)}, u32[]{:S(2)}) collective-permute-start(f32[3,16,18,1]{3,1,2,0:T(8,128)S(1)} %get-tuple-element.152), channel_id=1, source_target_pairs={{1,0},{2,1},{3,2},{5,4},{6,5},{7,6},{9,8},{10,9},{11,10},{13,12},{... | collective-permute-start | bytes 10376 | tf_op jit(solution)/shard_map/ppermute | solution.py:21
  174.8 14.6 %collective-permute-start.24 = (f32[3,16,18,1]{3,1,2,0:T(8,128)S(1)}, f32[3,16,18,1]{3,1,2,0:T(8,128)S(1)}, u32[]{:S(2)}, u32[]{:S(2)}) collective-permute-start(f32[3,16,18,1]{3,1,2,0:T(8,128)S(1)} %get-tuple-element.153), channel_id=1, source_target_pairs={{0,1},{1,2},{2,3},{4,5},{5,6},{6,7},{8,9},{9,10},{10,11},{12,13},{... | collective-permute-start | bytes 10376 | tf_op jit(solution)/shard_map/ppermute | solution.py:18
  202.5 43.4 %collective-permute-start.31 = (f32[3,16,18,1]{3,1,2,0:T(8,128)}, f32[3,16,18,1]{3,1,2,0:T(8,128)}, u32[]{:S(2)}, u32[]{:S(2)}) collective-permute-start(f32[3,16,18,1]{3,1,2,0:T(8,128)} %get-tuple-element.148), channel_id=1, source_target_pairs={{1,0},{2,1},{3,2},{5,4},{6,5},{7,6},{9,8},{10,9},{11,10},{13,12},{... | collective-permute-start | bytes 10376 | tf_op jit(solution)/shard_map/ppermute | solution.py:21
  204.4 41.5 %collective-permute-start.32 = (f32[3,16,18,1]{3,1,2,0:T(8,128)}, f32[3,16,18,1]{3,1,2,0:T(8,128)}, u32[]{:S(2)}, u32[]{:S(2)}) collective-permute-start(f32[3,16,18,1]{3,1,2,0:T(8,128)} %get-tuple-element.149), channel_id=1, source_target_pairs={{0,1},{1,2},{2,3},{4,5},{5,6},{6,7},{8,9},{9,10},{10,11},{12,13},{... | collective-permute-start | bytes 10376 | tf_op jit(solution)/shard_map/ppermute | solution.py:18
  353.9 25.3 %collective-permute-start.8 = (f32[3,16,16,128]{3,2,1,0:T(8,128)S(1)}, f32[3,16,16,128]{3,2,1,0:T(8,128)S(1)}, u32[]{:S(2)}, u32[]{:S(2)}) collective-permute-start(f32[3,16,16,128]{3,2,1,0:T(8,128)S(1)} %copy.748), channel_id=1, source_target_pairs={{0,16},{16,32},{32,48},{48,64},{64,80},{80,96},{96,112},{112,128},... | collective-permute-start | bytes 1179656 | tf_op jit(solution)/shard_map/while/body/eval_jaxpr/ppermute | solution.py:29
  418.3 25.3 %collective-permute-start.8 = (f32[3,16,16,128]{3,2,1,0:T(8,128)S(1)}, f32[3,16,16,128]{3,2,1,0:T(8,128)S(1)}, u32[]{:S(2)}, u32[]{:S(2)}) collective-permute-start(f32[3,16,16,128]{3,2,1,0:T(8,128)S(1)} %copy.748), channel_id=1, source_target_pairs={{0,16},{16,32},{32,48},{48,64},{64,80},{80,96},{96,112},{112,128},... | collective-permute-start | bytes 1179656 | tf_op jit(solution)/shard_map/while/body/eval_jaxpr/ppermute | solution.py:29
  482.6 25.3 %collective-permute-start.8 = (f32[3,16,16,128]{3,2,1,0:T(8,128)S(1)}, f32[3,16,16,128]{3,2,1,0:T(8,128)S(1)}, u32[]{:S(2)}, u32[]{:S(2)}) collective-permute-start(f32[3,16,16,128]{3,2,1,0:T(8,128)S(1)} %copy.748), channel_id=1, source_target_pairs={{0,16},{16,32},{32,48},{48,64},{64,80},{80,96},{96,112},{112,128},... | collective-permute-start | bytes 1179656 | tf_op jit(solution)/shard_map/while/body/eval_jaxpr/ppermute | solution.py:29
  546.9 25.3 %collective-permute-start.8 = (f32[3,16,16,128]{3,2,1,0:T(8,128)S(1)}, f32[3,16,16,128]{3,2,1,0:T(8,128)S(1)}, u32[]{:S(2)}, u32[]{:S(2)}) collective-permute-start(f32[3,16,16,128]{3,2,1,0:T(8,128)S(1)} %copy.748), channel_id=1, source_target_pairs={{0,16},{16,32},{32,48},{48,64},{64,80},{80,96},{96,112},{112,128},... | collective-permute-start | bytes 1179656 | tf_op jit(solution)/shard_map/while/body/eval_jaxpr/ppermute | solution.py:29
  611.2 25.3 %collective-permute-start.8 = (f32[3,16,16,128]{3,2,1,0:T(8,128)S(1)}, f32[3,16,16,128]{3,2,1,0:T(8,128)S(1)}, u32[]{:S(2)}, u32[]{:S(2)}) collective-permute-start(f32[3,16,16,128]{3,2,1,0:T(8,128)S(1)} %copy.748), channel_id=1, source_target_pairs={{0,16},{16,32},{32,48},{48,64},{64,80},{80,96},{96,112},{112,128},... | collective-permute-start | bytes 1179656 | tf_op jit(solution)/shard_map/while/body/eval_jaxpr/ppermute | solution.py:29
  675.5 25.3 %collective-permute-start.8 = (f32[3,16,16,128]{3,2,1,0:T(8,128)S(1)}, f32[3,16,16,128]{3,2,1,0:T(8,128)S(1)}, u32[]{:S(2)}, u32[]{:S(2)}) collective-permute-start(f32[3,16,16,128]{3,2,1,0:T(8,128)S(1)} %copy.748), channel_id=1, source_target_pairs={{0,16},{16,32},{32,48},{48,64},{64,80},{80,96},{96,112},{112,128},... | collective-permute-start | bytes 1179656 | tf_op jit(solution)/shard_map/while/body/eval_jaxpr/ppermute | solution.py:29
  739.8 25.3 %collective-permute-start.8 = (f32[3,16,16,128]{3,2,1,0:T(8,128)S(1)}, f32[3,16,16,128]{3,2,1,0:T(8,128)S(1)}, u32[]{:S(2)}, u32[]{:S(2)}) collective-permute-start(f32[3,16,16,128]{3,2,1,0:T(8,128)S(1)} %copy.748), channel_id=1, source_target_pairs={{0,16},{16,32},{32,48},{48,64},{64,80},{80,96},{96,112},{112,128},... | collective-permute-start | bytes 1179656 | tf_op jit(solution)/shard_map/while/body/eval_jaxpr/ppermute | solution.py:29
  804.1 25.3 %collective-permute-start.8 = (f32[3,16,16,128]{3,2,1,0:T(8,128)S(1)}, f32[3,16,16,128]{3,2,1,0:T(8,128)S(1)}, u32[]{:S(2)}, u32[]{:S(2)}) collective-permute-start(f32[3,16,16,128]{3,2,1,0:T(8,128)S(1)} %copy.748), channel_id=1, source_target_pairs={{0,16},{16,32},{32,48},{48,64},{64,80},{80,96},{96,112},{112,128},... | collective-permute-start | bytes 1179656 | tf_op jit(solution)/shard_map/while/body/eval_jaxpr/ppermute | solution.py:29
  868.4 25.3 %collective-permute-start.8 = (f32[3,16,16,128]{3,2,1,0:T(8,128)S(1)}, f32[3,16,16,128]{3,2,1,0:T(8,128)S(1)}, u32[]{:S(2)}, u32[]{:S(2)}) collective-permute-start(f32[3,16,16,128]{3,2,1,0:T(8,128)S(1)} %copy.748), channel_id=1, source_target_pairs={{0,16},{16,32},{32,48},{48,64},{64,80},{80,96},{96,112},{112,128},... | collective-permute-start | bytes 1179656 | tf_op jit(solution)/shard_map/while/body/eval_jaxpr/ppermute | solution.py:29
  932.7 25.3 %collective-permute-start.8 = (f32[3,16,16,128]{3,2,1,0:T(8,128)S(1)}, f32[3,16,16,128]{3,2,1,0:T(8,128)S(1)}, u32[]{:S(2)}, u32[]{:S(2)}) collective-permute-start(f32[3,16,16,128]{3,2,1,0:T(8,128)S(1)} %copy.748), channel_id=1, source_target_pairs={{0,16},{16,32},{32,48},{48,64},{64,80},{80,96},{96,112},{112,128},... | collective-permute-start | bytes 1179656 | tf_op jit(solution)/shard_map/while/body/eval_jaxpr/ppermute | solution.py:29
  997.0 25.3 %collective-permute-start.8 = (f32[3,16,16,128]{3,2,1,0:T(8,128)S(1)}, f32[3,16,16,128]{3,2,1,0:T(8,128)S(1)}, u32[]{:S(2)}, u32[]{:S(2)}) collective-permute-start(f32[3,16,16,128]{3,2,1,0:T(8,128)S(1)} %copy.748), channel_id=1, source_target_pairs={{0,16},{16,32},{32,48},{48,64},{64,80},{80,96},{96,112},{112,128},... | collective-permute-start | bytes 1179656 | tf_op jit(solution)/shard_map/while/body/eval_jaxpr/ppermute | solution.py:29
  1061.3 25.3 %collective-permute-start.8 = (f32[3,16,16,128]{3,2,1,0:T(8,128)S(1)}, f32[3,16,16,128]{3,2,1,0:T(8,128)S(1)}, u32[]{:S(2)}, u32[]{:S(2)}) collective-permute-start(f32[3,16,16,128]{3,2,1,0:T(8,128)S(1)} %copy.748), channel_id=1, source_target_pairs={{0,16},{16,32},{32,48},{48,64},{64,80},{80,96},{96,112},{112,128},... | collective-permute-start | bytes 1179656 | tf_op jit(solution)/shard_map/while/body/eval_jaxpr/ppermute | solution.py:29
  1125.6 25.3 %collective-permute-start.8 = (f32[3,16,16,128]{3,2,1,0:T(8,128)S(1)}, f32[3,16,16,128]{3,2,1,0:T(8,128)S(1)}, u32[]{:S(2)}, u32[]{:S(2)}) collective-permute-start(f32[3,16,16,128]{3,2,1,0:T(8,128)S(1)} %copy.748), channel_id=1, source_target_pairs={{0,16},{16,32},{32,48},{48,64},{64,80},{80,96},{96,112},{112,128},... | collective-permute-start | bytes 1179656 | tf_op jit(solution)/shard_map/while/body/eval_jaxpr/ppermute | solution.py:29
  1189.9 25.3 %collective-permute-start.8 = (f32[3,16,16,128]{3,2,1,0:T(8,128)S(1)}, f32[3,16,16,128]{3,2,1,0:T(8,128)S(1)}, u32[]{:S(2)}, u32[]{:S(2)}) collective-permute-start(f32[3,16,16,128]{3,2,1,0:T(8,128)S(1)} %copy.748), channel_id=1, source_target_pairs={{0,16},{16,32},{32,48},{48,64},{64,80},{80,96},{96,112},{112,128},... | collective-permute-start | bytes 1179656 | tf_op jit(solution)/shard_map/while/body/eval_jaxpr/ppermute | solution.py:29
  1254.2 25.3 %collective-permute-start.8 = (f32[3,16,16,128]{3,2,1,0:T(8,128)S(1)}, f32[3,16,16,128]{3,2,1,0:T(8,128)S(1)}, u32[]{:S(2)}, u32[]{:S(2)}) collective-permute-start(f32[3,16,16,128]{3,2,1,0:T(8,128)S(1)} %copy.748), channel_id=1, source_target_pairs={{0,16},{16,32},{32,48},{48,64},{64,80},{80,96},{96,112},{112,128},... | collective-permute-start | bytes 1179656 | tf_op jit(solution)/shard_map/while/body/eval_jaxpr/ppermute | solution.py:29
  1338.6 37.6 %collective-permute-start.45 = (f32[3,16,16,256]{3,2,1,0:T(8,128)S(1)}, f32[3,16,16,256]{3,2,1,0:T(8,128)S(1)}, u32[]{:S(2)}, u32[]{:S(2)}) collective-permute-start(f32[3,16,16,256]{3,2,1,0:T(8,128)S(1)} %add.395), channel_id=1, source_target_pairs={{0,16},{16,32},{32,48},{48,64},{64,80},{80,96},{96,112},{112,128},... | collective-permute-start | bytes 2359304 | tf_op jit(solution)/shard_map/ppermute | solution.py:29
  (257 other events, 1820.4 us)
where the time goes:
time: 1400 us; the launch traced here: 1380 us
  waiting for transfers between devices  465 us (33%)
  starting transfers between devices  424 us (30%)
  local copies, waits for them, and re-layouts  344 us (25%)
  other arithmetic  141 us (10%)
    ppermute x16, waiting for transfers between devices, passed_along(): return lax.ppermute(block, axis, route)  372 us
    ppermute x78, starting transfers between devices, padded_2(): lax.ppermute(lax.slice_in_dim(block, block.shape[dim] - width, None, axis...  236 us
    ppermute x78, starting transfers between devices, padded_2(): lax.ppermute(lax.slice_in_dim(block, 0, width, axis=dim), axis, backward)  156 us
    slice x10, local copies, waits for them, and re-layouts, restrict(): return 0.5 * (field[..., 0::2] + field[..., 1::2])  138 us
    while x210, local copies, waits for them, and re-layouts  59.5 us
    ppermute x78, waiting for transfers between devices, padded_2(): lax.ppermute(lax.slice_in_dim(block, block.shape[dim] - width, None, axis...  52.6 us
    slice x76, local copies, waits for them, and re-layouts, tendency(): upper_side = jnp.roll(centre, -1, axis=1)  41.6 us
    ppermute x78, waiting for transfers between devices, padded_2(): lax.ppermute(lax.slice_in_dim(block, 0, width, axis=dim), axis, backward)  39.7 us
  transfers between devices with their start and end apart: 172, of which 78 were waited for; matrix products, arithmetic and copies ran while one was open for 15% of the time, Pallas kernels for 0%

commit v1 on v0

v1 whole, which is shorter than its diff:
```python
import jax
import jax.numpy as jnp
from jax import lax
from jax.experimental import pallas as pl
from jax.experimental.pallas import tpu as pltpu
from jax.sharding import Mesh
from jax.sharding import PartitionSpec as P

viscosity = 0.1
slice_step = 0.25
half_step = 0.125
first_row = (5.0 / 24.0, 1.0 / 3.0, -1.0 / 24.0)
second_row = (-1.0 / 24.0, 1.0 / 3.0, 5.0 / 24.0)

f32 = jnp.float32
highest = lax.Precision.HIGHEST
group_axes = ("ty", "gx")


def lanes(shape):
    return lax.broadcasted_iota(jnp.int32, shape, len(shape) - 1)


def strided(u, k, x, half):
    return u[pl.ds(k * 512 + x // 8 * 16 + half * 8 + x % 8, 16, stride=32), :]


def edges_body(u, low_rows, high_rows, low_columns, high_columns):
    slot = lanes((16, 128)) // 8

    def each(k, carry):
        left = jnp.zeros((16, 128), f32)
        right = jnp.zeros((16, 128), f32)
        for x in range(16):
            a = strided(u, k, x, 0)
            b = strided(u, k, x, 1)
            if x < 3:
                low_rows[k, x, :, 0:128] = a
                low_rows[k, x, :, 128:256] = b
            if x > 12:
                high_rows[k, x - 13, :, 0:128] = a
                high_rows[k, x - 13, :, 128:256] = b
            turned_a = pltpu.roll(a, 8 * x, 1) if x else a
            turned_b = pltpu.roll(b, (8 * x + 8) % 128, 1) if x < 15 else b
            left = jnp.where(slot == x, turned_a, left)
            right = jnp.where(slot == x, turned_b, right)
        low_columns[k] = left
        high_columns[k] = right
        return carry

    lax.fori_loop(0, 9, each, 0)


def edges(u):
    rows = jax.ShapeDtypeStruct((9, 3, 16, 256), f32)
    columns = jax.ShapeDtypeStruct((9, 16, 128), f32)
    return pl.pallas_call(edges_body, out_shape=(rows, rows, columns, columns), name="edges")(u)


def tendency(below, row, above, reach, spacing):
    width = row[0].shape[-1]
    square = 1.0 / (spacing * spacing)
    out = []
    for c in range(3):
        u = row[c]
        up = pltpu.roll(u, 15, 0)
        down = pltpu.roll(u, 1, 0)
        north = pltpu.roll(u, width - reach, 1)
        south = pltpu.roll(u, reach, 1)
        laplace = (above[c] + below[c]) + (up + down) - (4.0 + 2.0 * square) * u
        laplace = laplace + (north + south) * square
        transport = (
            row[0] * (above[c] - below[c])
            + row[1] * ((north - south) * (1.0 / spacing))
            + row[2] * (up - down)
        )
        out.append(viscosity * laplace - 0.5 * transport)
    return out


def fine_body(place, u, before, after, south_0, south_1, south_2, north_0, north_1, north_2,
              sources, halves_1, halves_2, ue, v1, v2, rest, f0, h1, pair_u, pair_v, native_0, native_1):
    gx = place[0]
    gy = place[1]
    leader = place[2] == 0
    lane = lanes((16, 128))
    wide = lanes((16, 384))
    even = wide % 2 == 0
    low_ok = jnp.where(gx > 0, 1.0, 0.0).astype(f32)
    high_ok = jnp.where(gx < 3, 1.0, 0.0).astype(f32)
    north_ok = jnp.where(gy < 3, 1.0, 0.0).astype(f32)
    south_ok = jnp.where(gy > 0, 1.0, 0.0).astype(f32)
    columns_ok = jnp.where(wide < 256, 1.0, jnp.where(wide < 320, north_ok, south_ok))

    def gather(k, carry):
        for e in range(22):
            x = e - 3
            if x < 0:
                ue[k, e, :, 0:256] = before[k, e]
                a, b, slot = north_0, south_0, 16 + x
            elif x < 16:
                ue[k, e, :, 0:128] = strided(u, k, x, 0)
                ue[k, e, :, 128:256] = strided(u, k, x, 1)
                a, b, slot = north_1, south_1, x
            else:
                ue[k, e, :, 0:256] = after[k, x - 16]
                a, b, slot = north_2, south_2, x - 16
            a = a[k]
            b = b[k]
            if slot > 0:
                a = pltpu.roll(a, 128 - 8 * slot, 1)
            if slot < 15:
                b = pltpu.roll(b, 120 - 8 * slot, 1)
            ue[k, e, :, 256:384] = jnp.where(lane < 64, a, b)
        return carry

    lax.fori_loop(0, 9, gather, 0)

    def row_ok(e):
        return jnp.where(e < 3, low_ok, jnp.where(e > 18, high_ok, 1.0))

    def paired(field):
        return 0.5 * (field + jnp.where(even, pltpu.roll(field, 383, 1), pltpu.roll(field, 1, 1)))

    def first(e, carry):
        flux = []
        for node in range(3):
            rows = [[ue[3 * node + c, e + d] for c in range(3)] for d in (-1, 0, 1)]
            flux.append(tendency(*rows, 1, 1.0))
        ok = columns_ok * row_ok(e)
        for c in range(3):
            a, b, d = flux[0][c], flux[1][c], flux[2][c]
            start = ue[c, e]
            new = start + slice_step * (first_row[0] * a + first_row[1] * b + first_row[2] * d)
            new = new * ok
            v1[c, e] = new
            rest[c, e] = (
                slice_step * (second_row[0] * a + second_row[1] * b + second_row[2] * d)
                - half_step * b
            )
            f0[c, e] = a
            pair_u[c, e] = paired(start)
            pair_v[c, e] = paired(new)
        return carry

    lax.fori_loop(1, 21, first, 0)

    def second(e, carry):
        rows = [[v1[c, e + d] for c in range(3)] for d in (-1, 0, 1)]
        slope = tendency(*rows, 1, 1.0)
        ok = columns_ok * row_ok(e)
        for c in range(3):
            v2[c, e] = (rows[1][c] + half_step * slope[c] + rest[c, e]) * ok
            h1[c, e] = slope[c]
        return carry

    lax.fori_loop(2, 20, second, 0)

    def put(field, c, x, value):
        at = pl.ds((field * 3 + c) * 256 + x, 16, stride=16)
        native_0[at, :] = value[:, 0:128]
        native_1[at, :] = value[:, 128:256]

    def third(e, carry):
        rows = [[v2[c, e + d] for c in range(3)] for d in (-1, 0, 1)]
        slope = tendency(*rows, 1, 1.0)
        base_u = tendency(*[[pair_u[c, e + d] for c in range(3)] for d in (-1, 0, 1)], 2, 2.0)
        base_v = tendency(*[[pair_v[c, e + d] for c in range(3)] for d in (-1, 0, 1)], 2, 2.0)
        for c in range(3):
            a, b, d = f0[c, e], h1[c, e], slope[c]
            one = slice_step * (first_row[0] * a + first_row[1] * b + first_row[2] * d)
            two = slice_step * (second_row[0] * a + second_row[1] * b + second_row[2] * d)
            one = one + jnp.where(leader, ue[c, e], -half_step * base_u[c])
            two = two - half_step * base_v[c]
            put(0, c, e - 3, one)
            put(1, c, e - 3, two)
            put(2, c, e - 3, v1[c, e])
            put(3, c, e - 3, rows[1][c])
        return carry

    lax.fori_loop(3, 19, third, 0)

    fine = lanes((64, 128))
    own = fine // 2 == lax.broadcasted_iota(jnp.int32, (64, 128), 0)
    mean = jnp.where(own, 0.5, 0.0).astype(f32)
    half = jnp.where(own, jnp.where(fine % 2 == 0, 0.5, -0.5), 0.0).astype(f32)

    def contract(matrix, part, out, at):
        for native, to in ((native_0, 0), (native_1, 64)):
            out[to:to + 64, at:at + 256] = lax.dot_general(
                matrix, native[part * 256:(part + 1) * 256, :], (((1,), (1,)), ((), ())),
                precision=highest, preferred_element_type=f32,
            )

    for part in range(6):
        contract(mean, part, sources, part * 256)
    for part in range(3):
        contract(half, 6 + part, halves_1, part * 256)
        contract(half, 9 + part, halves_2, part * 256)


def fine_part(place, *arrays):
    vmem = pl.BlockSpec(memory_space=pltpu.VMEM)
    field = pltpu.VMEM((3, 22, 16, 384), f32)
    return pl.pallas_call(
        fine_body,
        out_shape=(
            jax.ShapeDtypeStruct((128, 1536), f32),
            jax.ShapeDtypeStruct((128, 768), f32),
            jax.ShapeDtypeStruct((128, 768), f32),
        ),
        in_specs=[pl.BlockSpec(memory_space=pltpu.SMEM)] + [vmem] * len(arrays),
        scratch_shapes=[pltpu.VMEM((9, 22, 16, 384), f32)] + [field] * 7 + [pltpu.VMEM((3072, 128), f32)] * 2,
        compiler_params=pltpu.CompilerParams(vmem_limit_bytes=60 * 2**20),
        name="fine",
    )(place, *arrays)


def stage_body(place, own, left, right, source, source_left, source_right, *rest):
    *outs, buffer_0, buffer_1 = rest
    last = outs[0]
    trace = outs[1] if len(outs) > 1 else None
    lane = lanes((24, 128))
    x_first = lane % 16 == 0
    x_last = lane % 16 == 15
    z_first = lane < 16
    z_last = lane >= 112
    row = lax.broadcasted_iota(jnp.int32, (24, 128), 0)
    inside = ((row >= 8) | (place[3] > 0)) & ((row < 16) | (place[3] < 63))

    for c in range(3):
        for t in range(8):
            buffer_0[c, t, 0:8] = left[c, t]
            buffer_0[c, t, 8:16] = own[c, t]
            buffer_0[c, t, 16:24] = right[c, t]

    def keep(j, field, buffer):
        for xh in range(4):
            for c in range(3):
                for zh in range(2):
                    at = (field * 6 + c * 2 + zh) * 128
                    trace[j * 4 + xh, :, at:at + 128] = buffer[c, xh * 2 + zh, 8:16]

    square = 0.25
    c_side = half_step * viscosity
    c_second = half_step * viscosity * square
    c_centre = 1.0 - half_step * viscosity * (4.0 + 2.0 * square)

    def step(j, field, old, new):
        for xh in range(4):
            u = [[old[c, 2 * xh + zh] for zh in range(2)] for c in range(3)]
            for zh in range(2):
                t = 2 * xh + zh
                k0 = u[0][zh] * (-0.5 * half_step)
                k1 = u[1][zh] * (-0.25 * half_step)
                k2 = u[2][zh] * (-0.5 * half_step)
                for c in range(3):
                    v = u[c][zh]
                    o = u[c][1 - zh]
                    after = pltpu.roll(old[c, t + 2], 15, 1) if xh < 3 else jnp.zeros((24, 128), f32)
                    before = pltpu.roll(old[c, t - 2], 113, 1) if xh > 0 else jnp.zeros((24, 128), f32)
                    east = jnp.where(x_last, after, pltpu.roll(v, 127, 1))
                    west = jnp.where(x_first, before, pltpu.roll(v, 1, 1))
                    up = jnp.where(z_last, pltpu.roll(o, 112, 1), pltpu.roll(v, 112, 1))
                    down = jnp.where(z_first, pltpu.roll(o, 16, 1), pltpu.roll(v, 16, 1))
                    north = pltpu.roll(v, 23, 0)
                    south = pltpu.roll(v, 1, 0)
                    at = (field * 6 + c * 2 + zh) * 128
                    pull = jnp.concatenate(
                        [r[j * 4 + xh, :, at:at + 128] for r in (source_left, source, source_right)], axis=0
                    )
                    value = (
                        c_centre * v
                        + c_side * ((east + west) + (up + down))
                        + c_second * (north + south)
                        + (k0 * (east - west) + k1 * (north - south) + k2 * (up - down))
                        + pull
                    )
                    new[c, t] = jnp.where(inside, value, 0.0)

    def one_slice(j, carry):
        if trace is not None:
            keep(j, 0, buffer_0)
        step(j, 0, buffer_0, buffer_1)
        if trace is not None:
            keep(j, 1, buffer_1)
        step(j, 1, buffer_1, buffer_0)
        if trace is not None:
            keep(j, 2, buffer_0)
        return carry

    lax.fori_loop(0, 4, one_slice, 0)
    for c in range(3):
        for t in range(8):
            last[c, t] = buffer_0[c, t, 8:16]


def stage(place, own, left, right, source, source_left, source_right, keeps):
    vmem = pl.BlockSpec(memory_space=pltpu.VMEM)
    shapes = [jax.ShapeDtypeStruct((3, 8, 8, 128), f32)]
    if keeps:
        shapes.append(jax.ShapeDtypeStruct((16, 8, 2304), f32))
    return pl.pallas_call(
        stage_body,
        out_shape=shapes,
        in_specs=[pl.BlockSpec(memory_space=pltpu.SMEM)] + [vmem] * 6,
        scratch_shapes=[pltpu.VMEM((3, 8, 24, 128), f32)] * 2,
        compiler_params=pltpu.CompilerParams(vmem_limit_bytes=60 * 2**20),
        name="stage",
    )(place, own, left, right, source, source_left, source_right)


def finish_body(place, start, coarse, halves_0, halves_1, halves_2, out):
    fine = lanes((128, 128))
    k = lax.broadcasted_iota(jnp.int32, (128, 128), 0)
    sign = jnp.where(k < 64, 1.0, jnp.where(fine % 2 == 0, 1.0, -1.0))
    matrix = jnp.where(fine // 2 == k % 64, sign, 0.0).astype(f32)
    for field, halves in enumerate((halves_0, halves_1, halves_2)):
        for c in range(3):
            at = field * 768 + c * 256
            for half in range(2):
                part = pl.ds(half * 64, 64)
                both = jnp.concatenate(
                    [coarse[part, at:at + 256], halves[part, c * 256:(c + 1) * 256]], axis=0
                )
                value = lax.dot_general(
                    both.T, matrix, (((1,), (0,)), ((), ())), precision=highest, preferred_element_type=f32
                )
                out[at // 8:at // 8 + 32, half] = value.reshape(32, 8, 128)

    @pl.when(place[2] == 0)
    def _():
        pltpu.sync_copy(start.at[pl.ds(0, 96)], out.at[pl.ds(0, 96)])


def finish(place, start, coarse, halves_0, halves_1, halves_2):
    vmem = pl.BlockSpec(memory_space=pltpu.VMEM)
    return pl.pallas_call(
        finish_body,
        out_shape=jax.ShapeDtypeStruct((288, 2, 8, 128), f32),
        in_specs=[pl.BlockSpec(memory_space=pltpu.SMEM), pl.BlockSpec(memory_space=pl.ANY)] + [vmem] * 4,
        compiler_params=pltpu.CompilerParams(vmem_limit_bytes=60 * 2**20),
        name="finish",
    )(place, start, coarse, halves_0, halves_1, halves_2)


def sent(block, axes, sizes, moves):
    strides = {}
    total = 1
    for axis in reversed(axes):
        strides[axis] = total
        total *= sizes[axis]
    pairs = []
    for source in range(total):
        target = source
        for axis, by in moves.items():
            at = source // strides[axis] % sizes[axis]
            if not 0 <= at + by < sizes[axis]:
                target = None
                break
            target += by * strides[axis]
        if target is not None:
            pairs.append((source, target))
    return lax.ppermute(block, axes if len(axes) > 1 else axes[0], pairs)


def solution(mesh):
    sizes = {"tz": 4, "ty": 4, "gx": 4, "gy": 4}
    fine_mesh = Mesh(mesh.devices.reshape(4, 4, 4, 4), tuple(sizes))
    lateral = ("gx", "gy")
    pieces = ("ty", "gx", "gy")

    def beside(block, by):
        name = lambda piece: (piece % 16) * 4 + piece // 16
        pairs = [(name(i), name(i + by)) for i in range(64) if 0 <= i + by < 64]
        return lax.ppermute(block, pieces, pairs)

    def per_device(provisional):
        tz, ty, gx, gy = (lax.axis_index(a) for a in sizes)
        place = jnp.stack([gx, gy, tz * 4 + ty, gy * 16 + ty * 4 + gx]).astype(jnp.int32)
        tiles = provisional.reshape(288, 8, 2, 128).transpose(0, 2, 1, 3)
        u = tiles.reshape(4608, 128)
        low_rows, high_rows, low_columns, high_columns = edges(u)
        after = sent(low_rows, lateral, sizes, {"gx": -1})
        before = sent(high_rows, lateral, sizes, {"gx": 1})
        south = [sent(high_columns, lateral, sizes, {"gx": -d, "gy": 1}) for d in (-1, 0, 1)]
        north = [sent(low_columns, lateral, sizes, {"gx": -d, "gy": -1}) for d in (-1, 0, 1)]
        sources, halves_1, halves_2 = fine_part(place, u, before, after, *south, *north)
        halves_0 = lax.ppermute(halves_2, ("tz", "ty"), [(i, i + 1) for i in range(15)])
        source = lax.all_to_all(sources.reshape(16, 8, 1536), group_axes, 0, 0)
        source_left = beside(source, 1)
        source_right = beside(source, -1)
        own = left = right = jnp.zeros((3, 8, 8, 128), f32)
        for turn in range(4):
            own, *kept = stage(place, own, left, right, source, source_left, source_right, turn == 3)
            if turn < 3:
                own = sent(own, ("tz",), sizes, {"tz": 1})
                left = beside(own, 1)
                right = beside(own, -1)
        coarse = lax.all_to_all(kept[0], group_axes, 0, 0).reshape(128, 2304)
        out = finish(place, tiles, coarse, halves_0, halves_1, halves_2)
        return out.transpose(0, 2, 1, 3).reshape(1, 3, 3, 16, 16, 256)

    spec = P(("tz", "ty"), None, None, None, "gx", "gy")
    return jax.shard_map(per_device, mesh=fine_mesh, in_specs=(spec,), out_specs=spec, check_vma=False)
```

time: 1400 us -> 234 us (0.17); the launches traced: 1380 us -> 233 us
  waiting for transfers between devices: 465 us -> 78.6 us
  starting transfers between devices: 424 us -> 72.1 us
  local copies, waits for them, and re-layouts: 344 us -> 5.78 us
  other arithmetic: 141 us -> 0.62 us
  Pallas kernels: 0 us -> 56.6 us
  blocking collectives: 0 us -> 19.1 us
    ppermute x172 -> x20, waiting for transfers between devices: 465 us -> 78.6 us  [the longest x1 31.4 us: per_device(): lax.ppermute(halves_2, ('tz', 'ty'), [(i, i + 1) for i in range(15)])]
    ppermute x172 -> x20, starting transfers between devices: 424 us -> 65.3 us  [the longest x8 34.2 us: beside(): return lax.ppermute(block, pieces, pairs)]
    slice x173 -> x0, local copies, waits for them, and re-layouts: 194 us -> none  [the longest x10 138 us: restrict(): return 0.5 * (field[..., 0::2] + field[..., 1::2])]
    add x33 -> x0, other arithmetic: 65.7 us -> none  [the longest x15 29.7 us: coarse_sweep(): chain_start + half_step * (tendency(padded_2(chain_start, (('gx', 2), ('g...]
    while x215 -> x0, local copies, waits for them, and re-layouts: 63.2 us -> none
    pallas_call x0 -> x7, Pallas kernels: none -> 56.6 us  [the longest x4 25 us: stage(): pl.pallas_call(stage_body, out_shape=shapes, in_specs=[pl.BlockSpec(memor...]
    ppermute x70 -> x0, local copies, waits for them, and re-layouts: 49 us -> none  [the longest x35 35 us: padded_2(): lax.ppermute(lax.slice_in_dim(block, block.shape[dim] - width, None, axis...]
    concatenate x40 -> x0, other arithmetic: 37.4 us -> none  [the longest x15 29.4 us: tendency(): upper_side = jnp.roll(centre, -1, axis=1)]
  transfers between devices with their start and end apart: 172 -> 21, of which waited for: 78 -> 13; matrix products, arithmetic and copies ran while one was open for 15% -> 0% of each run, Pallas kernels for 0% -> 0%
where the time goes in v1:
time: 234 us; the launch traced here: 233 us
  waiting for transfers between devices  78.6 us (34%)
  starting transfers between devices  72.1 us (31%)
  Pallas kernels  56.6 us (24%)
  blocking collectives  19.1 us (8%)
  local copies, waits for them, and re-layouts  5.78 us (2%)
    ppermute x8, starting transfers between devices, beside(): return lax.ppermute(block, pieces, pairs)  34.2 us
    ppermute x1, waiting for transfers between devices, per_device(): lax.ppermute(halves_2, ('tz', 'ty'), [(i, i + 1) for i in range(15)])  31.4 us
    ppermute x11, starting transfers between devices, sent(): return lax.ppermute(block, axes if len(axes) > 1 else axes[0], pairs)  27.2 us
    ppermute x11, waiting for transfers between devices, sent(): return lax.ppermute(block, axes if len(axes) > 1 else axes[0], pairs)  25.1 us
    pallas_call x4, Pallas kernels, stage(): pl.pallas_call(stage_body, out_shape=shapes, in_specs=[pl.BlockSpec(memor...  25 us
    pallas_call x1, Pallas kernels, fine_part(): pl.pallas_call(fine_body, out_shape=(jax.ShapeDtypeStruct((128, 1536), f3...  22.1 us
    ppermute x8, waiting for transfers between devices, beside(): return lax.ppermute(block, pieces, pairs)  22.1 us
    all_to_all x1, blocking collectives, per_device(): source = lax.all_to_all(sources.reshape(16, 8, 1536), group_axes, 0, 0)  19.1 us
  transfers between devices with their start and end apart: 21, of which 13 were waited for; matrix products, arithmetic and copies ran while one was open for 0% of the time, Pallas kernels for 0%

profile of v1, /device:TPU:130, one launch (start us, length us, event | category | flops | bytes accessed | tf_op | source)
XLA Modules:
  0.0 233.2 jit_solution(1508757056031430109)
XLA Ops:
  0.0 4.4 %edges.1 = (f32[9,3,16,256]{3,2,1,0:T(8,128)}, f32[9,3,16,256]{3,2,1,0:T(8,128)}, f32[9,16,128]{2,1,0:T(8,128)}, f32[9,16,128]{2,1,0:T(8,128)}) custom-call(f32[4608,128]{1,0:T(8,128)} %bitcast.14), custom_call_target="tpu_custom_call" | custom-call | tf_op jit(solution)/shard_map/edges/pallas_call | solution.py:57
  7.5 4.9 %collective-permute-start.2 = (f32[9,16,128]{2,1,0:T(8,128)}, f32[9,16,128]{2,1,0:T(8,128)S(1)}, u32[]{:S(2)}, u32[]{:S(2)}) collective-permute-start(f32[9,16,128]{2,1,0:T(8,128)} %get-tuple-element.15), channel_id=1, source_target_pairs={{0,5},{1,6},{2,7},{4,9},{5,10},{6,11},{8,13},{9,14},{10,15},{16,21... | collective-permute-start | bytes 221192 | tf_op jit(solution)/shard_map/ppermute | solution.py:364
  12.4 3.1 %collective-permute-start.3 = (f32[9,16,128]{2,1,0:T(8,128)}, f32[9,16,128]{2,1,0:T(8,128)S(1)}, u32[]{:S(2)}, u32[]{:S(2)}) collective-permute-start(f32[9,16,128]{2,1,0:T(8,128)} %get-tuple-element.15), channel_id=1, source_target_pairs={{0,1},{1,2},{2,3},{4,5},{5,6},{6,7},{8,9},{9,10},{10,11},{12,13},{... | collective-permute-start | bytes 221192 | tf_op jit(solution)/shard_map/ppermute | solution.py:364
  16.8 4.3 %collective-permute-start.5 = (f32[9,16,128]{2,1,0:T(8,128)}, f32[9,16,128]{2,1,0:T(8,128)S(1)}, u32[]{:S(2)}, u32[]{:S(2)}) collective-permute-start(f32[9,16,128]{2,1,0:T(8,128)} %get-tuple-element.16), channel_id=1, source_target_pairs={{1,4},{2,5},{3,6},{5,8},{6,9},{7,10},{9,12},{10,13},{11,14},{17,20... | collective-permute-start | bytes 221192 | tf_op jit(solution)/shard_map/ppermute | solution.py:364
  21.1 1.9 collective-permute-start.6
  25.0 2.6 %collective-permute-done.6.north_1 = f32[9,16,128]{2,1,0:T(8,128)S(1)} collective-permute-done((f32[9,16,128]{2,1,0:T(8,128)}, f32[9,16,128]{2,1,0:T(8,128)S(1)}, u32[]{:S(2)}, u32[]{:S(2)}) %collective-permute-start.6) | collective-permute-done | bytes 73760 | tf_op jit(solution)/shard_map/ppermute | solution.py:364
  27.6 3.2 %collective-permute-done.7.north_2 = f32[9,16,128]{2,1,0:T(8,128)S(1)} collective-permute-done((f32[9,16,128]{2,1,0:T(8,128)}, f32[9,16,128]{2,1,0:T(8,128)S(1)}, u32[]{:S(2)}, u32[]{:S(2)}) %collective-permute-start.7) | collective-permute-done | bytes 73760 | tf_op jit(solution)/shard_map/ppermute | solution.py:364
  32.3 22.1 %fine.1 = (f32[128,1536]{1,0:T(8,128)}, f32[128,768]{1,0:T(8,128)}, f32[128,768]{1,0:T(8,128)}) custom-call(s32[4]{0:T(128)} %pad_add_fusion.place, f32[4608,128]{1,0:T(8,128)} %bitcast.15, f32[9,3,16,256]{3,2,1,0:T(8,128)} %copy-done.4, f32[9,3,16,256]{3,2,1,0:T(8,128)} %copy-done.5, f32[9,16,128]{2,1,0:T(8,128)} %copy-done.17, f32[9,16,128]{2,1,0:T(8,128)} %copy-done.18, ...), custom_call_target="tpu_custom_call" | custom-call | tf_op jit(solution)/shard_map/fine/pallas_call | solution.py:205
  54.4 19.1 %all_to_all.10.source = f32[16,8,1536]{2,1,0:T(8,128)S(1)} all-to-all(f32[16,8,1536]{2,1,0:T(8,128)} %bitcast.18), channel_id=1, replica_groups=mesh['tz'=4,'ty'=4,'gx'=4,'gy'=4] {'ty','gx'}, dimensions={0} | all-to-all | bytes 1572864 | tf_op jit(solution)/shard_map/all_to_all | solution.py:390
  73.5 1.9 collective-permute-start.8
  75.4 6.7 %collective-permute-start.9 = (f32[16,8,1536]{2,1,0:T(8,128)S(1)}, f32[16,8,1536]{2,1,0:T(8,128)S(1)}, u32[]{:S(2)}, u32[]{:S(2)}) collective-permute-start(f32[16,8,1536]{2,1,0:T(8,128)S(1)} %all_to_all.10.source), channel_id=1, source_target_pairs={{4,0},{8,4},{12,8},{16,12},{20,16},{24,20},{28,24},{32,28},{36,32}... | collective-permute-start | bytes 2359304 | tf_op jit(solution)/shard_map/ppermute | solution.py:376
  82.1 15.5 %collective-permute-done.8.source_left = f32[16,8,1536]{2,1,0:T(8,128)S(1)} collective-permute-done((f32[16,8,1536]{2,1,0:T(8,128)S(1)}, f32[16,8,1536]{2,1,0:T(8,128)S(1)}, u32[]{:S(2)}, u32[]{:S(2)}) %collective-permute-start.8) | collective-permute-done | bytes 786464 | tf_op jit(solution)/shard_map/ppermute | solution.py:376
  98.8 6.2 %stage.4 = f32[3,8,8,128]{3,2,1,0:T(8,128)} custom-call(s32[4]{0:T(128)} %pad_add_fusion.place, f32[3,8,8,128]{3,2,1,0:T(8,128)} %broadcast_in_dim.3.own.left.right, f32[3,8,8,128]{3,2,1,0:T(8,128)} %broadcast_in_dim.3.own.left.right, f32[3,8,8,128]{3,2,1,0:T(8,128)} %broadcast_in_dim.3.own.left.right, f32[16,8,1536]{2,1,0:T(8,128)} %copy-done, ...), custom_call_target="tpu_custom_call" | custom-call | tf_op jit(solution)/shard_map/stage/pallas_call | solution.py:303
  105.0 3.4 %collective-permute-start.10 = (f32[3,8,8,128]{3,2,1,0:T(8,128)}, f32[3,8,8,128]{3,2,1,0:T(8,128)S(1)}, u32[]{:S(2)}, u32[]{:S(2)}) collective-permute-start(f32[3,8,8,128]{3,2,1,0:T(8,128)} %stage.4), channel_id=1, source_target_pairs={{0,64},{64,128},{128,192},{1,65},{65,129},{129,193},{2,66},{66,130... | collective-permute-start | bytes 294920 | tf_op jit(solution)/shard_map/ppermute | solution.py:364
  108.4 5.6 %collective-permute-done.10.own = f32[3,8,8,128]{3,2,1,0:T(8,128)S(1)} collective-permute-done((f32[3,8,8,128]{3,2,1,0:T(8,128)}, f32[3,8,8,128]{3,2,1,0:T(8,128)S(1)}, u32[]{:S(2)}, u32[]{:S(2)}) %collective-permute-start.10) | collective-permute-done | bytes 98336 | tf_op jit(solution)/shard_map/ppermute | solution.py:364
  114.0 1.9 collective-permute-start.11
  115.9 6.7 %collective-permute-start.12 = (f32[3,8,8,128]{3,2,1,0:T(8,128)S(1)}, f32[3,8,8,128]{3,2,1,0:T(8,128)S(1)}, u32[]{:S(2)}, u32[]{:S(2)}) collective-permute-start(f32[3,8,8,128]{3,2,1,0:T(8,128)S(1)} %collective-permute-done.10.own), channel_id=1, source_target_pairs={{4,0},{8,4},{12,8},{16,12},{20,16},{24,20},{28,24},{32,28},{36,32}... | collective-permute-start | bytes 294920 | tf_op jit(solution)/shard_map/ppermute | solution.py:376
  125.4 6.2 %stage.5 = f32[3,8,8,128]{3,2,1,0:T(8,128)} custom-call(s32[4]{0:T(128)} %pad_add_fusion.place, f32[3,8,8,128]{3,2,1,0:T(8,128)} %copy-done.9, f32[3,8,8,128]{3,2,1,0:T(8,128)} %copy-done.13, f32[3,8,8,128]{3,2,1,0:T(8,128)} %copy-done.15, f32[16,8,1536]{2,1,0:T(8,128)} %copy-done, f32[16,8,1536]{2,1,0:T(8,128)} %copy-done.1, f32[16,8,1536]{2,1,0:T(8,128)} %copy-done.2), custom_call_target="tpu_custom_call" | custom-call | tf_op jit(solution)/shard_map/stage/pallas_call | solution.py:303
  131.6 2.0 collective-permute-start.13
  133.6 6.8 %collective-permute-done.13.own = f32[3,8,8,128]{3,2,1,0:T(8,128)S(1)} collective-permute-done((f32[3,8,8,128]{3,2,1,0:T(8,128)}, f32[3,8,8,128]{3,2,1,0:T(8,128)S(1)}, u32[]{:S(2)}, u32[]{:S(2)}) %collective-permute-start.13) | collective-permute-done | bytes 98336 | tf_op jit(solution)/shard_map/ppermute | solution.py:364
  140.4 1.9 collective-permute-start.14
  142.3 6.7 %collective-permute-start.15 = (f32[3,8,8,128]{3,2,1,0:T(8,128)S(1)}, f32[3,8,8,128]{3,2,1,0:T(8,128)S(1)}, u32[]{:S(2)}, u32[]{:S(2)}) collective-permute-start(f32[3,8,8,128]{3,2,1,0:T(8,128)S(1)} %collective-permute-done.13.own), channel_id=1, source_target_pairs={{4,0},{8,4},{12,8},{16,12},{20,16},{24,20},{28,24},{32,28},{36,32}... | collective-permute-start | bytes 294920 | tf_op jit(solution)/shard_map/ppermute | solution.py:376
  151.8 6.2 %stage.6 = f32[3,8,8,128]{3,2,1,0:T(8,128)} custom-call(s32[4]{0:T(128)} %pad_add_fusion.place, f32[3,8,8,128]{3,2,1,0:T(8,128)} %copy-done.10, f32[3,8,8,128]{3,2,1,0:T(8,128)} %copy-done.14, f32[3,8,8,128]{3,2,1,0:T(8,128)} %copy-done.16, f32[16,8,1536]{2,1,0:T(8,128)} %copy-done, f32[16,8,1536]{2,1,0:T(8,128)} %copy-done.1, f32[16,8,1536]{2,1,0:T(8,128)} %copy-done.2), custom_call_target="tpu_custom_call" | custom-call | tf_op jit(solution)/shard_map/stage/pallas_call | solution.py:303
  158.0 2.0 collective-permute-start.16
  160.1 6.9 %collective-permute-done.16.own = f32[3,8,8,128]{3,2,1,0:T(8,128)S(1)} collective-permute-done((f32[3,8,8,128]{3,2,1,0:T(8,128)}, f32[3,8,8,128]{3,2,1,0:T(8,128)S(1)}, u32[]{:S(2)}, u32[]{:S(2)}) %collective-permute-start.16) | collective-permute-done | bytes 98336 | tf_op jit(solution)/shard_map/ppermute | solution.py:364
  167.0 1.9 collective-permute-start.17
  168.9 6.7 %collective-permute-start.18 = (f32[3,8,8,128]{3,2,1,0:T(8,128)S(1)}, f32[3,8,8,128]{3,2,1,0:T(8,128)S(1)}, u32[]{:S(2)}, u32[]{:S(2)}) collective-permute-start(f32[3,8,8,128]{3,2,1,0:T(8,128)S(1)} %collective-permute-done.16.own), channel_id=1, source_target_pairs={{4,0},{8,4},{12,8},{16,12},{20,16},{24,20},{28,24},{32,28},{36,32}... | collective-permute-start | bytes 294920 | tf_op jit(solution)/shard_map/ppermute | solution.py:376
  178.4 6.4 %stage.7 = (f32[3,8,8,128]{3,2,1,0:T(8,128)}, f32[16,8,2304]{2,1,0:T(8,128)}) custom-call(s32[4]{0:T(128)} %pad_add_fusion.place, f32[3,8,8,128]{3,2,1,0:T(8,128)} %copy-done.8, f32[3,8,8,128]{3,2,1,0:T(8,128)} %copy-done.11, f32[3,8,8,128]{3,2,1,0:T(8,128)} %copy-done.12, f32[16,8,1536]{2,1,0:T(8,128)} %copy-done, f32[16,8,1536]{2,1,0:T(8,128)} %copy-done.1, ...), custom_call_target="tpu_custom_call" | custom-call | tf_op jit(solution)/shard_map/stage/pallas_call | solution.py:303
  184.8 6.8 %all-to-all-start.1 = ((f32[16,8,2304]{2,1,0:T(8,128)}), f32[16,8,2304]{2,1,0:T(8,128)S(1)}, u32[]{:S(2)}, u32[]{:S(2)}) async-start(f32[16,8,2304]{2,1,0:T(8,128)} %get-tuple-element.18), calls=%async_computation.1 | async-start | bytes 2359296 | tf_op jit(solution)/shard_map/all_to_all | solution.py:400
  191.6 3.8 %collective-permute-start.19 = (f32[128,768]{1,0:T(8,128)S(1)}, f32[128,768]{1,0:T(8,128)S(1)}, u32[]{:S(2)}, u32[]{:S(2)}) collective-permute-start(f32[128,768]{1,0:T(8,128)S(1)} %copy-done.6), channel_id=1, source_target_pairs={{0,16},{16,32},{32,48},{48,64},{64,80},{80,96},{96,112},{112,128},... | collective-permute-start | bytes 1179656 | tf_op jit(solution)/shard_map/ppermute | solution.py:389
  195.5 31.4 %collective-permute-done.19.halves_0 = f32[128,768]{1,0:T(8,128)S(1)} collective-permute-done((f32[128,768]{1,0:T(8,128)S(1)}, f32[128,768]{1,0:T(8,128)S(1)}, u32[]{:S(2)}, u32[]{:S(2)}) %collective-permute-start.19) | collective-permute-done | bytes 393248 | tf_op jit(solution)/shard_map/ppermute | solution.py:389
  228.1 5.1 %finish.1 = f32[288,2,8,128]{3,2,1,0:T(8,128)} custom-call(s32[4]{0:T(128)} %pad_add_fusion.place, f32[288,2,8,128]{3,2,1,0:T(8,128)} %bitcast.16, f32[128,2304]{1,0:T(8,128)} %bitcast.17, f32[128,768]{1,0:T(8,128)} %copy-done.7, f32[128,768]{1,0:T(8,128)} %get-tuple-element.20.halves_1, f32[128,768]{1,0:T(8,128)} %get-tuple-element.19.halves_2), custom_call_target="tpu_custom_call" | custom-call | tf_op jit(solution)/shard_map/finish/pallas_call | solution.py:338
  (66 shorter events, 18.6 us)
Async XLA Ops:
  4.4 26.3 %collective-permute-start = (f32[9,3,16,256]{3,2,1,0:T(8,128)}, f32[9,3,16,256]{3,2,1,0:T(8,128)S(1)}, u32[]{:S(2)}, u32[]{:S(2)}) collective-permute-start(f32[9,3,16,256]{3,2,1,0:T(8,128)} %get-tuple-element.13), channel_id=1, source_target_pairs={{0,4},{1,5},{2,6},{3,7},{4,8},{5,9},{6,10},{7,11},{8,12},{9,13},{1... | collective-permute-start | bytes 1327112 | tf_op jit(solution)/shard_map/ppermute | solution.py:364
  6.2 24.6 %collective-permute-start.1 = (f32[9,3,16,256]{3,2,1,0:T(8,128)}, f32[9,3,16,256]{3,2,1,0:T(8,128)S(1)}, u32[]{:S(2)}, u32[]{:S(2)}) collective-permute-start(f32[9,3,16,256]{3,2,1,0:T(8,128)} %get-tuple-element.14), channel_id=1, source_target_pairs={{4,0},{5,1},{6,2},{7,3},{8,4},{9,5},{10,6},{11,7},{12,8},{13,9},{1... | collective-permute-start | bytes 1327112 | tf_op jit(solution)/shard_map/ppermute | solution.py:364
  7.5 9.3 %collective-permute-start.2 = (f32[9,16,128]{2,1,0:T(8,128)}, f32[9,16,128]{2,1,0:T(8,128)S(1)}, u32[]{:S(2)}, u32[]{:S(2)}) collective-permute-start(f32[9,16,128]{2,1,0:T(8,128)} %get-tuple-element.15), channel_id=1, source_target_pairs={{0,5},{1,6},{2,7},{4,9},{5,10},{6,11},{8,13},{9,14},{10,15},{16,21... | collective-permute-start | bytes 221192 | tf_op jit(solution)/shard_map/ppermute | solution.py:364
  12.4 8.7 %collective-permute-start.3 = (f32[9,16,128]{2,1,0:T(8,128)}, f32[9,16,128]{2,1,0:T(8,128)S(1)}, u32[]{:S(2)}, u32[]{:S(2)}) collective-permute-start(f32[9,16,128]{2,1,0:T(8,128)} %get-tuple-element.15), channel_id=1, source_target_pairs={{0,1},{1,2},{2,3},{4,5},{5,6},{6,7},{8,9},{9,10},{10,11},{12,13},{... | collective-permute-start | bytes 221192 | tf_op jit(solution)/shard_map/ppermute | solution.py:364
  15.5 7.6 %collective-permute-start.4 = (f32[9,16,128]{2,1,0:T(8,128)}, f32[9,16,128]{2,1,0:T(8,128)S(1)}, u32[]{:S(2)}, u32[]{:S(2)}) collective-permute-start(f32[9,16,128]{2,1,0:T(8,128)} %get-tuple-element.15), channel_id=1, source_target_pairs={{4,1},{5,2},{6,3},{8,5},{9,6},{10,7},{12,9},{13,10},{14,11},{20,17... | collective-permute-start | bytes 221192 | tf_op jit(solution)/shard_map/ppermute | solution.py:364
  16.8 13.9 %copy-start.17 = (f32[9,16,128]{2,1,0:T(8,128)}, f32[9,16,128]{2,1,0:T(8,128)S(1)}, u32[]{:S(2)}) copy-start(f32[9,16,128]{2,1,0:T(8,128)S(1)} %collective-permute-done.2.south_0) | copy-start | bytes 221188
  16.8 8.2 %collective-permute-start.5 = (f32[9,16,128]{2,1,0:T(8,128)}, f32[9,16,128]{2,1,0:T(8,128)S(1)}, u32[]{:S(2)}, u32[]{:S(2)}) collective-permute-start(f32[9,16,128]{2,1,0:T(8,128)} %get-tuple-element.16), channel_id=1, source_target_pairs={{1,4},{2,5},{3,6},{5,8},{6,9},{7,10},{9,12},{10,13},{11,14},{17,20... | collective-permute-start | bytes 221192 | tf_op jit(solution)/shard_map/ppermute | solution.py:364
  21.1 9.7 %copy-start.18 = (f32[9,16,128]{2,1,0:T(8,128)}, f32[9,16,128]{2,1,0:T(8,128)S(1)}, u32[]{:S(2)}) copy-start(f32[9,16,128]{2,1,0:T(8,128)S(1)} %collective-permute-done.3.south_1) | copy-start | bytes 221188
  21.1 6.5 %collective-permute-start.6 = (f32[9,16,128]{2,1,0:T(8,128)}, f32[9,16,128]{2,1,0:T(8,128)S(1)}, u32[]{:S(2)}, u32[]{:S(2)}) collective-permute-start(f32[9,16,128]{2,1,0:T(8,128)} %get-tuple-element.16), channel_id=1, source_target_pairs={{1,0},{2,1},{3,2},{5,4},{6,5},{7,6},{9,8},{10,9},{11,10},{13,12},{... | collective-permute-start | bytes 221192 | tf_op jit(solution)/shard_map/ppermute | solution.py:364
  23.1 7.7 %copy-start.19 = (f32[9,16,128]{2,1,0:T(8,128)}, f32[9,16,128]{2,1,0:T(8,128)S(1)}, u32[]{:S(2)}) copy-start(f32[9,16,128]{2,1,0:T(8,128)S(1)} %collective-permute-done.4.south_2) | copy-start | bytes 221188
  23.1 7.7 %collective-permute-start.7 = (f32[9,16,128]{2,1,0:T(8,128)}, f32[9,16,128]{2,1,0:T(8,128)S(1)}, u32[]{:S(2)}, u32[]{:S(2)}) collective-permute-start(f32[9,16,128]{2,1,0:T(8,128)} %get-tuple-element.16), channel_id=1, source_target_pairs={{5,0},{6,1},{7,2},{9,4},{10,5},{11,6},{13,8},{14,9},{15,10},{21,16... | collective-permute-start | bytes 221192 | tf_op jit(solution)/shard_map/ppermute | solution.py:364
  25.0 5.8 %copy-start.20 = (f32[9,16,128]{2,1,0:T(8,128)}, f32[9,16,128]{2,1,0:T(8,128)S(1)}, u32[]{:S(2)}) copy-start(f32[9,16,128]{2,1,0:T(8,128)S(1)} %collective-permute-done.5.north_0) | copy-start | bytes 221188
  27.6 3.2 %copy-start.21 = (f32[9,16,128]{2,1,0:T(8,128)}, f32[9,16,128]{2,1,0:T(8,128)S(1)}, u32[]{:S(2)}) copy-start(f32[9,16,128]{2,1,0:T(8,128)S(1)} %collective-permute-done.6.north_1) | copy-start | bytes 221188
  73.5 24.8 %copy-start = (f32[16,8,1536]{2,1,0:T(8,128)}, f32[16,8,1536]{2,1,0:T(8,128)S(1)}, u32[]{:S(2)}) copy-start(f32[16,8,1536]{2,1,0:T(8,128)S(1)} %all_to_all.10.source) | copy-start | bytes 2359300
  73.5 24.1 %collective-permute-start.8 = (f32[16,8,1536]{2,1,0:T(8,128)S(1)}, f32[16,8,1536]{2,1,0:T(8,128)S(1)}, u32[]{:S(2)}, u32[]{:S(2)}) collective-permute-start(f32[16,8,1536]{2,1,0:T(8,128)S(1)} %all_to_all.10.source), channel_id=1, source_target_pairs={{0,4},{4,8},{8,12},{12,16},{16,20},{20,24},{24,28},{28,32},{32,36}... | collective-permute-start | bytes 2359304 | tf_op jit(solution)/shard_map/ppermute | solution.py:376
  75.4 22.2 %collective-permute-start.9 = (f32[16,8,1536]{2,1,0:T(8,128)S(1)}, f32[16,8,1536]{2,1,0:T(8,128)S(1)}, u32[]{:S(2)}, u32[]{:S(2)}) collective-permute-start(f32[16,8,1536]{2,1,0:T(8,128)S(1)} %all_to_all.10.source), channel_id=1, source_target_pairs={{4,0},{8,4},{12,8},{16,12},{20,16},{24,20},{28,24},{32,28},{36,32}... | collective-permute-start | bytes 2359304 | tf_op jit(solution)/shard_map/ppermute | solution.py:376
  105.0 9.0 %collective-permute-start.10 = (f32[3,8,8,128]{3,2,1,0:T(8,128)}, f32[3,8,8,128]{3,2,1,0:T(8,128)S(1)}, u32[]{:S(2)}, u32[]{:S(2)}) collective-permute-start(f32[3,8,8,128]{3,2,1,0:T(8,128)} %stage.4), channel_id=1, source_target_pairs={{0,64},{64,128},{128,192},{1,65},{65,129},{129,193},{2,66},{66,130... | collective-permute-start | bytes 294920 | tf_op jit(solution)/shard_map/ppermute | solution.py:364
  114.0 10.8 %copy-start.9 = (f32[3,8,8,128]{3,2,1,0:T(8,128)}, f32[3,8,8,128]{3,2,1,0:T(8,128)S(1)}, u32[]{:S(2)}) copy-start(f32[3,8,8,128]{3,2,1,0:T(8,128)S(1)} %collective-permute-done.10.own) | copy-start | bytes 294916
  114.0 8.9 %collective-permute-start.11 = (f32[3,8,8,128]{3,2,1,0:T(8,128)S(1)}, f32[3,8,8,128]{3,2,1,0:T(8,128)S(1)}, u32[]{:S(2)}, u32[]{:S(2)}) collective-permute-start(f32[3,8,8,128]{3,2,1,0:T(8,128)S(1)} %collective-permute-done.10.own), channel_id=1, source_target_pairs={{0,4},{4,8},{8,12},{12,16},{16,20},{20,24},{24,28},{28,32},{32,36}... | collective-permute-start | bytes 294920 | tf_op jit(solution)/shard_map/ppermute | solution.py:376
  115.9 8.8 %collective-permute-start.12 = (f32[3,8,8,128]{3,2,1,0:T(8,128)S(1)}, f32[3,8,8,128]{3,2,1,0:T(8,128)S(1)}, u32[]{:S(2)}, u32[]{:S(2)}) collective-permute-start(f32[3,8,8,128]{3,2,1,0:T(8,128)S(1)} %collective-permute-done.10.own), channel_id=1, source_target_pairs={{4,0},{8,4},{12,8},{16,12},{20,16},{24,20},{28,24},{32,28},{36,32}... | collective-permute-start | bytes 294920 | tf_op jit(solution)/shard_map/ppermute | solution.py:376
  131.6 8.8 %collective-permute-start.13 = (f32[3,8,8,128]{3,2,1,0:T(8,128)}, f32[3,8,8,128]{3,2,1,0:T(8,128)S(1)}, u32[]{:S(2)}, u32[]{:S(2)}) collective-permute-start(f32[3,8,8,128]{3,2,1,0:T(8,128)} %stage.5), channel_id=1, source_target_pairs={{0,64},{64,128},{128,192},{1,65},{65,129},{129,193},{2,66},{66,130... | collective-permute-start | bytes 294920 | tf_op jit(solution)/shard_map/ppermute | solution.py:364
  140.4 10.8 %copy-start.10 = (f32[3,8,8,128]{3,2,1,0:T(8,128)}, f32[3,8,8,128]{3,2,1,0:T(8,128)S(1)}, u32[]{:S(2)}) copy-start(f32[3,8,8,128]{3,2,1,0:T(8,128)S(1)} %collective-permute-done.13.own) | copy-start | bytes 294916
  140.4 8.9 %collective-permute-start.14 = (f32[3,8,8,128]{3,2,1,0:T(8,128)S(1)}, f32[3,8,8,128]{3,2,1,0:T(8,128)S(1)}, u32[]{:S(2)}, u32[]{:S(2)}) collective-permute-start(f32[3,8,8,128]{3,2,1,0:T(8,128)S(1)} %collective-permute-done.13.own), channel_id=1, source_target_pairs={{0,4},{4,8},{8,12},{12,16},{16,20},{20,24},{24,28},{28,32},{32,36}... | collective-permute-start | bytes 294920 | tf_op jit(solution)/shard_map/ppermute | solution.py:376
  142.3 8.8 %collective-permute-start.15 = (f32[3,8,8,128]{3,2,1,0:T(8,128)S(1)}, f32[3,8,8,128]{3,2,1,0:T(8,128)S(1)}, u32[]{:S(2)}, u32[]{:S(2)}) collective-permute-start(f32[3,8,8,128]{3,2,1,0:T(8,128)S(1)} %collective-permute-done.13.own), channel_id=1, source_target_pairs={{4,0},{8,4},{12,8},{16,12},{20,16},{24,20},{28,24},{32,28},{36,32}... | collective-permute-start | bytes 294920 | tf_op jit(solution)/shard_map/ppermute | solution.py:376
  158.0 33.6 %copy-start.6 = (f32[128,768]{1,0:T(8,128)S(1)}, f32[128,768]{1,0:T(8,128)}, u32[]{:S(2)}) copy-start(f32[128,768]{1,0:T(8,128)} %get-tuple-element.19.halves_2) | copy-start | bytes 1179652
  158.0 8.9 %collective-permute-start.16 = (f32[3,8,8,128]{3,2,1,0:T(8,128)}, f32[3,8,8,128]{3,2,1,0:T(8,128)S(1)}, u32[]{:S(2)}, u32[]{:S(2)}) collective-permute-start(f32[3,8,8,128]{3,2,1,0:T(8,128)} %stage.6), channel_id=1, source_target_pairs={{0,64},{64,128},{128,192},{1,65},{65,129},{129,193},{2,66},{66,130... | collective-permute-start | bytes 294920 | tf_op jit(solution)/shard_map/ppermute | solution.py:364
  167.0 10.8 %copy-start.8 = (f32[3,8,8,128]{3,2,1,0:T(8,128)}, f32[3,8,8,128]{3,2,1,0:T(8,128)S(1)}, u32[]{:S(2)}) copy-start(f32[3,8,8,128]{3,2,1,0:T(8,128)S(1)} %collective-permute-done.16.own) | copy-start | bytes 294916
  167.0 8.9 %collective-permute-start.17 = (f32[3,8,8,128]{3,2,1,0:T(8,128)S(1)}, f32[3,8,8,128]{3,2,1,0:T(8,128)S(1)}, u32[]{:S(2)}, u32[]{:S(2)}) collective-permute-start(f32[3,8,8,128]{3,2,1,0:T(8,128)S(1)} %collective-permute-done.16.own), channel_id=1, source_target_pairs={{0,4},{4,8},{8,12},{12,16},{16,20},{20,24},{24,28},{28,32},{32,36}... | collective-permute-start | bytes 294920 | tf_op jit(solution)/shard_map/ppermute | solution.py:376
  168.9 8.8 %collective-permute-start.18 = (f32[3,8,8,128]{3,2,1,0:T(8,128)S(1)}, f32[3,8,8,128]{3,2,1,0:T(8,128)S(1)}, u32[]{:S(2)}, u32[]{:S(2)}) collective-permute-start(f32[3,8,8,128]{3,2,1,0:T(8,128)S(1)} %collective-permute-done.16.own), channel_id=1, source_target_pairs={{4,0},{8,4},{12,8},{16,12},{20,16},{24,20},{28,24},{32,28},{36,32}... | collective-permute-start | bytes 294920 | tf_op jit(solution)/shard_map/ppermute | solution.py:376
  175.9 1.8 copy-start.11
  184.8 42.1 %all-to-all-start.1 = ((f32[16,8,2304]{2,1,0:T(8,128)}), f32[16,8,2304]{2,1,0:T(8,128)S(1)}, u32[]{:S(2)}, u32[]{:S(2)}) async-start(f32[16,8,2304]{2,1,0:T(8,128)} %get-tuple-element.18), calls=%async_computation.1 | async-start | bytes 2359296 | tf_op jit(solution)/shard_map/all_to_all | solution.py:400
  191.6 35.3 %collective-permute-start.19 = (f32[128,768]{1,0:T(8,128)S(1)}, f32[128,768]{1,0:T(8,128)S(1)}, u32[]{:S(2)}, u32[]{:S(2)}) collective-permute-start(f32[128,768]{1,0:T(8,128)S(1)} %copy-done.6), channel_id=1, source_target_pairs={{0,16},{16,32},{32,48},{48,64},{64,80},{80,96},{96,112},{112,128},... | collective-permute-start | bytes 1179656 | tf_op jit(solution)/shard_map/ppermute | solution.py:389
  (12 other events, 11.8 us)

commit v2 on v1

--- a/solution.py
+++ b/solution.py
@@ -5,6 +5,7 @@
 from jax.experimental.pallas import tpu as pltpu
 from jax.sharding import Mesh
 from jax.sharding import PartitionSpec as P
+
 
 viscosity = 0.1
 slice_step = 0.25
@@ -57,6 +58,19 @@
     return pl.pallas_call(edges_body, out_shape=(rows, rows, columns, columns), name="edges")(u)
 
 
+def corners_body(south, north, up, down):
+    lane = lanes((16, 128))
+    for k in range(9):
+        turned = pltpu.roll(north[k], 64, 1)
+        up[k] = jnp.where(lane >= 64, south[k], turned)
+        down[k] = jnp.where(lane < 64, south[k], turned)
+
+
+def corners(south, north):
+    shape = jax.ShapeDtypeStruct((9, 16, 128), f32)
+    return pl.pallas_call(corners_body, out_shape=(shape, shape), name="corners")(south, north)
+
+
 def tendency(below, row, above, reach, spacing):
     width = row[0].shape[-1]
     square = 1.0 / (spacing * spacing)
@@ -78,7 +92,7 @@
     return out
 
 
-def fine_body(place, u, before, after, south_0, south_1, south_2, north_0, north_1, north_2,
+def fine_body(place, u, before, after, south, north, corner_before, corner_after,
               sources, halves_1, halves_2, ue, v1, v2, rest, f0, h1, pair_u, pair_v, native_0, native_1):
     gx = place[0]
     gy = place[1]
@@ -97,20 +111,20 @@
             x = e - 3
             if x < 0:
                 ue[k, e, :, 0:256] = before[k, e]
-                a, b, slot = north_0, south_0, 16 + x
+                a, b, slot_a, slot_b = corner_before, corner_before, 8 + x, 16 + x
             elif x < 16:
                 ue[k, e, :, 0:128] = strided(u, k, x, 0)
                 ue[k, e, :, 128:256] = strided(u, k, x, 1)
-                a, b, slot = north_1, south_1, x
+                a, b, slot_a, slot_b = north, south, x, x
             else:
                 ue[k, e, :, 0:256] = after[k, x - 16]
-                a, b, slot = north_2, south_2, x - 16
+                a, b, slot_a, slot_b = corner_after, corner_after, x - 8, x - 16
             a = a[k]
             b = b[k]
-            if slot > 0:
-                a = pltpu.roll(a, 128 - 8 * slot, 1)
-            if slot < 15:
-                b = pltpu.roll(b, 120 - 8 * slot, 1)
+            if slot_a > 0:
+                a = pltpu.roll(a, 128 - 8 * slot_a, 1)
+            if slot_b < 15:
+                b = pltpu.roll(b, 120 - 8 * slot_b, 1)
             ue[k, e, :, 256:384] = jnp.where(lane < 64, a, b)
         return carry
 
@@ -216,6 +230,25 @@
     )(place, *arrays)
 
 
+def pack_body(source, to_right, to_left):
+    row = lax.broadcasted_iota(jnp.int32, (8, 768), 0)
+    for j in range(2):
+        for field in range(2):
+            k = 2 * j + field
+            for xh in range(4):
+                one = source[j * 4 + xh, :, field * 768:(field + 1) * 768]
+                two = source[(3 - j) * 4 + xh, :, (1 - field) * 768:(2 - field) * 768]
+                right = pltpu.roll(two, k, 0) if k else two
+                left = pltpu.roll(two, 8 - k, 0) if k else two
+                to_right[j * 4 + xh, :, field * 768:(field + 1) * 768] = jnp.where(row > k, one, right)
+                to_left[j * 4 + xh, :, field * 768:(field + 1) * 768] = jnp.where(row < 7 - k, one, left)
+
+
+def pack(source):
+    shape = jax.ShapeDtypeStruct((8, 8, 1536), f32)
+    return pl.pallas_call(pack_body, out_shape=(shape, shape), name="pack")(source)
+
+
 def stage_body(place, own, left, right, source, source_left, source_right, *rest):
     *outs, buffer_0, buffer_1 = rest
     last = outs[0]
@@ -246,7 +279,8 @@
     c_second = half_step * viscosity * square
     c_centre = 1.0 - half_step * viscosity * (4.0 + 2.0 * square)
 
-    def step(j, field, old, new):
+    def step(j, field, old, new, late):
+        k = 2 * j + field
         for xh in range(4):
             u = [[old[c, 2 * xh + zh] for zh in range(2)] for c in range(3)]
             for zh in range(2):
@@ -266,8 +300,15 @@
                     north = pltpu.roll(v, 23, 0)
                     south = pltpu.roll(v, 1, 0)
                     at = (field * 6 + c * 2 + zh) * 128
+                    if late:
+                        there = ((1 - field) * 6 + c * 2 + zh) * 128
+                        pull_left = pltpu.roll(source_left[(3 - j) * 4 + xh, :, there:there + 128], 1 + k, 0)
+                        pull_right = pltpu.roll(source_right[(3 - j) * 4 + xh, :, there:there + 128], 7 - k, 0)
+                    else:
+                        pull_left = source_left[j * 4 + xh, :, at:at + 128]
+                        pull_right = source_right[j * 4 + xh, :, at:at + 128]
                     pull = jnp.concatenate(
-                        [r[j * 4 + xh, :, at:at + 128] for r in (source_left, source, source_right)], axis=0
+                        [pull_left, source[j * 4 + xh, :, at:at + 128], pull_right], axis=0
                     )
                     value = (
                         c_centre * v
@@ -278,18 +319,19 @@
                     )
                     new[c, t] = jnp.where(inside, value, 0.0)
 
-    def one_slice(j, carry):
+    def one_slice(j, late):
         if trace is not None:
             keep(j, 0, buffer_0)
-        step(j, 0, buffer_0, buffer_1)
+        step(j, 0, buffer_0, buffer_1, late)
         if trace is not None:
             keep(j, 1, buffer_1)
-        step(j, 1, buffer_1, buffer_0)
+        step(j, 1, buffer_1, buffer_0, late)
         if trace is not None:
             keep(j, 2, buffer_0)
-        return carry
-
-    lax.fori_loop(0, 4, one_slice, 0)
+        return late
+
+    lax.fori_loop(0, 2, lambda j, carry: one_slice(j, False) or carry, 0)
+    lax.fori_loop(2, 4, lambda j, carry: (one_slice(j, True), carry)[1], 0)
     for c in range(3):
         for t in range(8):
             last[c, t] = buffer_0[c, t, 8:16]
@@ -367,7 +409,6 @@
 def solution(mesh):
     sizes = {"tz": 4, "ty": 4, "gx": 4, "gy": 4}
     fine_mesh = Mesh(mesh.devices.reshape(4, 4, 4, 4), tuple(sizes))
-    lateral = ("gx", "gy")
     pieces = ("ty", "gx", "gy")
 
     def beside(block, by):
@@ -381,15 +422,21 @@
         tiles = provisional.reshape(288, 8, 2, 128).transpose(0, 2, 1, 3)
         u = tiles.reshape(4608, 128)
         low_rows, high_rows, low_columns, high_columns = edges(u)
-        after = sent(low_rows, lateral, sizes, {"gx": -1})
-        before = sent(high_rows, lateral, sizes, {"gx": 1})
-        south = [sent(high_columns, lateral, sizes, {"gx": -d, "gy": 1}) for d in (-1, 0, 1)]
-        north = [sent(low_columns, lateral, sizes, {"gx": -d, "gy": -1}) for d in (-1, 0, 1)]
-        sources, halves_1, halves_2 = fine_part(place, u, before, after, *south, *north)
+        after = sent(low_rows, ("gx",), sizes, {"gx": -1})
+        before = sent(high_rows, ("gx",), sizes, {"gx": 1})
+        south = sent(high_columns, ("gy",), sizes, {"gy": 1})
+        north = sent(low_columns, ("gy",), sizes, {"gy": -1})
+        up, down = corners(south, north)
+        corner_before = sent(up, ("gx",), sizes, {"gx": 1})
+        corner_after = sent(down, ("gx",), sizes, {"gx": -1})
+        sources, halves_1, halves_2 = fine_part(
+            place, u, before, after, south, north, corner_before, corner_after
+        )
         halves_0 = lax.ppermute(halves_2, ("tz", "ty"), [(i, i + 1) for i in range(15)])
         source = lax.all_to_all(sources.reshape(16, 8, 1536), group_axes, 0, 0)
-        source_left = beside(source, 1)
-        source_right = beside(source, -1)
+        to_right, to_left = pack(source)
+        source_left = beside(to_right, 1)
+        source_right = beside(to_left, -1)
         own = left = right = jnp.zeros((3, 8, 8, 128), f32)
         for turn in range(4):
             own, *kept = stage(place, own, left, right, source, source_left, source_right, turn == 3)
@@ -402,4 +449,5 @@
         return out.transpose(0, 2, 1, 3).reshape(1, 3, 3, 16, 16, 256)
 
     spec = P(("tz", "ty"), None, None, None, "gx", "gy")
+
     return jax.shard_map(per_device, mesh=fine_mesh, in_specs=(spec,), out_specs=spec, check_vma=False)

time: 234 us -> 225 us (0.962)
  starting transfers between devices: 72.1 us -> 50.2 us
  waiting for transfers between devices: 78.6 us -> 86.3 us
    ppermute x8, starting transfers between devices: 34.2 us -> 22.8 us  [beside(): return lax.ppermute(block, pieces, pairs)]
    ppermute x11 -> x9, starting transfers between devices: 27.2 us -> 19.9 us  [sent(): return lax.ppermute(block, axes if len(axes) > 1 else axes[0], pairs)]
    ppermute x8, waiting for transfers between devices: 22.1 us -> 27.5 us  [beside(): return lax.ppermute(block, pieces, pairs)]
    pallas_call x0 -> x2, Pallas kernels: none -> 3.76 us  [the longest x1 2.08 us: pack(): pl.pallas_call(pack_body, out_shape=(shape, shape), name='pack')(source)]
    all_to_all x1, starting transfers between devices: 6.81 us -> 3.7 us  [per_device(): coarse = lax.all_to_all(kept[0], group_axes, 0, 0).reshape(128, 2304)]
    ppermute x11 -> x9, waiting for transfers between devices: 25.1 us -> 27.3 us  [sent(): return lax.ppermute(block, axes if len(axes) > 1 else axes[0], pairs)]
    unnamed x46 -> x40, local copies, waits for them, and re-layouts: 5.09 us -> 5.53 us
  transfers between devices with their start and end apart: 21 -> 19, of which waited for: 13 -> 12; matrix products, arithmetic and copies ran while one was open for 0% -> 0% of each run, Pallas kernels for 0% -> 1%
where the time goes in v2:
time: 225 us; the launch traced here: 223 us
  waiting for transfers between devices  86.3 us (38%)
  Pallas kernels  58.9 us (26%)
  starting transfers between devices  50.2 us (22%)
  blocking collectives  20.9 us (9%)
  local copies, waits for them, and re-layouts  6.22 us (3%)
    ppermute x1, waiting for transfers between devices, per_device(): lax.ppermute(halves_2, ('tz', 'ty'), [(i, i + 1) for i in range(15)])  31.5 us
    ppermute x8, waiting for transfers between devices, beside(): return lax.ppermute(block, pieces, pairs)  27.5 us
    ppermute x9, waiting for transfers between devices, sent(): return lax.ppermute(block, axes if len(axes) > 1 else axes[0], pairs)  27.3 us
    pallas_call x4, Pallas kernels, stage(): pl.pallas_call(stage_body, out_shape=shapes, in_specs=[pl.BlockSpec(memor...  23.5 us
    ppermute x8, starting transfers between devices, beside(): return lax.ppermute(block, pieces, pairs)  22.8 us
    pallas_call x1, Pallas kernels, fine_part(): pl.pallas_call(fine_body, out_shape=(jax.ShapeDtypeStruct((128, 1536), f3...  22.1 us
    all_to_all x1, blocking collectives, per_device(): source = lax.all_to_all(sources.reshape(16, 8, 1536), group_axes, 0, 0)  20.9 us
    ppermute x9, starting transfers between devices, sent(): return lax.ppermute(block, axes if len(axes) > 1 else axes[0], pairs)  19.9 us
  transfers between devices with their start and end apart: 19, of which 12 were waited for; matrix products, arithmetic and copies ran while one was open for 0% of the time, Pallas kernels for 1%

profile of v2, /device:TPU:130, one launch (start us, length us, event | category | flops | bytes accessed | tf_op | source)
XLA Modules:
  0.0 223.4 jit_solution(3284786345955400369)
XLA Ops:
  0.0 4.4 %edges.1 = (f32[9,3,16,256]{3,2,1,0:T(8,128)}, f32[9,3,16,256]{3,2,1,0:T(8,128)}, f32[9,16,128]{2,1,0:T(8,128)}, f32[9,16,128]{2,1,0:T(8,128)}) custom-call(f32[4608,128]{1,0:T(8,128)} %bitcast.14), custom_call_target="tpu_custom_call" | custom-call | tf_op jit(solution)/shard_map/edges/pallas_call | solution.py:58
  7.5 3.4 %collective-permute-start.2 = (f32[9,16,128]{2,1,0:T(8,128)}, f32[9,16,128]{2,1,0:T(8,128)S(1)}, u32[]{:S(2)}, u32[]{:S(2)}) collective-permute-start(f32[9,16,128]{2,1,0:T(8,128)} %get-tuple-element.19), channel_id=1, source_target_pairs={{0,1},{1,2},{2,3},{4,5},{5,6},{6,7},{8,9},{9,10},{10,11},{12,13},{... | collective-permute-start | bytes 221192 | tf_op jit(solution)/shard_map/ppermute | solution.py:406
  10.9 2.4 %collective-permute-start.3 = (f32[9,16,128]{2,1,0:T(8,128)}, f32[9,16,128]{2,1,0:T(8,128)S(1)}, u32[]{:S(2)}, u32[]{:S(2)}) collective-permute-start(f32[9,16,128]{2,1,0:T(8,128)} %get-tuple-element.20), channel_id=1, source_target_pairs={{1,0},{2,1},{3,2},{5,4},{6,5},{7,6},{9,8},{10,9},{11,10},{13,12},{... | collective-permute-start | bytes 221192 | tf_op jit(solution)/shard_map/ppermute | solution.py:406
  13.9 3.5 %collective-permute-done.3.north = f32[9,16,128]{2,1,0:T(8,128)S(1)} collective-permute-done((f32[9,16,128]{2,1,0:T(8,128)}, f32[9,16,128]{2,1,0:T(8,128)S(1)}, u32[]{:S(2)}, u32[]{:S(2)}) %collective-permute-start.3) | collective-permute-done | bytes 73760 | tf_op jit(solution)/shard_map/ppermute | solution.py:406
  19.8 2.4 %collective-permute-start.4 = (f32[9,16,128]{2,1,0:T(8,128)}, f32[9,16,128]{2,1,0:T(8,128)S(1)}, u32[]{:S(2)}, u32[]{:S(2)}) collective-permute-start(f32[9,16,128]{2,1,0:T(8,128)} %get-tuple-element.21), channel_id=1, source_target_pairs={{0,4},{4,8},{8,12},{1,5},{5,9},{9,13},{2,6},{6,10},{10,14},{3,7},{... | collective-permute-start | bytes 221192 | tf_op jit(solution)/shard_map/ppermute | solution.py:406
  24.1 3.9 %collective-permute-done.5.corner_after = f32[9,16,128]{2,1,0:T(8,128)S(1)} collective-permute-done((f32[9,16,128]{2,1,0:T(8,128)}, f32[9,16,128]{2,1,0:T(8,128)S(1)}, u32[]{:S(2)}, u32[]{:S(2)}) %collective-permute-start.5) | collective-permute-done | bytes 73760 | tf_op jit(solution)/shard_map/ppermute | solution.py:406
  29.6 22.1 %fine.1 = (f32[128,1536]{1,0:T(8,128)}, f32[128,768]{1,0:T(8,128)}, f32[128,768]{1,0:T(8,128)}) custom-call(s32[4]{0:T(128)} %pad_add_fusion.place, f32[4608,128]{1,0:T(8,128)} %bitcast.15, f32[9,3,16,256]{3,2,1,0:T(8,128)} %copy-done.3, f32[9,3,16,256]{3,2,1,0:T(8,128)} %copy-done.4, f32[9,16,128]{2,1,0:T(8,128)} %copy-done.7, f32[9,16,128]{2,1,0:T(8,128)} %copy-done.8, ...), custom_call_target="tpu_custom_call" | custom-call | tf_op jit(solution)/shard_map/fine/pallas_call | solution.py:219
  51.7 20.9 %all_to_all.10.source = f32[16,8,1536]{2,1,0:T(8,128)} all-to-all(f32[16,8,1536]{2,1,0:T(8,128)} %bitcast.18), channel_id=1, replica_groups=mesh['tz'=4,'ty'=4,'gx'=4,'gy'=4] {'ty','gx'}, dimensions={0} | all-to-all | bytes 1572864 | tf_op jit(solution)/shard_map/all_to_all | solution.py:436
  72.6 2.1 pack.1
  76.6 6.7 %collective-permute-start.7 = (f32[8,8,1536]{2,1,0:T(8,128)}, f32[8,8,1536]{2,1,0:T(8,128)S(1)}, u32[]{:S(2)}, u32[]{:S(2)}) collective-permute-start(f32[8,8,1536]{2,1,0:T(8,128)} %get-tuple-element.25), channel_id=1, source_target_pairs={{4,0},{8,4},{12,8},{16,12},{20,16},{24,20},{28,24},{32,28},{36,32}... | collective-permute-start | bytes 1179656 | tf_op jit(solution)/shard_map/ppermute | solution.py:417
  83.3 7.7 %collective-permute-done.6.source_left = f32[8,8,1536]{2,1,0:T(8,128)S(1)} collective-permute-done((f32[8,8,1536]{2,1,0:T(8,128)}, f32[8,8,1536]{2,1,0:T(8,128)S(1)}, u32[]{:S(2)}, u32[]{:S(2)}) %collective-permute-start.6) | collective-permute-done | bytes 393248 | tf_op jit(solution)/shard_map/ppermute | solution.py:417
  91.9 5.8 %stage.4 = f32[3,8,8,128]{3,2,1,0:T(8,128)} custom-call(s32[4]{0:T(128)} %pad_add_fusion.place, f32[3,8,8,128]{3,2,1,0:T(8,128)} %broadcast_in_dim.3.own.left.right, f32[3,8,8,128]{3,2,1,0:T(8,128)} %broadcast_in_dim.3.own.left.right, f32[3,8,8,128]{3,2,1,0:T(8,128)} %broadcast_in_dim.3.own.left.right, f32[16,8,1536]{2,1,0:T(8,128)} %all_to_all.10.source, ...), custom_call_target="tpu_custom_call" | custom-call | tf_op jit(solution)/shard_map/stage/pallas_call | solution.py:345
  97.7 3.4 %collective-permute-start.8 = (f32[3,8,8,128]{3,2,1,0:T(8,128)}, f32[3,8,8,128]{3,2,1,0:T(8,128)S(1)}, u32[]{:S(2)}, u32[]{:S(2)}) collective-permute-start(f32[3,8,8,128]{3,2,1,0:T(8,128)} %stage.4), channel_id=1, source_target_pairs={{0,64},{64,128},{128,192},{1,65},{65,129},{129,193},{2,66},{66,130... | collective-permute-start | bytes 294920 | tf_op jit(solution)/shard_map/ppermute | solution.py:406
  101.1 5.4 %collective-permute-done.8.own = f32[3,8,8,128]{3,2,1,0:T(8,128)S(1)} collective-permute-done((f32[3,8,8,128]{3,2,1,0:T(8,128)}, f32[3,8,8,128]{3,2,1,0:T(8,128)S(1)}, u32[]{:S(2)}, u32[]{:S(2)}) %collective-permute-start.8) | collective-permute-done | bytes 98336 | tf_op jit(solution)/shard_map/ppermute | solution.py:406
  106.5 3.6 %collective-permute-start.10 = (f32[3,8,8,128]{3,2,1,0:T(8,128)S(1)}, f32[3,8,8,128]{3,2,1,0:T(8,128)S(1)}, u32[]{:S(2)}, u32[]{:S(2)}) collective-permute-start(f32[3,8,8,128]{3,2,1,0:T(8,128)S(1)} %collective-permute-done.8.own), channel_id=1, source_target_pairs={{4,0},{8,4},{12,8},{16,12},{20,16},{24,20},{28,24},{32,28},{36,32}... | collective-permute-start | bytes 294920 | tf_op jit(solution)/shard_map/ppermute | solution.py:417
  110.1 1.9 collective-permute-start.9
  113.2 5.9 %collective-permute-done.9.left = f32[3,8,8,128]{3,2,1,0:T(8,128)S(1)} collective-permute-done((f32[3,8,8,128]{3,2,1,0:T(8,128)S(1)}, f32[3,8,8,128]{3,2,1,0:T(8,128)S(1)}, u32[]{:S(2)}, u32[]{:S(2)}) %collective-permute-start.9) | collective-permute-done | bytes 98336 | tf_op jit(solution)/shard_map/ppermute | solution.py:417
  119.7 5.8 %stage.5 = f32[3,8,8,128]{3,2,1,0:T(8,128)} custom-call(s32[4]{0:T(128)} %pad_add_fusion.place, f32[3,8,8,128]{3,2,1,0:T(8,128)} %copy-done.10, f32[3,8,8,128]{3,2,1,0:T(8,128)} %copy-done.16, f32[3,8,8,128]{3,2,1,0:T(8,128)} %copy-done.14, f32[16,8,1536]{2,1,0:T(8,128)} %all_to_all.10.source, f32[8,8,1536]{2,1,0:T(8,128)} %copy-done, f32[8,8,1536]{2,1,0:T(8,128)} %copy-done.1), custom_call_target="tpu_custom_call" | custom-call | tf_op jit(solution)/shard_map/stage/pallas_call | solution.py:345
  125.5 1.9 collective-permute-start.11
  127.4 6.9 %collective-permute-done.11.own = f32[3,8,8,128]{3,2,1,0:T(8,128)S(1)} collective-permute-done((f32[3,8,8,128]{3,2,1,0:T(8,128)}, f32[3,8,8,128]{3,2,1,0:T(8,128)S(1)}, u32[]{:S(2)}, u32[]{:S(2)}) %collective-permute-start.11) | collective-permute-done | bytes 98336 | tf_op jit(solution)/shard_map/ppermute | solution.py:406
  136.2 2.4 %collective-permute-start.12 = (f32[3,8,8,128]{3,2,1,0:T(8,128)S(1)}, f32[3,8,8,128]{3,2,1,0:T(8,128)S(1)}, u32[]{:S(2)}, u32[]{:S(2)}) collective-permute-start(f32[3,8,8,128]{3,2,1,0:T(8,128)S(1)} %collective-permute-done.11.own), channel_id=1, source_target_pairs={{0,4},{4,8},{8,12},{12,16},{16,20},{20,24},{24,28},{28,32},{32,36}... | collective-permute-start | bytes 294920 | tf_op jit(solution)/shard_map/ppermute | solution.py:417
  138.6 6.5 %collective-permute-done.12.left = f32[3,8,8,128]{3,2,1,0:T(8,128)S(1)} collective-permute-done((f32[3,8,8,128]{3,2,1,0:T(8,128)S(1)}, f32[3,8,8,128]{3,2,1,0:T(8,128)S(1)}, u32[]{:S(2)}, u32[]{:S(2)}) %collective-permute-start.12) | collective-permute-done | bytes 98336 | tf_op jit(solution)/shard_map/ppermute | solution.py:417
  145.8 5.8 %stage.6 = f32[3,8,8,128]{3,2,1,0:T(8,128)} custom-call(s32[4]{0:T(128)} %pad_add_fusion.place, f32[3,8,8,128]{3,2,1,0:T(8,128)} %copy-done.11, f32[3,8,8,128]{3,2,1,0:T(8,128)} %copy-done.17, f32[3,8,8,128]{3,2,1,0:T(8,128)} %copy-done.15, f32[16,8,1536]{2,1,0:T(8,128)} %all_to_all.10.source, f32[8,8,1536]{2,1,0:T(8,128)} %copy-done, f32[8,8,1536]{2,1,0:T(8,128)} %copy-done.1), custom_call_target="tpu_custom_call" | custom-call | tf_op jit(solution)/shard_map/stage/pallas_call | solution.py:345
  151.6 2.0 collective-permute-start.14
  153.6 6.9 %collective-permute-done.14.own = f32[3,8,8,128]{3,2,1,0:T(8,128)S(1)} collective-permute-done((f32[3,8,8,128]{3,2,1,0:T(8,128)}, f32[3,8,8,128]{3,2,1,0:T(8,128)S(1)}, u32[]{:S(2)}, u32[]{:S(2)}) %collective-permute-start.14) | collective-permute-done | bytes 98336 | tf_op jit(solution)/shard_map/ppermute | solution.py:406
  162.5 2.6 %collective-permute-start.15 = (f32[3,8,8,128]{3,2,1,0:T(8,128)S(1)}, f32[3,8,8,128]{3,2,1,0:T(8,128)S(1)}, u32[]{:S(2)}, u32[]{:S(2)}) collective-permute-start(f32[3,8,8,128]{3,2,1,0:T(8,128)S(1)} %collective-permute-done.14.own), channel_id=1, source_target_pairs={{0,4},{4,8},{8,12},{12,16},{16,20},{20,24},{24,28},{28,32},{32,36}... | collective-permute-start | bytes 294920 | tf_op jit(solution)/shard_map/ppermute | solution.py:417
  165.1 6.3 %collective-permute-done.15.left = f32[3,8,8,128]{3,2,1,0:T(8,128)S(1)} collective-permute-done((f32[3,8,8,128]{3,2,1,0:T(8,128)S(1)}, f32[3,8,8,128]{3,2,1,0:T(8,128)S(1)}, u32[]{:S(2)}, u32[]{:S(2)}) %collective-permute-start.15) | collective-permute-done | bytes 98336 | tf_op jit(solution)/shard_map/ppermute | solution.py:417
  172.1 6.1 %stage.7 = (f32[3,8,8,128]{3,2,1,0:T(8,128)}, f32[16,8,2304]{2,1,0:T(8,128)}) custom-call(s32[4]{0:T(128)} %pad_add_fusion.place, f32[3,8,8,128]{3,2,1,0:T(8,128)} %copy-done.9, f32[3,8,8,128]{3,2,1,0:T(8,128)} %copy-done.13, f32[3,8,8,128]{3,2,1,0:T(8,128)} %copy-done.12, f32[16,8,1536]{2,1,0:T(8,128)} %all_to_all.10.source, f32[8,8,1536]{2,1,0:T(8,128)} %copy-done, ...), custom_call_target="tpu_custom_call" | custom-call | tf_op jit(solution)/shard_map/stage/pallas_call | solution.py:345
  178.2 3.7 %all-to-all-start.1 = ((f32[16,8,2304]{2,1,0:T(8,128)}), f32[16,8,2304]{2,1,0:T(8,128)S(1)}, u32[]{:S(2)}, u32[]{:S(2)}) async-start(f32[16,8,2304]{2,1,0:T(8,128)} %get-tuple-element.26), calls=%async_computation.1 | async-start | bytes 2359296 | tf_op jit(solution)/shard_map/all_to_all | solution.py:447
  181.9 3.7 %collective-permute-start.17 = (f32[128,768]{1,0:T(8,128)S(1)}, f32[128,768]{1,0:T(8,128)S(1)}, u32[]{:S(2)}, u32[]{:S(2)}) collective-permute-start(f32[128,768]{1,0:T(8,128)S(1)} %copy-done.5), channel_id=1, source_target_pairs={{0,16},{16,32},{32,48},{48,64},{64,80},{80,96},{96,112},{112,128},... | collective-permute-start | bytes 1179656 | tf_op jit(solution)/shard_map/ppermute | solution.py:435
  185.7 31.5 %collective-permute-done.17.halves_0 = f32[128,768]{1,0:T(8,128)S(1)} collective-permute-done((f32[128,768]{1,0:T(8,128)S(1)}, f32[128,768]{1,0:T(8,128)S(1)}, u32[]{:S(2)}, u32[]{:S(2)}) %collective-permute-start.17) | collective-permute-done | bytes 393248 | tf_op jit(solution)/shard_map/ppermute | solution.py:435
  218.3 5.1 %finish.1 = f32[288,2,8,128]{3,2,1,0:T(8,128)} custom-call(s32[4]{0:T(128)} %pad_add_fusion.place, f32[288,2,8,128]{3,2,1,0:T(8,128)} %bitcast.16, f32[128,2304]{1,0:T(8,128)} %bitcast.17, f32[128,768]{1,0:T(8,128)} %copy-done.6, f32[128,768]{1,0:T(8,128)} %get-tuple-element.28.halves_1, f32[128,768]{1,0:T(8,128)} %get-tuple-element.27.halves_2), custom_call_target="tpu_custom_call" | custom-call | tf_op jit(solution)/shard_map/finish/pallas_call | solution.py:380
  (58 shorter events, 20.4 us)
Async XLA Ops:
  4.4 23.7 %collective-permute-start = (f32[9,3,16,256]{3,2,1,0:T(8,128)}, f32[9,3,16,256]{3,2,1,0:T(8,128)S(1)}, u32[]{:S(2)}, u32[]{:S(2)}) collective-permute-start(f32[9,3,16,256]{3,2,1,0:T(8,128)} %get-tuple-element.17), channel_id=1, source_target_pairs={{0,4},{4,8},{8,12},{1,5},{5,9},{9,13},{2,6},{6,10},{10,14},{3,7},{... | collective-permute-start | bytes 1327112 | tf_op jit(solution)/shard_map/ppermute | solution.py:406
  6.2 21.9 %collective-permute-start.1 = (f32[9,3,16,256]{3,2,1,0:T(8,128)}, f32[9,3,16,256]{3,2,1,0:T(8,128)S(1)}, u32[]{:S(2)}, u32[]{:S(2)}) collective-permute-start(f32[9,3,16,256]{3,2,1,0:T(8,128)} %get-tuple-element.18), channel_id=1, source_target_pairs={{4,0},{8,4},{12,8},{5,1},{9,5},{13,9},{6,2},{10,6},{14,10},{7,3},{... | collective-permute-start | bytes 1327112 | tf_op jit(solution)/shard_map/ppermute | solution.py:406
  7.5 6.5 %collective-permute-start.2 = (f32[9,16,128]{2,1,0:T(8,128)}, f32[9,16,128]{2,1,0:T(8,128)S(1)}, u32[]{:S(2)}, u32[]{:S(2)}) collective-permute-start(f32[9,16,128]{2,1,0:T(8,128)} %get-tuple-element.19), channel_id=1, source_target_pairs={{0,1},{1,2},{2,3},{4,5},{5,6},{6,7},{8,9},{9,10},{10,11},{12,13},{... | collective-permute-start | bytes 221192 | tf_op jit(solution)/shard_map/ppermute | solution.py:406
  10.9 6.6 %collective-permute-start.3 = (f32[9,16,128]{2,1,0:T(8,128)}, f32[9,16,128]{2,1,0:T(8,128)S(1)}, u32[]{:S(2)}, u32[]{:S(2)}) collective-permute-start(f32[9,16,128]{2,1,0:T(8,128)} %get-tuple-element.20), channel_id=1, source_target_pairs={{1,0},{2,1},{3,2},{5,4},{6,5},{7,6},{9,8},{10,9},{11,10},{13,12},{... | collective-permute-start | bytes 221192 | tf_op jit(solution)/shard_map/ppermute | solution.py:406
  13.9 3.5 %copy-start.7 = (f32[9,16,128]{2,1,0:T(8,128)}, f32[9,16,128]{2,1,0:T(8,128)S(1)}, u32[]{:S(2)}) copy-start(f32[9,16,128]{2,1,0:T(8,128)S(1)} %collective-permute-done.2.south) | copy-start | bytes 221188
  19.8 4.4 %collective-permute-start.4 = (f32[9,16,128]{2,1,0:T(8,128)}, f32[9,16,128]{2,1,0:T(8,128)S(1)}, u32[]{:S(2)}, u32[]{:S(2)}) collective-permute-start(f32[9,16,128]{2,1,0:T(8,128)} %get-tuple-element.21), channel_id=1, source_target_pairs={{0,4},{4,8},{8,12},{1,5},{5,9},{9,13},{2,6},{6,10},{10,14},{3,7},{... | collective-permute-start | bytes 221192 | tf_op jit(solution)/shard_map/ppermute | solution.py:406
  22.2 5.9 %collective-permute-start.5 = (f32[9,16,128]{2,1,0:T(8,128)}, f32[9,16,128]{2,1,0:T(8,128)S(1)}, u32[]{:S(2)}, u32[]{:S(2)}) collective-permute-start(f32[9,16,128]{2,1,0:T(8,128)} %get-tuple-element.22), channel_id=1, source_target_pairs={{4,0},{8,4},{12,8},{5,1},{9,5},{13,9},{6,2},{10,6},{14,10},{7,3},{... | collective-permute-start | bytes 221192 | tf_op jit(solution)/shard_map/ppermute | solution.py:406
  24.1 3.9 %copy-start.18 = (f32[9,16,128]{2,1,0:T(8,128)}, f32[9,16,128]{2,1,0:T(8,128)S(1)}, u32[]{:S(2)}) copy-start(f32[9,16,128]{2,1,0:T(8,128)S(1)} %collective-permute-done.4.corner_before) | copy-start | bytes 221188
  28.1 0.8 copy-start.3
  74.7 16.2 %collective-permute-start.6 = (f32[8,8,1536]{2,1,0:T(8,128)}, f32[8,8,1536]{2,1,0:T(8,128)S(1)}, u32[]{:S(2)}, u32[]{:S(2)}) collective-permute-start(f32[8,8,1536]{2,1,0:T(8,128)} %get-tuple-element.24), channel_id=1, source_target_pairs={{0,4},{4,8},{8,12},{12,16},{16,20},{20,24},{24,28},{28,32},{32,36}... | collective-permute-start | bytes 1179656 | tf_op jit(solution)/shard_map/ppermute | solution.py:417
  76.6 14.3 %collective-permute-start.7 = (f32[8,8,1536]{2,1,0:T(8,128)}, f32[8,8,1536]{2,1,0:T(8,128)S(1)}, u32[]{:S(2)}, u32[]{:S(2)}) collective-permute-start(f32[8,8,1536]{2,1,0:T(8,128)} %get-tuple-element.25), channel_id=1, source_target_pairs={{4,0},{8,4},{12,8},{16,12},{20,16},{24,20},{28,24},{32,28},{36,32}... | collective-permute-start | bytes 1179656 | tf_op jit(solution)/shard_map/ppermute | solution.py:417
  91.0 0.8 copy-start
  91.0 0.9 copy-start.1
  97.7 8.8 %collective-permute-start.8 = (f32[3,8,8,128]{3,2,1,0:T(8,128)}, f32[3,8,8,128]{3,2,1,0:T(8,128)S(1)}, u32[]{:S(2)}, u32[]{:S(2)}) collective-permute-start(f32[3,8,8,128]{3,2,1,0:T(8,128)} %stage.4), channel_id=1, source_target_pairs={{0,64},{64,128},{128,192},{1,65},{65,129},{129,193},{2,66},{66,130... | collective-permute-start | bytes 294920 | tf_op jit(solution)/shard_map/ppermute | solution.py:406
  106.5 12.5 %copy-start.10 = (f32[3,8,8,128]{3,2,1,0:T(8,128)}, f32[3,8,8,128]{3,2,1,0:T(8,128)S(1)}, u32[]{:S(2)}) copy-start(f32[3,8,8,128]{3,2,1,0:T(8,128)S(1)} %collective-permute-done.8.own) | copy-start | bytes 294916
  106.5 6.6 %collective-permute-start.10 = (f32[3,8,8,128]{3,2,1,0:T(8,128)S(1)}, f32[3,8,8,128]{3,2,1,0:T(8,128)S(1)}, u32[]{:S(2)}, u32[]{:S(2)}) collective-permute-start(f32[3,8,8,128]{3,2,1,0:T(8,128)S(1)} %collective-permute-done.8.own), channel_id=1, source_target_pairs={{4,0},{8,4},{12,8},{16,12},{20,16},{24,20},{28,24},{32,28},{36,32}... | collective-permute-start | bytes 294920 | tf_op jit(solution)/shard_map/ppermute | solution.py:417
  110.1 8.9 %collective-permute-start.9 = (f32[3,8,8,128]{3,2,1,0:T(8,128)S(1)}, f32[3,8,8,128]{3,2,1,0:T(8,128)S(1)}, u32[]{:S(2)}, u32[]{:S(2)}) collective-permute-start(f32[3,8,8,128]{3,2,1,0:T(8,128)S(1)} %collective-permute-done.8.own), channel_id=1, source_target_pairs={{0,4},{4,8},{8,12},{12,16},{16,20},{20,24},{24,28},{28,32},{32,36}... | collective-permute-start | bytes 294920 | tf_op jit(solution)/shard_map/ppermute | solution.py:417
  113.2 5.9 %copy-start.14 = (f32[3,8,8,128]{3,2,1,0:T(8,128)}, f32[3,8,8,128]{3,2,1,0:T(8,128)S(1)}, u32[]{:S(2)}) copy-start(f32[3,8,8,128]{3,2,1,0:T(8,128)S(1)} %collective-permute-done.10.right) | copy-start | bytes 294916
  125.5 8.8 %collective-permute-start.11 = (f32[3,8,8,128]{3,2,1,0:T(8,128)}, f32[3,8,8,128]{3,2,1,0:T(8,128)S(1)}, u32[]{:S(2)}, u32[]{:S(2)}) collective-permute-start(f32[3,8,8,128]{3,2,1,0:T(8,128)} %stage.5), channel_id=1, source_target_pairs={{0,64},{64,128},{128,192},{1,65},{65,129},{129,193},{2,66},{66,130... | collective-permute-start | bytes 294920 | tf_op jit(solution)/shard_map/ppermute | solution.py:406
  134.3 10.9 %copy-start.11 = (f32[3,8,8,128]{3,2,1,0:T(8,128)}, f32[3,8,8,128]{3,2,1,0:T(8,128)S(1)}, u32[]{:S(2)}) copy-start(f32[3,8,8,128]{3,2,1,0:T(8,128)S(1)} %collective-permute-done.11.own) | copy-start | bytes 294916
  134.3 4.3 %collective-permute-start.13 = (f32[3,8,8,128]{3,2,1,0:T(8,128)S(1)}, f32[3,8,8,128]{3,2,1,0:T(8,128)S(1)}, u32[]{:S(2)}, u32[]{:S(2)}) collective-permute-start(f32[3,8,8,128]{3,2,1,0:T(8,128)S(1)} %collective-permute-done.11.own), channel_id=1, source_target_pairs={{4,0},{8,4},{12,8},{16,12},{20,16},{24,20},{28,24},{32,28},{36,32}... | collective-permute-start | bytes 294920 | tf_op jit(solution)/shard_map/ppermute | solution.py:417
  136.2 8.9 %collective-permute-start.12 = (f32[3,8,8,128]{3,2,1,0:T(8,128)S(1)}, f32[3,8,8,128]{3,2,1,0:T(8,128)S(1)}, u32[]{:S(2)}, u32[]{:S(2)}) collective-permute-start(f32[3,8,8,128]{3,2,1,0:T(8,128)S(1)} %collective-permute-done.11.own), channel_id=1, source_target_pairs={{0,4},{4,8},{8,12},{12,16},{16,20},{20,24},{24,28},{28,32},{32,36}... | collective-permute-start | bytes 294920 | tf_op jit(solution)/shard_map/ppermute | solution.py:417
  138.6 6.5 %copy-start.15 = (f32[3,8,8,128]{3,2,1,0:T(8,128)}, f32[3,8,8,128]{3,2,1,0:T(8,128)S(1)}, u32[]{:S(2)}) copy-start(f32[3,8,8,128]{3,2,1,0:T(8,128)S(1)} %collective-permute-done.13.right) | copy-start | bytes 294916
  151.6 30.3 %copy-start.5 = (f32[128,768]{1,0:T(8,128)S(1)}, f32[128,768]{1,0:T(8,128)}, u32[]{:S(2)}) copy-start(f32[128,768]{1,0:T(8,128)} %get-tuple-element.27.halves_2) | copy-start | bytes 1179652
  151.6 8.9 %collective-permute-start.14 = (f32[3,8,8,128]{3,2,1,0:T(8,128)}, f32[3,8,8,128]{3,2,1,0:T(8,128)S(1)}, u32[]{:S(2)}, u32[]{:S(2)}) collective-permute-start(f32[3,8,8,128]{3,2,1,0:T(8,128)} %stage.6), channel_id=1, source_target_pairs={{0,64},{64,128},{128,192},{1,65},{65,129},{129,193},{2,66},{66,130... | collective-permute-start | bytes 294920 | tf_op jit(solution)/shard_map/ppermute | solution.py:406
  160.5 10.9 %copy-start.9 = (f32[3,8,8,128]{3,2,1,0:T(8,128)}, f32[3,8,8,128]{3,2,1,0:T(8,128)S(1)}, u32[]{:S(2)}) copy-start(f32[3,8,8,128]{3,2,1,0:T(8,128)S(1)} %collective-permute-done.14.own) | copy-start | bytes 294916
  160.5 4.5 %collective-permute-start.16 = (f32[3,8,8,128]{3,2,1,0:T(8,128)S(1)}, f32[3,8,8,128]{3,2,1,0:T(8,128)S(1)}, u32[]{:S(2)}, u32[]{:S(2)}) collective-permute-start(f32[3,8,8,128]{3,2,1,0:T(8,128)S(1)} %collective-permute-done.14.own), channel_id=1, source_target_pairs={{4,0},{8,4},{12,8},{16,12},{20,16},{24,20},{28,24},{32,28},{36,32}... | collective-permute-start | bytes 294920 | tf_op jit(solution)/shard_map/ppermute | solution.py:417
  162.5 8.9 %collective-permute-start.15 = (f32[3,8,8,128]{3,2,1,0:T(8,128)S(1)}, f32[3,8,8,128]{3,2,1,0:T(8,128)S(1)}, u32[]{:S(2)}, u32[]{:S(2)}) collective-permute-start(f32[3,8,8,128]{3,2,1,0:T(8,128)S(1)} %collective-permute-done.14.own), channel_id=1, source_target_pairs={{0,4},{4,8},{8,12},{12,16},{16,20},{20,24},{24,28},{28,32},{32,36}... | collective-permute-start | bytes 294920 | tf_op jit(solution)/shard_map/ppermute | solution.py:417
  165.1 6.3 %copy-start.12 = (f32[3,8,8,128]{3,2,1,0:T(8,128)}, f32[3,8,8,128]{3,2,1,0:T(8,128)S(1)}, u32[]{:S(2)}) copy-start(f32[3,8,8,128]{3,2,1,0:T(8,128)S(1)} %collective-permute-done.16.right) | copy-start | bytes 294916
  178.2 38.9 %all-to-all-start.1 = ((f32[16,8,2304]{2,1,0:T(8,128)}), f32[16,8,2304]{2,1,0:T(8,128)S(1)}, u32[]{:S(2)}, u32[]{:S(2)}) async-start(f32[16,8,2304]{2,1,0:T(8,128)} %get-tuple-element.26), calls=%async_computation.1 | async-start | bytes 2359296 | tf_op jit(solution)/shard_map/all_to_all | solution.py:447
  181.9 35.2 %collective-permute-start.17 = (f32[128,768]{1,0:T(8,128)S(1)}, f32[128,768]{1,0:T(8,128)S(1)}, u32[]{:S(2)}, u32[]{:S(2)}) collective-permute-start(f32[128,768]{1,0:T(8,128)S(1)} %copy-done.5), channel_id=1, source_target_pairs={{0,16},{16,32},{32,48},{48,64},{64,80},{80,96},{96,112},{112,128},... | collective-permute-start | bytes 1179656 | tf_op jit(solution)/shard_map/ppermute | solution.py:435
  217.1 1.2 copy-start.2
  (7 other events, 4.7 us)

commit v3 on v2

v3 whole, which is shorter than its diff:
```python
import functools

import jax
import jax.numpy as jnp
from jax import lax
from jax.experimental import pallas as pl
from jax.experimental.pallas import tpu as pltpu
from jax.sharding import Mesh
from jax.sharding import PartitionSpec as P


viscosity = 0.1
slice_step = 0.25
half_step = 0.125
first_row = (5.0 / 24.0, 1.0 / 3.0, -1.0 / 24.0)
second_row = (-1.0 / 24.0, 1.0 / 3.0, 5.0 / 24.0)

f32 = jnp.float32
group_axes = ("ty", "gx")


def near(*arrays):
    return tuple(pltpu.with_memory_space_constraint(a, pltpu.VMEM) for a in arrays)


def lanes(shape):
    return lax.broadcasted_iota(jnp.int32, shape, len(shape) - 1)


def strided(u, k, x, half):
    at = k * 512 + x // 8 * 16 + half * 8 + x % 8
    return jnp.concatenate([u[pl.ds(at + 32 * odd, 8, stride=64), :] for odd in (0, 1)], axis=0)


def edges_body(u, low_rows, high_rows, low_columns, high_columns):
    slot = lanes((16, 128)) // 8
    k = pl.program_id(0)
    left = jnp.zeros((16, 128), f32)
    right = jnp.zeros((16, 128), f32)
    for x in range(16):
        a = strided(u, 0, x, 0)
        b = strided(u, 0, x, 1)
        if x < 3:
            low_rows[k, x, :, 0:128] = a
            low_rows[k, x, :, 128:256] = b
        if x > 12:
            high_rows[k, x - 13, :, 0:128] = a
            high_rows[k, x - 13, :, 128:256] = b
        turned_a = pltpu.roll(a, 8 * x, 1) if x else a
        turned_b = pltpu.roll(b, (8 * x + 8) % 128, 1) if x < 15 else b
        left = jnp.where(slot == x, turned_a, left)
        right = jnp.where(slot == x, turned_b, right)
    low_columns[k] = left
    high_columns[k] = right


def edges(u):
    vmem = pl.BlockSpec(memory_space=pltpu.VMEM)
    rows = pltpu.VMEM((9, 3, 16, 256), f32)
    columns = pltpu.VMEM((9, 16, 128), f32)
    return pl.pallas_call(
        edges_body,
        grid=(9,),
        in_specs=[pl.BlockSpec((512, 128), lambda k: (k, 0))],
        out_specs=[vmem] * 4,
        out_shape=(rows, rows, columns, columns),
        compiler_params=pltpu.CompilerParams(vmem_limit_bytes=8 * 2**20),
        name="edges",
    )(u)


def corners_body(south, north, up, down):
    lane = lanes((16, 128))
    for k in range(9):
        turned = pltpu.roll(north[k], 64, 1)
        up[k] = jnp.where(lane >= 64, south[k], turned)
        down[k] = jnp.where(lane < 64, south[k], turned)


def corners(south, north):
    vmem = pl.BlockSpec(memory_space=pltpu.VMEM)
    shape = pltpu.VMEM((9, 16, 128), f32)
    return pl.pallas_call(
        corners_body,
        in_specs=[vmem] * 2,
        out_specs=[vmem] * 2,
        out_shape=(shape, shape),
        compiler_params=pltpu.CompilerParams(vmem_limit_bytes=8 * 2**20),
        name="corners",
    )(*near(south, north))


def tendency(below, row, above, reach, spacing):
    width = row[0].shape[-1]
    square = 1.0 / (spacing * spacing)
    out = []
    for c in range(3):
        u = row[c]
        up = jnp.concatenate([u[8:16], pltpu.roll(u[0:8], 7, 0)], axis=0)
        down = jnp.concatenate([pltpu.roll(u[8:16], 1, 0), u[0:8]], axis=0)
        north = pltpu.roll(u, width - reach, 1)
        south = pltpu.roll(u, reach, 1)
        laplace = (above[c] + below[c]) + (up + down) - (4.0 + 2.0 * square) * u
        laplace = laplace + (north + south) * square
        transport = (
            row[0] * (above[c] - below[c])
            + row[1] * ((north - south) * (1.0 / spacing))
            + row[2] * (up - down)
        )
        out.append(viscosity * laplace - 0.5 * transport)
    return out


def fine_body(place, u, before, after, south, north, corner_before, corner_after,
              sources, halves_1, halves_2, ue, v1, v2, rest, f0, h1, pair_u, pair_v, native_0, native_1, turned):
    gx = place[0]
    gy = place[1]
    leader = place[2] == 0
    lane = lanes((16, 128))
    wide = lanes((16, 384))
    even = wide % 2 == 0
    low_ok = jnp.where(gx > 0, 1.0, 0.0).astype(f32)
    high_ok = jnp.where(gx < 3, 1.0, 0.0).astype(f32)
    north_ok = jnp.where(gy < 3, 1.0, 0.0).astype(f32)
    south_ok = jnp.where(gy > 0, 1.0, 0.0).astype(f32)
    columns_ok = jnp.where(wide < 256, 1.0, jnp.where(wide < 320, north_ok, south_ok))

    def gather(k, carry):
        for e in range(22):
            x = e - 3
            if x < 0:
                ue[k, e, :, 0:256] = before[k, e]
                a, b, slot_a, slot_b = corner_before, corner_before, 8 + x, 16 + x
            elif x < 16:
                ue[k, e, :, 0:128] = strided(u, k, x, 0)
                ue[k, e, :, 128:256] = strided(u, k, x, 1)
                a, b, slot_a, slot_b = north, south, x, x
            else:
                ue[k, e, :, 0:256] = after[k, x - 16]
                a, b, slot_a, slot_b = corner_after, corner_after, x - 8, x - 16
            a = a[k]
            b = b[k]
            if slot_a > 0:
                a = pltpu.roll(a, 128 - 8 * slot_a, 1)
            if slot_b < 15:
                b = pltpu.roll(b, 120 - 8 * slot_b, 1)
            ue[k, e, :, 256:384] = jnp.where(lane < 64, a, b)
        return carry

    lax.fori_loop(0, 9, gather, 0)

    def row_ok(e):
        return jnp.where(e < 3, low_ok, jnp.where(e > 18, high_ok, 1.0))

    def paired(field):
        return 0.5 * (field + jnp.where(even, pltpu.roll(field, 383, 1), pltpu.roll(field, 1, 1)))

    def first(e, carry):
        flux = []
        for node in range(3):
            rows = [[ue[3 * node + c, e + d] for c in range(3)] for d in (-1, 0, 1)]
            flux.append(tendency(*rows, 1, 1.0))
        ok = columns_ok * row_ok(e)
        for c in range(3):
            a, b, d = flux[0][c], flux[1][c], flux[2][c]
            start = ue[c, e]
            new = start + slice_step * (first_row[0] * a + first_row[1] * b + first_row[2] * d)
            new = new * ok
            v1[c, e] = new
            rest[c, e] = (
                slice_step * (second_row[0] * a + second_row[1] * b + second_row[2] * d)
                - half_step * b
            )
            f0[c, e] = a
            pair_u[c, e] = paired(start)
            pair_v[c, e] = paired(new)
        return carry

    lax.fori_loop(1, 21, first, 0)

    def second(e, carry):
        rows = [[v1[c, e + d] for c in range(3)] for d in (-1, 0, 1)]
        slope = tendency(*rows, 1, 1.0)
        ok = columns_ok * row_ok(e)
        for c in range(3):
            v2[c, e] = (rows[1][c] + half_step * slope[c] + rest[c, e]) * ok
            h1[c, e] = slope[c]
        return carry

    lax.fori_loop(2, 20, second, 0)

    def put(field, c, x, value):
        for odd in (0, 1):
            at = pl.ds((field * 3 + c) * 256 + x % 2 * 128 + x // 2 + odd * 8, 8, stride=16)
            native_0[at, :] = value[odd * 8:odd * 8 + 8, 0:128]
            native_1[at, :] = value[odd * 8:odd * 8 + 8, 128:256]

    def third(e, carry):
        rows = [[v2[c, e + d] for c in range(3)] for d in (-1, 0, 1)]
        slope = tendency(*rows, 1, 1.0)
        base_u = tendency(*[[pair_u[c, e + d] for c in range(3)] for d in (-1, 0, 1)], 2, 2.0)
        base_v = tendency(*[[pair_v[c, e + d] for c in range(3)] for d in (-1, 0, 1)], 2, 2.0)
        for c in range(3):
            a, b, d = f0[c, e], h1[c, e], slope[c]
            one = slice_step * (first_row[0] * a + first_row[1] * b + first_row[2] * d)
            two = slice_step * (second_row[0] * a + second_row[1] * b + second_row[2] * d)
            one = one + jnp.where(leader, ue[c, e], -half_step * base_u[c])
            two = two - half_step * base_v[c]
            put(0, c, e - 3, one)
            put(1, c, e - 3, two)
            put(2, c, e - 3, v1[c, e])
            put(3, c, e - 3, rows[1][c])
        return carry

    lax.fori_loop(3, 19, third, 0)

    def compact(c, carry):
        for field in range(4):
            for odd in (0, 1):
                start = pl.multiple_of((field * 3 + c) * 256 + odd * 128, 128)
                for half, native in enumerate((native_0, native_1)):
                    at = (field * 2 + odd) * 2 + half
                    turned[at] = native[pl.ds(start, 128), :].T
                    one = turned[at, pl.ds(0, 64, stride=2), :]
                    two = turned[at, pl.ds(1, 64, stride=2), :]
                    rows = pl.ds(half * 64, 64)
                    tile = pl.ds(pl.multiple_of(c * 256 + odd * 128, 128), 128)
                    if field < 2:
                        tile = pl.ds(pl.multiple_of(field * 768 + c * 256 + odd * 128, 128), 128)
                        sources[rows, tile] = 0.5 * (one + two)
                    elif field == 2:
                        halves_1[rows, tile] = 0.5 * (one - two)
                    else:
                        halves_2[rows, tile] = 0.5 * (one - two)
        return carry

    lax.fori_loop(0, 3, compact, 0)


def fine_part(place, u, *arrays):
    vmem = pl.BlockSpec(memory_space=pltpu.VMEM)
    field = pltpu.VMEM((3, 22, 16, 384), f32)
    return pl.pallas_call(
        fine_body,
        out_shape=(pltpu.VMEM((128, 1536), f32), pltpu.VMEM((128, 768), f32), pltpu.VMEM((128, 768), f32)),
        in_specs=[pl.BlockSpec(memory_space=pltpu.SMEM)] + [vmem] * (1 + len(arrays)),
        out_specs=[vmem] * 3,
        scratch_shapes=[pltpu.VMEM((9, 22, 16, 384), f32)]
        + [field] * 7
        + [pltpu.VMEM((3072, 128), f32)] * 2
        + [pltpu.VMEM((16, 128, 128), f32)],
        compiler_params=pltpu.CompilerParams(vmem_limit_bytes=36 * 2**20),
        name="fine",
    )(place, u, *near(*arrays))


def pack_body(source, to_right, to_left):
    row = lax.broadcasted_iota(jnp.int32, (8, 768), 0)
    for j in range(2):
        for field in range(2):
            k = 2 * j + field
            for xh in range(4):
                one = source[j * 4 + xh, :, field * 768:(field + 1) * 768]
                two = source[(3 - j) * 4 + xh, :, (1 - field) * 768:(2 - field) * 768]
                right = pltpu.roll(two, k, 0) if k else two
                left = pltpu.roll(two, 8 - k, 0) if k else two
                to_right[j * 4 + xh, :, field * 768:(field + 1) * 768] = jnp.where(row > k, one, right)
                to_left[j * 4 + xh, :, field * 768:(field + 1) * 768] = jnp.where(row < 7 - k, one, left)


def pack(source):
    vmem = pl.BlockSpec(memory_space=pltpu.VMEM)
    shape = pltpu.VMEM((8, 8, 1536), f32)
    return pl.pallas_call(
        pack_body,
        in_specs=[vmem],
        out_specs=[vmem] * 2,
        out_shape=(shape, shape),
        compiler_params=pltpu.CompilerParams(vmem_limit_bytes=8 * 2**20),
        name="pack",
    )(*near(source))


def stage_body(place, *rest, begins, ends):
    rest = list(rest)
    starts = () if begins else (rest.pop(0), rest.pop(0), rest.pop(0))
    source, source_left, source_right, result, buffer_0, buffer_1 = rest
    lane = lanes((24, 128))
    x_first = lane % 8 == 0
    x_last = lane % 8 == 7
    row = lax.broadcasted_iota(jnp.int32, (24, 128), 0)
    inside = ((row >= 8) | (place[3] > 0)) & ((row < 16) | (place[3] < 63))

    for c in range(3):
        for t in range(8):
            for buffer in (buffer_0, buffer_1):
                buffer[c, t, 0:8] = jnp.zeros((8, 128), f32)
                buffer[c, t, 32:40] = jnp.zeros((8, 128), f32)
            if begins:
                buffer_0[c, t, 8:32] = jnp.zeros((24, 128), f32)
            else:
                own, left, right = starts
                buffer_0[c, t, 8:16] = left[c, t]
                buffer_0[c, t, 16:24] = own[c, t]
                buffer_0[c, t, 24:32] = right[c, t]

    def keep(j, field, buffer):
        for xh in range(4):
            for c in range(3):
                for odd in range(2):
                    at = (field * 6 + c * 2 + odd) * 128
                    result[j * 4 + xh, :, at:at + 128] = buffer[c, xh * 2 + odd, 16:24]

    square = 0.25
    c_side = half_step * viscosity
    c_second = half_step * viscosity * square
    c_centre = 1.0 - half_step * viscosity * (4.0 + 2.0 * square)

    def step(j, field, old, new, late):
        k = 2 * j + field
        for xh in range(4):
            for odd in range(2):
                t = 2 * xh + odd
                u = [old[c, t, 8:32] for c in range(3)]
                k0 = u[0] * (-0.5 * half_step)
                k1 = u[1] * (-0.25 * half_step)
                k2 = u[2] * (-0.5 * half_step)
                for c in range(3):
                    v = u[c]
                    other = old[c, t + 1 - 2 * odd, 8:32]
                    if odd:
                        beyond = pltpu.roll(old[c, t + 1, 8:32], 7, 1) if xh < 3 else 0.0
                        east = jnp.where(x_last, beyond, pltpu.roll(other, 127, 1))
                        west = other
                    else:
                        beyond = pltpu.roll(old[c, t - 1, 8:32], 121, 1) if xh > 0 else 0.0
                        east = other
                        west = jnp.where(x_first, beyond, pltpu.roll(other, 1, 1))
                    up = pltpu.roll(v, 120, 1)
                    down = pltpu.roll(v, 8, 1)
                    north = old[c, t, 9:33]
                    south = old[c, t, 7:31]
                    at = (field * 6 + c * 2 + odd) * 128
                    if late:
                        there = ((1 - field) * 6 + c * 2 + odd) * 128
                        pull_left = pltpu.roll(source_left[(3 - j) * 4 + xh, :, there:there + 128], (1 + k) % 8, 0)
                        pull_right = pltpu.roll(source_right[(3 - j) * 4 + xh, :, there:there + 128], 7 - k, 0)
                    else:
                        pull_left = source_left[j * 4 + xh, :, at:at + 128]
                        pull_right = source_right[j * 4 + xh, :, at:at + 128]
                    pull = jnp.concatenate(
                        [pull_left, source[j * 4 + xh, :, at:at + 128], pull_right], axis=0
                    )
                    value = (
                        c_centre * v
                        + c_side * ((east + west) + (up + down))
                        + c_second * (north + south)
                        + (k0 * (east - west) + k1 * (north - south) + k2 * (up - down))
                        + pull
                    )
                    new[c, t, 8:32] = jnp.where(inside, value, 0.0)

    def one_slice(j, late):
        if ends:
            keep(j, 0, buffer_0)
        step(j, 0, buffer_0, buffer_1, late)
        if ends:
            keep(j, 1, buffer_1)
        step(j, 1, buffer_1, buffer_0, late)
        if ends:
            keep(j, 2, buffer_0)

    def early(j, carry):
        one_slice(j, False)
        return carry

    def later(j, carry):
        one_slice(j, True)
        return carry

    lax.fori_loop(0, 2, early, 0)
    lax.fori_loop(2, 4, later, 0)
    if not ends:
        for c in range(3):
            for t in range(8):
                result[c, t] = buffer_0[c, t, 16:24]


def stage(place, starts, sources, ends):
    vmem = pl.BlockSpec(memory_space=pltpu.VMEM)
    arrays = near(*starts, *sources)
    return pl.pallas_call(
        functools.partial(stage_body, begins=not starts, ends=ends),
        out_shape=pltpu.VMEM((16, 8, 2304) if ends else (3, 8, 8, 128), f32),
        in_specs=[pl.BlockSpec(memory_space=pltpu.SMEM)] + [vmem] * len(arrays),
        out_specs=vmem,
        scratch_shapes=[pltpu.VMEM((3, 8, 40, 128), f32)] * 2,
        compiler_params=pltpu.CompilerParams(vmem_limit_bytes=12 * 2**20),
        name="stage",
    )(place, *arrays)


def finish_body(place, start, coarse, halves_0, halves_1, halves_2, out, mixed, rows):
    for field, halves in enumerate((halves_0, halves_1, halves_2)):
        def each(c, carry):
            for half in range(2):
                part = pl.ds(half * 64, 64)
                for odd in range(2):
                    tile = pl.multiple_of(c * 256 + odd * 128, 128)
                    w = coarse[part, pl.ds(field * 768 + tile, 128)]
                    e = halves[part, pl.ds(tile, 128)]
                    at = half * 2 + odd
                    mixed[at, pl.ds(0, 64, stride=2), :] = w + e
                    mixed[at, pl.ds(1, 64, stride=2), :] = w - e
                    rows[half, pl.ds(odd, 128, stride=2), :] = mixed[at].T
                out[pl.ds((field * 3 + c) * 32, 32), half] = rows[half].reshape(32, 8, 128)
            return carry

        lax.fori_loop(0, 3, each, 0)

    @pl.when(place[2] == 0)
    def _():
        pltpu.sync_copy(start.at[pl.ds(0, 96)], out.at[pl.ds(0, 96)])


def finish(place, start, coarse, *halves):
    vmem = pl.BlockSpec(memory_space=pltpu.VMEM)
    return pl.pallas_call(
        finish_body,
        out_shape=jax.ShapeDtypeStruct((288, 2, 8, 128), f32),
        in_specs=[pl.BlockSpec(memory_space=pltpu.SMEM), pl.BlockSpec(memory_space=pl.ANY)] + [vmem] * 4,
        scratch_shapes=[pltpu.VMEM((4, 128, 128), f32), pltpu.VMEM((2, 256, 128), f32)],
        compiler_params=pltpu.CompilerParams(vmem_limit_bytes=16 * 2**20),
        name="finish",
    )(place, start, *near(coarse, *halves))


def sent(block, axes, sizes, moves):
    strides = {}
    total = 1
    for axis in reversed(axes):
        strides[axis] = total
        total *= sizes[axis]
    pairs = []
    for source in range(total):
        target = source
        for axis, by in moves.items():
            at = source // strides[axis] % sizes[axis]
            if not 0 <= at + by < sizes[axis]:
                target = None
                break
            target += by * strides[axis]
        if target is not None:
            pairs.append((source, target))
    return lax.ppermute(block, axes if len(axes) > 1 else axes[0], pairs)


def solution(mesh):
    sizes = {"tz": 4, "ty": 4, "gx": 4, "gy": 4}
    fine_mesh = Mesh(mesh.devices.reshape(4, 4, 4, 4), tuple(sizes))
    pieces = ("ty", "gx", "gy")

    def beside(block, by):
        name = lambda piece: (piece % 16) * 4 + piece // 16
        pairs = [(name(i), name(i + by)) for i in range(64) if 0 <= i + by < 64]
        return lax.ppermute(block, pieces, pairs)

    def per_device(provisional):
        tz, ty, gx, gy = (lax.axis_index(a) for a in sizes)
        place = jnp.stack([gx, gy, tz * 4 + ty, gy * 16 + ty * 4 + gx]).astype(jnp.int32)
        tiles = provisional.reshape(288, 8, 2, 128).transpose(0, 2, 1, 3)
        u = tiles.reshape(4608, 128)
        low_rows, high_rows, low_columns, high_columns = edges(u)
        after = sent(low_rows, ("gx",), sizes, {"gx": -1})
        before = sent(high_rows, ("gx",), sizes, {"gx": 1})
        south = sent(high_columns, ("gy",), sizes, {"gy": 1})
        north = sent(low_columns, ("gy",), sizes, {"gy": -1})
        up, down = corners(south, north)
        corner_before = sent(up, ("gx",), sizes, {"gx": 1})
        corner_after = sent(down, ("gx",), sizes, {"gx": -1})
        sources, halves_1, halves_2 = fine_part(
            place, u, before, after, south, north, corner_before, corner_after
        )
        halves_0 = lax.ppermute(halves_2, ("tz", "ty"), [(i, i + 1) for i in range(15)])
        source = lax.all_to_all(sources.reshape(16, 8, 1536), group_axes, 0, 0)
        to_right, to_left = pack(source)
        source_left = beside(to_right, 1)
        source_right = beside(to_left, -1)
        starts = ()
        for turn in range(4):
            own = stage(place, starts, (source, source_left, source_right), turn == 3)
            if turn < 3:
                own = sent(own, ("tz",), sizes, {"tz": 1})
                starts = (own, beside(own, 1), beside(own, -1))
        coarse = lax.all_to_all(own, group_axes, 0, 0).reshape(128, 2304)
        out = finish(place, tiles, coarse, halves_0, halves_1, halves_2)
        return out.transpose(0, 2, 1, 3).reshape(1, 3, 3, 16, 16, 256)

    spec = P(("tz", "ty"), None, None, None, "gx", "gy")

    return jax.shard_map(per_device, mesh=fine_mesh, in_specs=(spec,), out_specs=spec, check_vma=False)
```

time: 225 us -> 201 us (0.89)
  Pallas kernels: 58.9 us -> 36.1 us
    pallas_call x8, Pallas kernels: 53.8 us -> 32.5 us  [the longest x1 17 us: fine_part(): pl.pallas_call(fine_body, out_shape=(pltpu.VMEM((128, 1536), f32), pltpu....]
    unnamed x40 -> x18, local copies, waits for them, and re-layouts: 5.53 us -> 6.44 us
  transfers between devices with their start and end apart: 19 -> 19, of which waited for: 12 -> 12; matrix products, arithmetic and copies ran while one was open for 0% -> 0% of each run, Pallas kernels for 1% -> 0%
where the time goes in v3:
time: 201 us; the launch traced here: 199 us
  waiting for transfers between devices  85.9 us (43%)
  starting transfers between devices  50 us (25%)
  Pallas kernels  36.1 us (18%)
  blocking collectives  20.6 us (10%)
  local copies, waits for them, and re-layouts  6.44 us (3%)
    ppermute x1, waiting for transfers between devices, per_device(): lax.ppermute(halves_2, ('tz', 'ty'), [(i, i + 1) for i in range(15)])  31.6 us
    ppermute x8, waiting for transfers between devices, beside(): return lax.ppermute(block, pieces, pairs)  27.5 us
    ppermute x9, waiting for transfers between devices, sent(): return lax.ppermute(block, axes if len(axes) > 1 else axes[0], pairs)  26.7 us
    ppermute x8, starting transfers between devices, beside(): return lax.ppermute(block, pieces, pairs)  22.7 us
    all_to_all x1, blocking collectives, per_device(): source = lax.all_to_all(sources.reshape(16, 8, 1536), group_axes, 0, 0)  20.6 us
    ppermute x9, starting transfers between devices, sent(): return lax.ppermute(block, axes if len(axes) > 1 else axes[0], pairs)  19.9 us
    pallas_call x1, Pallas kernels, fine_part(): pl.pallas_call(fine_body, out_shape=(pltpu.VMEM((128, 1536), f32), pltpu....  17 us
    pallas_call x4, Pallas kernels, stage(): pl.pallas_call(functools.partial(stage_body, begins=not starts, ends=ends...  12.7 us
  transfers between devices with their start and end apart: 19, of which 12 were waited for; matrix products, arithmetic and copies ran while one was open for 0% of the time, Pallas kernels for 0%

profile of v3, /device:TPU:130, one launch (start us, length us, event | category | flops | bytes accessed | tf_op | source)
XLA Modules:
  0.0 199.4 jit_solution(5871536899394586273)
XLA Ops:
  1.7 2.7 %edges.1 = (f32[9,3,16,256]{3,2,1,0:T(8,128)}, f32[9,3,16,256]{3,2,1,0:T(8,128)}, f32[9,16,128]{2,1,0:T(8,128)S(1)}, f32[9,16,128]{2,1,0:T(8,128)S(1)}) custom-call(f32[4608,128]{1,0:T(8,128)S(1)} %bitcast.14), custom_call_target="tpu_custom_call" | custom-call | tf_op jit(solution)/shard_map/edges/pallas_call | solution.py:61
  7.4 3.4 %collective-permute-start.2 = (f32[9,16,128]{2,1,0:T(8,128)S(1)}, f32[9,16,128]{2,1,0:T(8,128)S(1)}, u32[]{:S(2)}, u32[]{:S(2)}) collective-permute-start(f32[9,16,128]{2,1,0:T(8,128)S(1)} %get-tuple-element.18), channel_id=1, source_target_pairs={{0,1},{1,2},{2,3},{4,5},{5,6},{6,7},{8,9},{9,10},{10,11},{12,13},{... | collective-permute-start | bytes 221192 | tf_op jit(solution)/shard_map/ppermute | solution.py:455
  10.9 2.4 %collective-permute-start.3 = (f32[9,16,128]{2,1,0:T(8,128)S(1)}, f32[9,16,128]{2,1,0:T(8,128)S(1)}, u32[]{:S(2)}, u32[]{:S(2)}) collective-permute-start(f32[9,16,128]{2,1,0:T(8,128)S(1)} %get-tuple-element.19), channel_id=1, source_target_pairs={{1,0},{2,1},{3,2},{5,4},{6,5},{7,6},{9,8},{10,9},{11,10},{13,12},{... | collective-permute-start | bytes 221192 | tf_op jit(solution)/shard_map/ppermute | solution.py:455
  13.7 3.5 %collective-permute-done.3.north = f32[9,16,128]{2,1,0:T(8,128)S(1)} collective-permute-done((f32[9,16,128]{2,1,0:T(8,128)S(1)}, f32[9,16,128]{2,1,0:T(8,128)S(1)}, u32[]{:S(2)}, u32[]{:S(2)}) %collective-permute-start.3) | collective-permute-done | bytes 73760 | tf_op jit(solution)/shard_map/ppermute | solution.py:455
  17.3 2.4 %collective-permute-start.4 = (f32[9,16,128]{2,1,0:T(8,128)S(1)}, f32[9,16,128]{2,1,0:T(8,128)S(1)}, u32[]{:S(2)}, u32[]{:S(2)}) collective-permute-start(f32[9,16,128]{2,1,0:T(8,128)S(1)} %get-tuple-element.20), channel_id=1, source_target_pairs={{0,4},{4,8},{8,12},{1,5},{5,9},{9,13},{2,6},{6,10},{10,14},{3,7},{... | collective-permute-start | bytes 221192 | tf_op jit(solution)/shard_map/ppermute | solution.py:455
  21.1 4.3 %collective-permute-done.5.corner_after = f32[9,16,128]{2,1,0:T(8,128)S(1)} collective-permute-done((f32[9,16,128]{2,1,0:T(8,128)S(1)}, f32[9,16,128]{2,1,0:T(8,128)S(1)}, u32[]{:S(2)}, u32[]{:S(2)}) %collective-permute-start.5) | collective-permute-done | bytes 73760 | tf_op jit(solution)/shard_map/ppermute | solution.py:455
  25.4 17.0 %fine.1 = (f32[128,1536]{1,0:T(8,128)S(1)}, f32[128,768]{1,0:T(8,128)S(1)}, f32[128,768]{1,0:T(8,128)S(1)}) custom-call(s32[4]{0:T(128)S(1)} %pad_add_fusion.place, f32[4608,128]{1,0:T(8,128)S(1)} %bitcast.15, f32[9,3,16,256]{3,2,1,0:T(8,128)S(1)} %collective-permute-done.before, f32[9,3,16,256]{3,2,1,0:T(8,128)S(1)} %collective-permute-done.1.after, ...), custom_call_target="tpu_custom_call" | custom-call | tf_op jit(solution)/shard_map/fine/pallas_call | solution.py:243
  42.5 20.6 %all_to_all.10.source.rest_0_.rest_3_ = f32[16,8,1536]{2,1,0:T(8,128)S(1)} all-to-all(f32[16,8,1536]{2,1,0:T(8,128)S(1)} %bitcast.18), channel_id=1, replica_groups=mesh['tz'=4,'ty'=4,'gx'=4,'gy'=4] {'ty','gx'}, dimensions={0} | all-to-all | bytes 1572864 | tf_op jit(solution)/shard_map/all_to_all | solution.py:485
  63.2 1.9 collective-permute-start.6
  65.1 6.7 %collective-permute-start.7 = (f32[8,8,1536]{2,1,0:T(8,128)S(1)}, f32[8,8,1536]{2,1,0:T(8,128)S(1)}, u32[]{:S(2)}, u32[]{:S(2)}) collective-permute-start(f32[8,8,1536]{2,1,0:T(8,128)S(1)} %get-tuple-element.24), channel_id=1, source_target_pairs={{4,0},{8,4},{12,8},{16,12},{20,16},{24,20},{28,24},{32,28},{36,32}... | collective-permute-start | bytes 1179656 | tf_op jit(solution)/shard_map/ppermute | solution.py:466
  71.7 7.5 %collective-permute-done.6.rest_1_.rest_4_ = f32[8,8,1536]{2,1,0:T(8,128)S(1)} collective-permute-done((f32[8,8,1536]{2,1,0:T(8,128)S(1)}, f32[8,8,1536]{2,1,0:T(8,128)S(1)}, u32[]{:S(2)}, u32[]{:S(2)}) %collective-permute-start.6) | collective-permute-done | bytes 393248 | tf_op jit(solution)/shard_map/ppermute | solution.py:466
  79.2 3.2 %stage.4 = f32[3,8,8,128]{3,2,1,0:T(8,128)S(1)} custom-call(s32[4]{0:T(128)S(1)} %pad_add_fusion.place, f32[16,8,1536]{2,1,0:T(8,128)S(1)} %all_to_all.10.source.rest_0_.rest_3_, f32[8,8,1536]{2,1,0:T(8,128)S(1)} %collective-permute-done.6.rest_1_.rest_4_, f32[8,8,1536]{2,1,0:T(8,128)S(1)} %collective-permute-done.7.rest_2_.rest_5_), custom_call_target="tpu_custom_call" | custom-call | tf_op jit(solution)/shard_map/stage/pallas_call | solution.py:392
  82.4 3.4 %collective-permute-start.8 = (f32[3,8,8,128]{3,2,1,0:T(8,128)S(1)}, f32[3,8,8,128]{3,2,1,0:T(8,128)S(1)}, u32[]{:S(2)}, u32[]{:S(2)}) collective-permute-start(f32[3,8,8,128]{3,2,1,0:T(8,128)S(1)} %stage.4), channel_id=1, source_target_pairs={{0,64},{64,128},{128,192},{1,65},{65,129},{129,193},{2,66},{66,130... | collective-permute-start | bytes 294920 | tf_op jit(solution)/shard_map/ppermute | solution.py:455
  85.8 5.2 %collective-permute-done.8.rest_0_ = f32[3,8,8,128]{3,2,1,0:T(8,128)S(1)} collective-permute-done((f32[3,8,8,128]{3,2,1,0:T(8,128)S(1)}, f32[3,8,8,128]{3,2,1,0:T(8,128)S(1)}, u32[]{:S(2)}, u32[]{:S(2)}) %collective-permute-start.8) | collective-permute-done | bytes 98336 | tf_op jit(solution)/shard_map/ppermute | solution.py:455
  91.0 3.6 %collective-permute-start.10 = (f32[3,8,8,128]{3,2,1,0:T(8,128)S(1)}, f32[3,8,8,128]{3,2,1,0:T(8,128)S(1)}, u32[]{:S(2)}, u32[]{:S(2)}) collective-permute-start(f32[3,8,8,128]{3,2,1,0:T(8,128)S(1)} %collective-permute-done.8.rest_0_), channel_id=1, source_target_pairs={{4,0},{8,4},{12,8},{16,12},{20,16},{24,20},{28,24},{32,28},{36,32}... | collective-permute-start | bytes 294920 | tf_op jit(solution)/shard_map/ppermute | solution.py:466
  94.6 1.9 collective-permute-start.9
  97.7 5.8 %collective-permute-done.9.rest_1_ = f32[3,8,8,128]{3,2,1,0:T(8,128)S(1)} collective-permute-done((f32[3,8,8,128]{3,2,1,0:T(8,128)S(1)}, f32[3,8,8,128]{3,2,1,0:T(8,128)S(1)}, u32[]{:S(2)}, u32[]{:S(2)}) %collective-permute-start.9) | collective-permute-done | bytes 98336 | tf_op jit(solution)/shard_map/ppermute | solution.py:466
  103.5 3.2 %stage.5 = f32[3,8,8,128]{3,2,1,0:T(8,128)S(1)} custom-call(s32[4]{0:T(128)S(1)} %pad_add_fusion.place, f32[3,8,8,128]{3,2,1,0:T(8,128)S(1)} %collective-permute-done.8.rest_0_, f32[3,8,8,128]{3,2,1,0:T(8,128)S(1)} %collective-permute-done.9.rest_1_, f32[3,8,8,128]{3,2,1,0:T(8,128)S(1)} %collective-permute-done.10.rest_2_, ...), custom_call_target="tpu_custom_call" | custom-call | tf_op jit(solution)/shard_map/stage/pallas_call | solution.py:392
  106.7 2.1 %collective-permute-start.11 = (f32[3,8,8,128]{3,2,1,0:T(8,128)S(1)}, f32[3,8,8,128]{3,2,1,0:T(8,128)S(1)}, u32[]{:S(2)}, u32[]{:S(2)}) collective-permute-start(f32[3,8,8,128]{3,2,1,0:T(8,128)S(1)} %stage.5), channel_id=1, source_target_pairs={{0,64},{64,128},{128,192},{1,65},{65,129},{129,193},{2,66},{66,130... | collective-permute-start | bytes 294920 | tf_op jit(solution)/shard_map/ppermute | solution.py:455
  108.8 6.6 %collective-permute-done.11.rest_0_ = f32[3,8,8,128]{3,2,1,0:T(8,128)S(1)} collective-permute-done((f32[3,8,8,128]{3,2,1,0:T(8,128)S(1)}, f32[3,8,8,128]{3,2,1,0:T(8,128)S(1)}, u32[]{:S(2)}, u32[]{:S(2)}) %collective-permute-start.11) | collective-permute-done | bytes 98336 | tf_op jit(solution)/shard_map/ppermute | solution.py:455
  117.3 2.4 %collective-permute-start.12 = (f32[3,8,8,128]{3,2,1,0:T(8,128)S(1)}, f32[3,8,8,128]{3,2,1,0:T(8,128)S(1)}, u32[]{:S(2)}, u32[]{:S(2)}) collective-permute-start(f32[3,8,8,128]{3,2,1,0:T(8,128)S(1)} %collective-permute-done.11.rest_0_), channel_id=1, source_target_pairs={{0,4},{4,8},{8,12},{12,16},{16,20},{20,24},{24,28},{28,32},{32,36}... | collective-permute-start | bytes 294920 | tf_op jit(solution)/shard_map/ppermute | solution.py:466
  119.7 6.5 %collective-permute-done.12.rest_1_ = f32[3,8,8,128]{3,2,1,0:T(8,128)S(1)} collective-permute-done((f32[3,8,8,128]{3,2,1,0:T(8,128)S(1)}, f32[3,8,8,128]{3,2,1,0:T(8,128)S(1)}, u32[]{:S(2)}, u32[]{:S(2)}) %collective-permute-start.12) | collective-permute-done | bytes 98336 | tf_op jit(solution)/shard_map/ppermute | solution.py:466
  126.2 3.2 %stage.6 = f32[3,8,8,128]{3,2,1,0:T(8,128)S(1)} custom-call(s32[4]{0:T(128)S(1)} %pad_add_fusion.place, f32[3,8,8,128]{3,2,1,0:T(8,128)S(1)} %collective-permute-done.11.rest_0_, f32[3,8,8,128]{3,2,1,0:T(8,128)S(1)} %collective-permute-done.12.rest_1_, f32[3,8,8,128]{3,2,1,0:T(8,128)S(1)} %collective-permute-done.13.rest_2_, ...), custom_call_target="tpu_custom_call" | custom-call | tf_op jit(solution)/shard_map/stage/pallas_call | solution.py:392
  129.4 1.9 collective-permute-start.14
  131.3 6.7 %collective-permute-done.14.rest_0_ = f32[3,8,8,128]{3,2,1,0:T(8,128)S(1)} collective-permute-done((f32[3,8,8,128]{3,2,1,0:T(8,128)S(1)}, f32[3,8,8,128]{3,2,1,0:T(8,128)S(1)}, u32[]{:S(2)}, u32[]{:S(2)}) %collective-permute-start.14) | collective-permute-done | bytes 98336 | tf_op jit(solution)/shard_map/ppermute | solution.py:455
  139.9 2.4 %collective-permute-start.15 = (f32[3,8,8,128]{3,2,1,0:T(8,128)S(1)}, f32[3,8,8,128]{3,2,1,0:T(8,128)S(1)}, u32[]{:S(2)}, u32[]{:S(2)}) collective-permute-start(f32[3,8,8,128]{3,2,1,0:T(8,128)S(1)} %collective-permute-done.14.rest_0_), channel_id=1, source_target_pairs={{0,4},{4,8},{8,12},{12,16},{16,20},{20,24},{24,28},{28,32},{32,36}... | collective-permute-start | bytes 294920 | tf_op jit(solution)/shard_map/ppermute | solution.py:466
  142.3 6.5 %collective-permute-done.15.rest_1_ = f32[3,8,8,128]{3,2,1,0:T(8,128)S(1)} collective-permute-done((f32[3,8,8,128]{3,2,1,0:T(8,128)S(1)}, f32[3,8,8,128]{3,2,1,0:T(8,128)S(1)}, u32[]{:S(2)}, u32[]{:S(2)}) %collective-permute-start.15) | collective-permute-done | bytes 98336 | tf_op jit(solution)/shard_map/ppermute | solution.py:466
  148.9 3.2 %stage.7 = f32[16,8,2304]{2,1,0:T(8,128)S(1)} custom-call(s32[4]{0:T(128)S(1)} %pad_add_fusion.place, f32[3,8,8,128]{3,2,1,0:T(8,128)S(1)} %collective-permute-done.14.rest_0_, f32[3,8,8,128]{3,2,1,0:T(8,128)S(1)} %collective-permute-done.15.rest_1_, f32[3,8,8,128]{3,2,1,0:T(8,128)S(1)} %collective-permute-done.16.rest_2_, ...), custom_call_target="tpu_custom_call" | custom-call | tf_op jit(solution)/shard_map/stage/pallas_call | solution.py:392
  153.1 3.7 %all-to-all-start.1 = ((f32[16,8,2304]{2,1,0:T(8,128)}), f32[16,8,2304]{2,1,0:T(8,128)S(1)}, u32[]{:S(2)}, u32[]{:S(2)}) async-start(f32[16,8,2304]{2,1,0:T(8,128)} %copy-done.2), calls=%async_computation.1 | async-start | bytes 2359296 | tf_op jit(solution)/shard_map/all_to_all | solution.py:495
  156.8 3.7 %collective-permute-start.17 = (f32[128,768]{1,0:T(8,128)}, f32[128,768]{1,0:T(8,128)S(1)}, u32[]{:S(2)}, u32[]{:S(2)}) collective-permute-start(f32[128,768]{1,0:T(8,128)} %copy-done.5), channel_id=1, source_target_pairs={{0,16},{16,32},{32,48},{48,64},{64,80},{80,96},{96,112},{112,128},... | collective-permute-start | bytes 1179656 | tf_op jit(solution)/shard_map/ppermute | solution.py:484
  160.5 31.6 %collective-permute-done.17.halves_0 = f32[128,768]{1,0:T(8,128)S(1)} collective-permute-done((f32[128,768]{1,0:T(8,128)}, f32[128,768]{1,0:T(8,128)S(1)}, u32[]{:S(2)}, u32[]{:S(2)}) %collective-permute-start.17) | collective-permute-done | bytes 393248 | tf_op jit(solution)/shard_map/ppermute | solution.py:484
  195.9 3.5 %finish.1 = f32[288,2,8,128]{3,2,1,0:T(8,128)} custom-call(s32[4]{0:T(128)S(1)} %pad_add_fusion.place, f32[288,2,8,128]{3,2,1,0:T(8,128)S(1)} %bitcast.16, f32[128,2304]{1,0:T(8,128)S(1)} %bitcast.17, f32[128,768]{1,0:T(8,128)S(1)} %copy-done.8, f32[128,768]{1,0:T(8,128)S(1)} %copy-done.4, f32[128,768]{1,0:T(8,128)S(1)} %copy-done.6), custom_call_target="tpu_custom_call" | custom-call | tf_op jit(solution)/shard_map/finish/pallas_call | solution.py:428
  (35 shorter events, 16.4 us)
Async XLA Ops:
  0.0 1.7 copy-start
  1.7 23.8 %copy-start.1 = (f32[1,3,3,16,16,256]{5,4,3,2,1,0:T(8,128)S(1)}, f32[1,3,3,16,16,256]{5,4,3,2,1,0:T(8,128)}, u32[]{:S(2)}) copy-start(f32[1,3,3,16,16,256]{5,4,3,2,1,0:T(8,128)} %param.1) | copy-start | bytes 7077892
  4.4 21.0 %collective-permute-start = (f32[9,3,16,256]{3,2,1,0:T(8,128)}, f32[9,3,16,256]{3,2,1,0:T(8,128)S(1)}, u32[]{:S(2)}, u32[]{:S(2)}) collective-permute-start(f32[9,3,16,256]{3,2,1,0:T(8,128)} %get-tuple-element.16), channel_id=1, source_target_pairs={{0,4},{4,8},{8,12},{1,5},{5,9},{9,13},{2,6},{6,10},{10,14},{3,7},{... | collective-permute-start | bytes 1327112 | tf_op jit(solution)/shard_map/ppermute | solution.py:455
  6.1 19.3 %collective-permute-start.1 = (f32[9,3,16,256]{3,2,1,0:T(8,128)}, f32[9,3,16,256]{3,2,1,0:T(8,128)S(1)}, u32[]{:S(2)}, u32[]{:S(2)}) collective-permute-start(f32[9,3,16,256]{3,2,1,0:T(8,128)} %get-tuple-element.17), channel_id=1, source_target_pairs={{4,0},{8,4},{12,8},{5,1},{9,5},{13,9},{6,2},{10,6},{14,10},{7,3},{... | collective-permute-start | bytes 1327112 | tf_op jit(solution)/shard_map/ppermute | solution.py:455
  7.4 6.2 %collective-permute-start.2 = (f32[9,16,128]{2,1,0:T(8,128)S(1)}, f32[9,16,128]{2,1,0:T(8,128)S(1)}, u32[]{:S(2)}, u32[]{:S(2)}) collective-permute-start(f32[9,16,128]{2,1,0:T(8,128)S(1)} %get-tuple-element.18), channel_id=1, source_target_pairs={{0,1},{1,2},{2,3},{4,5},{5,6},{6,7},{8,9},{9,10},{10,11},{12,13},{... | collective-permute-start | bytes 221192 | tf_op jit(solution)/shard_map/ppermute | solution.py:455
  10.9 6.4 %collective-permute-start.3 = (f32[9,16,128]{2,1,0:T(8,128)S(1)}, f32[9,16,128]{2,1,0:T(8,128)S(1)}, u32[]{:S(2)}, u32[]{:S(2)}) collective-permute-start(f32[9,16,128]{2,1,0:T(8,128)S(1)} %get-tuple-element.19), channel_id=1, source_target_pairs={{1,0},{2,1},{3,2},{5,4},{6,5},{7,6},{9,8},{10,9},{11,10},{13,12},{... | collective-permute-start | bytes 221192 | tf_op jit(solution)/shard_map/ppermute | solution.py:455
  17.3 3.8 %collective-permute-start.4 = (f32[9,16,128]{2,1,0:T(8,128)S(1)}, f32[9,16,128]{2,1,0:T(8,128)S(1)}, u32[]{:S(2)}, u32[]{:S(2)}) collective-permute-start(f32[9,16,128]{2,1,0:T(8,128)S(1)} %get-tuple-element.20), channel_id=1, source_target_pairs={{0,4},{4,8},{8,12},{1,5},{5,9},{9,13},{2,6},{6,10},{10,14},{3,7},{... | collective-permute-start | bytes 221192 | tf_op jit(solution)/shard_map/ppermute | solution.py:455
  19.7 5.7 %collective-permute-start.5 = (f32[9,16,128]{2,1,0:T(8,128)S(1)}, f32[9,16,128]{2,1,0:T(8,128)S(1)}, u32[]{:S(2)}, u32[]{:S(2)}) collective-permute-start(f32[9,16,128]{2,1,0:T(8,128)S(1)} %get-tuple-element.21), channel_id=1, source_target_pairs={{4,0},{8,4},{12,8},{5,1},{9,5},{13,9},{6,2},{10,6},{14,10},{7,3},{... | collective-permute-start | bytes 221192 | tf_op jit(solution)/shard_map/ppermute | solution.py:455
  42.5 64.3 %copy-start.3 = (f32[128,768]{1,0:T(8,128)}, f32[128,768]{1,0:T(8,128)S(1)}, u32[]{:S(2)}) copy-start(f32[128,768]{1,0:T(8,128)S(1)} %get-tuple-element.26.halves_1) | copy-start | bytes 1179652
  42.5 64.3 %copy-start.5 = (f32[128,768]{1,0:T(8,128)}, f32[128,768]{1,0:T(8,128)S(1)}, u32[]{:S(2)}) copy-start(f32[128,768]{1,0:T(8,128)S(1)} %get-tuple-element.25.halves_2) | copy-start | bytes 1179652
  63.2 16.1 %collective-permute-start.6 = (f32[8,8,1536]{2,1,0:T(8,128)S(1)}, f32[8,8,1536]{2,1,0:T(8,128)S(1)}, u32[]{:S(2)}, u32[]{:S(2)}) collective-permute-start(f32[8,8,1536]{2,1,0:T(8,128)S(1)} %get-tuple-element.23), channel_id=1, source_target_pairs={{0,4},{4,8},{8,12},{12,16},{16,20},{20,24},{24,28},{28,32},{32,36}... | collective-permute-start | bytes 1179656 | tf_op jit(solution)/shard_map/ppermute | solution.py:466
  65.1 14.1 %collective-permute-start.7 = (f32[8,8,1536]{2,1,0:T(8,128)S(1)}, f32[8,8,1536]{2,1,0:T(8,128)S(1)}, u32[]{:S(2)}, u32[]{:S(2)}) collective-permute-start(f32[8,8,1536]{2,1,0:T(8,128)S(1)} %get-tuple-element.24), channel_id=1, source_target_pairs={{4,0},{8,4},{12,8},{16,12},{20,16},{24,20},{28,24},{32,28},{36,32}... | collective-permute-start | bytes 1179656 | tf_op jit(solution)/shard_map/ppermute | solution.py:466
  82.4 8.6 %collective-permute-start.8 = (f32[3,8,8,128]{3,2,1,0:T(8,128)S(1)}, f32[3,8,8,128]{3,2,1,0:T(8,128)S(1)}, u32[]{:S(2)}, u32[]{:S(2)}) collective-permute-start(f32[3,8,8,128]{3,2,1,0:T(8,128)S(1)} %stage.4), channel_id=1, source_target_pairs={{0,64},{64,128},{128,192},{1,65},{65,129},{129,193},{2,66},{66,130... | collective-permute-start | bytes 294920 | tf_op jit(solution)/shard_map/ppermute | solution.py:455
  91.0 6.7 %collective-permute-start.10 = (f32[3,8,8,128]{3,2,1,0:T(8,128)S(1)}, f32[3,8,8,128]{3,2,1,0:T(8,128)S(1)}, u32[]{:S(2)}, u32[]{:S(2)}) collective-permute-start(f32[3,8,8,128]{3,2,1,0:T(8,128)S(1)} %collective-permute-done.8.rest_0_), channel_id=1, source_target_pairs={{4,0},{8,4},{12,8},{16,12},{20,16},{24,20},{28,24},{32,28},{36,32}... | collective-permute-start | bytes 294920 | tf_op jit(solution)/shard_map/ppermute | solution.py:466
  94.6 8.9 %collective-permute-start.9 = (f32[3,8,8,128]{3,2,1,0:T(8,128)S(1)}, f32[3,8,8,128]{3,2,1,0:T(8,128)S(1)}, u32[]{:S(2)}, u32[]{:S(2)}) collective-permute-start(f32[3,8,8,128]{3,2,1,0:T(8,128)S(1)} %collective-permute-done.8.rest_0_), channel_id=1, source_target_pairs={{0,4},{4,8},{8,12},{12,16},{16,20},{20,24},{24,28},{28,32},{32,36}... | collective-permute-start | bytes 294920 | tf_op jit(solution)/shard_map/ppermute | solution.py:466
  106.7 8.6 %collective-permute-start.11 = (f32[3,8,8,128]{3,2,1,0:T(8,128)S(1)}, f32[3,8,8,128]{3,2,1,0:T(8,128)S(1)}, u32[]{:S(2)}, u32[]{:S(2)}) collective-permute-start(f32[3,8,8,128]{3,2,1,0:T(8,128)S(1)} %stage.5), channel_id=1, source_target_pairs={{0,64},{64,128},{128,192},{1,65},{65,129},{129,193},{2,66},{66,130... | collective-permute-start | bytes 294920 | tf_op jit(solution)/shard_map/ppermute | solution.py:455
  115.4 4.3 %collective-permute-start.13 = (f32[3,8,8,128]{3,2,1,0:T(8,128)S(1)}, f32[3,8,8,128]{3,2,1,0:T(8,128)S(1)}, u32[]{:S(2)}, u32[]{:S(2)}) collective-permute-start(f32[3,8,8,128]{3,2,1,0:T(8,128)S(1)} %collective-permute-done.11.rest_0_), channel_id=1, source_target_pairs={{4,0},{8,4},{12,8},{16,12},{20,16},{24,20},{28,24},{32,28},{36,32}... | collective-permute-start | bytes 294920 | tf_op jit(solution)/shard_map/ppermute | solution.py:466
  117.3 8.9 %collective-permute-start.12 = (f32[3,8,8,128]{3,2,1,0:T(8,128)S(1)}, f32[3,8,8,128]{3,2,1,0:T(8,128)S(1)}, u32[]{:S(2)}, u32[]{:S(2)}) collective-permute-start(f32[3,8,8,128]{3,2,1,0:T(8,128)S(1)} %collective-permute-done.11.rest_0_), channel_id=1, source_target_pairs={{0,4},{4,8},{8,12},{12,16},{16,20},{20,24},{24,28},{28,32},{32,36}... | collective-permute-start | bytes 294920 | tf_op jit(solution)/shard_map/ppermute | solution.py:466
  129.4 8.6 %collective-permute-start.14 = (f32[3,8,8,128]{3,2,1,0:T(8,128)S(1)}, f32[3,8,8,128]{3,2,1,0:T(8,128)S(1)}, u32[]{:S(2)}, u32[]{:S(2)}) collective-permute-start(f32[3,8,8,128]{3,2,1,0:T(8,128)S(1)} %stage.6), channel_id=1, source_target_pairs={{0,64},{64,128},{128,192},{1,65},{65,129},{129,193},{2,66},{66,130... | collective-permute-start | bytes 294920 | tf_op jit(solution)/shard_map/ppermute | solution.py:455
  138.0 4.3 %collective-permute-start.16 = (f32[3,8,8,128]{3,2,1,0:T(8,128)S(1)}, f32[3,8,8,128]{3,2,1,0:T(8,128)S(1)}, u32[]{:S(2)}, u32[]{:S(2)}) collective-permute-start(f32[3,8,8,128]{3,2,1,0:T(8,128)S(1)} %collective-permute-done.14.rest_0_), channel_id=1, source_target_pairs={{4,0},{8,4},{12,8},{16,12},{20,16},{24,20},{28,24},{32,28},{36,32}... | collective-permute-start | bytes 294920 | tf_op jit(solution)/shard_map/ppermute | solution.py:466
  139.9 8.9 %collective-permute-start.15 = (f32[3,8,8,128]{3,2,1,0:T(8,128)S(1)}, f32[3,8,8,128]{3,2,1,0:T(8,128)S(1)}, u32[]{:S(2)}, u32[]{:S(2)}) collective-permute-start(f32[3,8,8,128]{3,2,1,0:T(8,128)S(1)} %collective-permute-done.14.rest_0_), channel_id=1, source_target_pairs={{0,4},{4,8},{8,12},{12,16},{16,20},{20,24},{24,28},{28,32},{32,36}... | collective-permute-start | bytes 294920 | tf_op jit(solution)/shard_map/ppermute | solution.py:466
  152.0 1.0 copy-start.2
  153.1 39.9 %all-to-all-start.1 = ((f32[16,8,2304]{2,1,0:T(8,128)}), f32[16,8,2304]{2,1,0:T(8,128)S(1)}, u32[]{:S(2)}, u32[]{:S(2)}) async-start(f32[16,8,2304]{2,1,0:T(8,128)} %copy-done.2), calls=%async_computation.1 | async-start | bytes 2359296 | tf_op jit(solution)/shard_map/all_to_all | solution.py:495
  156.8 35.4 %collective-permute-start.17 = (f32[128,768]{1,0:T(8,128)}, f32[128,768]{1,0:T(8,128)S(1)}, u32[]{:S(2)}, u32[]{:S(2)}) collective-permute-start(f32[128,768]{1,0:T(8,128)} %copy-done.5), channel_id=1, source_target_pairs={{0,16},{16,32},{32,48},{48,64},{64,80},{80,96},{96,112},{112,128},... | collective-permute-start | bytes 1179656 | tf_op jit(solution)/shard_map/ppermute | solution.py:484
  192.1 0.8 copy-start.7
  192.9 1.0 copy-start.4
  193.9 1.0 copy-start.6
  194.9 1.0 copy-start.8

commit v4 on v3

--- a/solution.py
+++ b/solution.py
@@ -19,6 +19,14 @@
 group_axes = ("ty", "gx")
 
 
+def snake(piece):
+    return piece if piece // 4 % 2 == 0 else piece // 4 * 4 + 3 - piece % 4
+
+
+def device_of(piece, gy):
+    return jnp.where(gy % 2 == 0, snake(piece), snake(15 - piece))
+
+
 def near(*arrays):
     return tuple(pltpu.with_memory_space_constraint(a, pltpu.VMEM) for a in arrays)
 
@@ -32,62 +40,67 @@
     return jnp.concatenate([u[pl.ds(at + 32 * odd, 8, stride=64), :] for odd in (0, 1)], axis=0)
 
 
-def edges_body(u, low_rows, high_rows, low_columns, high_columns):
-    slot = lanes((16, 128)) // 8
-    k = pl.program_id(0)
-    left = jnp.zeros((16, 128), f32)
-    right = jnp.zeros((16, 128), f32)
-    for x in range(16):
-        a = strided(u, 0, x, 0)
-        b = strided(u, 0, x, 1)
-        if x < 3:
-            low_rows[k, x, :, 0:128] = a
-            low_rows[k, x, :, 128:256] = b
-        if x > 12:
-            high_rows[k, x - 13, :, 0:128] = a
-            high_rows[k, x - 13, :, 128:256] = b
-        turned_a = pltpu.roll(a, 8 * x, 1) if x else a
-        turned_b = pltpu.roll(b, (8 * x + 8) % 128, 1) if x < 15 else b
-        left = jnp.where(slot == x, turned_a, left)
-        right = jnp.where(slot == x, turned_b, right)
-    low_columns[k] = left
-    high_columns[k] = right
+def edges_body(u, field, low_rows, high_rows, held, arrived):
+    copies = [pltpu.make_async_copy(u.at[pl.ds(512 * k, 512)], held.at[pl.ds(512 * k, 512)], arrived.at[k]) for k in range(9)]
+    for copy in copies:
+        copy.start()
+    for k in range(9):
+        copies[k].wait()
+        for x in range(16):
+            for half in range(2):
+                at = pl.ds(half * 128, 128)
+                row = strided(held, k, x, half)
+                field[k, x, :, at] = row
+                if x < 3:
+                    low_rows[k, x, :, at] = row
+                if x > 12:
+                    high_rows[k, x - 13, :, at] = row
 
 
 def edges(u):
     vmem = pl.BlockSpec(memory_space=pltpu.VMEM)
     rows = pltpu.VMEM((9, 3, 16, 256), f32)
-    columns = pltpu.VMEM((9, 16, 128), f32)
     return pl.pallas_call(
         edges_body,
-        grid=(9,),
-        in_specs=[pl.BlockSpec((512, 128), lambda k: (k, 0))],
-        out_specs=[vmem] * 4,
-        out_shape=(rows, rows, columns, columns),
-        compiler_params=pltpu.CompilerParams(vmem_limit_bytes=8 * 2**20),
+        in_specs=[pl.BlockSpec(memory_space=pltpu.HBM)],
+        out_specs=[vmem] * 3,
+        out_shape=(pltpu.VMEM((9, 16, 16, 256), f32), rows, rows),
+        scratch_shapes=[pltpu.VMEM((4608, 128), f32), pltpu.SemaphoreType.DMA((9,))],
+        compiler_params=pltpu.CompilerParams(vmem_limit_bytes=12 * 2**20),
         name="edges",
-    )(u)
-
-
-def corners_body(south, north, up, down):
-    lane = lanes((16, 128))
-    for k in range(9):
-        turned = pltpu.roll(north[k], 64, 1)
-        up[k] = jnp.where(lane >= 64, south[k], turned)
-        down[k] = jnp.where(lane < 64, south[k], turned)
-
-
-def corners(south, north):
+    )(pltpu.with_memory_space_constraint(u, pltpu.HBM))
+
+
+def columns_body(field, before, after, low_columns, high_columns):
+    slot = lanes((16, 128)) // 4
+
+    def each(k, carry):
+        left = jnp.zeros((16, 128), f32)
+        right = jnp.zeros((16, 128), f32)
+        for e in range(22):
+            ref, x = (before, e) if e < 3 else (field, e - 3) if e < 19 else (after, e - 19)
+            a = ref[k, x, :, 0:128]
+            b = ref[k, x, :, 128:256]
+            left = jnp.where(slot == e, pltpu.roll(a, 4 * e, 1) if e else a, left)
+            right = jnp.where(slot == e, pltpu.roll(b, 4 * e + 4, 1), right)
+        low_columns[k] = left
+        high_columns[k] = right
+        return carry
+
+    lax.fori_loop(0, 9, each, 0)
+
+
+def columns(field, before, after):
     vmem = pl.BlockSpec(memory_space=pltpu.VMEM)
     shape = pltpu.VMEM((9, 16, 128), f32)
     return pl.pallas_call(
-        corners_body,
-        in_specs=[vmem] * 2,
+        columns_body,
+        in_specs=[vmem] * 3,
         out_specs=[vmem] * 2,
         out_shape=(shape, shape),
         compiler_params=pltpu.CompilerParams(vmem_limit_bytes=8 * 2**20),
-        name="corners",
-    )(*near(south, north))
+        name="columns",
+    )(*near(field, before, after))
 
 
 def tendency(below, row, above, reach, spacing):
@@ -107,14 +120,17 @@
             + row[1] * ((north - south) * (1.0 / spacing))
             + row[2] * (up - down)
         )
-        out.append(viscosity * laplace - 0.5 * transport)
+        out.append((2.0 * viscosity) * laplace - transport)
     return out
 
 
-def fine_body(place, u, before, after, south, north, corner_before, corner_after,
+def fine_body(place, field, before, after, south, north,
               sources, halves_1, halves_2, ue, v1, v2, rest, f0, h1, pair_u, pair_v, native_0, native_1, turned):
     gx = place[0]
     gy = place[1]
+    quarter = 0.5 * slice_step
+    one_0, one_1, one_2 = (quarter * w for w in first_row)
+    two_0, two_1, two_2 = (quarter * w for w in second_row)
     leader = place[2] == 0
     lane = lanes((16, 128))
     wide = lanes((16, 384))
@@ -126,25 +142,13 @@
     columns_ok = jnp.where(wide < 256, 1.0, jnp.where(wide < 320, north_ok, south_ok))
 
     def gather(k, carry):
+        a = north[k]
+        b = south[k]
         for e in range(22):
-            x = e - 3
-            if x < 0:
-                ue[k, e, :, 0:256] = before[k, e]
-                a, b, slot_a, slot_b = corner_before, corner_before, 8 + x, 16 + x
-            elif x < 16:
-                ue[k, e, :, 0:128] = strided(u, k, x, 0)
-                ue[k, e, :, 128:256] = strided(u, k, x, 1)
-                a, b, slot_a, slot_b = north, south, x, x
-            else:
-                ue[k, e, :, 0:256] = after[k, x - 16]
-                a, b, slot_a, slot_b = corner_after, corner_after, x - 8, x - 16
-            a = a[k]
-            b = b[k]
-            if slot_a > 0:
-                a = pltpu.roll(a, 128 - 8 * slot_a, 1)
-            if slot_b < 15:
-                b = pltpu.roll(b, 120 - 8 * slot_b, 1)
-            ue[k, e, :, 256:384] = jnp.where(lane < 64, a, b)
+            ref, x = (before, e) if e < 3 else (field, e - 3) if e < 19 else (after, e - 19)
+            ue[k, e, :, 0:256] = ref[k, x]
+            right = pltpu.roll(a, 128 - 4 * e, 1) if e else a
+            ue[k, e, :, 256:384] = jnp.where(lane < 64, right, pltpu.roll(b, 124 - 4 * e, 1))
         return carry
 
     lax.fori_loop(0, 9, gather, 0)
@@ -164,13 +168,9 @@
         for c in range(3):
             a, b, d = flux[0][c], flux[1][c], flux[2][c]
             start = ue[c, e]
-            new = start + slice_step * (first_row[0] * a + first_row[1] * b + first_row[2] * d)
-            new = new * ok
+            new = (start + (one_0 * a + one_1 * b + one_2 * d)) * ok
             v1[c, e] = new
-            rest[c, e] = (
-                slice_step * (second_row[0] * a + second_row[1] * b + second_row[2] * d)
-                - half_step * b
-            )
+            rest[c, e] = two_0 * a + (two_1 - 0.5 * half_step) * b + two_2 * d
             f0[c, e] = a
             pair_u[c, e] = paired(start)
             pair_v[c, e] = paired(new)
@@ -183,7 +183,7 @@
         slope = tendency(*rows, 1, 1.0)
         ok = columns_ok * row_ok(e)
         for c in range(3):
-            v2[c, e] = (rows[1][c] + half_step * slope[c] + rest[c, e]) * ok
+            v2[c, e] = (rows[1][c] + (0.5 * half_step) * slope[c] + rest[c, e]) * ok
             h1[c, e] = slope[c]
         return carry
 
@@ -202,10 +202,10 @@
         base_v = tendency(*[[pair_v[c, e + d] for c in range(3)] for d in (-1, 0, 1)], 2, 2.0)
         for c in range(3):
             a, b, d = f0[c, e], h1[c, e], slope[c]
-            one = slice_step * (first_row[0] * a + first_row[1] * b + first_row[2] * d)
-            two = slice_step * (second_row[0] * a + second_row[1] * b + second_row[2] * d)
-            one = one + jnp.where(leader, ue[c, e], -half_step * base_u[c])
-            two = two - half_step * base_v[c]
+            one = one_0 * a + one_1 * b + one_2 * d
+            two = two_0 * a + two_1 * b + two_2 * d
+            one = one + jnp.where(leader, ue[c, e], (-0.5 * half_step) * base_u[c])
+            two = two - (0.5 * half_step) * base_v[c]
             put(0, c, e - 3, one)
             put(1, c, e - 3, two)
             put(2, c, e - 3, v1[c, e])
@@ -227,7 +227,9 @@
                     tile = pl.ds(pl.multiple_of(c * 256 + odd * 128, 128), 128)
                     if field < 2:
                         tile = pl.ds(pl.multiple_of(field * 768 + c * 256 + odd * 128, 128), 128)
-                        sources[rows, tile] = 0.5 * (one + two)
+                        mean = 0.5 * (one + two)
+                        for i in range(8):
+                            sources[device_of(half * 8 + i, gy), :, tile] = mean[8 * i:8 * i + 8]
                     elif field == 2:
                         halves_1[rows, tile] = 0.5 * (one - two)
                     else:
@@ -237,13 +239,17 @@
     lax.fori_loop(0, 3, compact, 0)
 
 
-def fine_part(place, u, *arrays):
+def fine_part(place, *arrays):
     vmem = pl.BlockSpec(memory_space=pltpu.VMEM)
     field = pltpu.VMEM((3, 22, 16, 384), f32)
     return pl.pallas_call(
         fine_body,
-        out_shape=(pltpu.VMEM((128, 1536), f32), pltpu.VMEM((128, 768), f32), pltpu.VMEM((128, 768), f32)),
-        in_specs=[pl.BlockSpec(memory_space=pltpu.SMEM)] + [vmem] * (1 + len(arrays)),
+        out_shape=(
+            pltpu.VMEM((16, 8, 1536), f32),
+            jax.ShapeDtypeStruct((128, 768), f32),
+            pltpu.VMEM((128, 768), f32),
+        ),
+        in_specs=[pl.BlockSpec(memory_space=pltpu.SMEM)] + [vmem] * len(arrays),
         out_specs=[vmem] * 3,
         scratch_shapes=[pltpu.VMEM((9, 22, 16, 384), f32)]
         + [field] * 7
@@ -251,7 +257,7 @@
         + [pltpu.VMEM((16, 128, 128), f32)],
         compiler_params=pltpu.CompilerParams(vmem_limit_bytes=36 * 2**20),
         name="fine",
-    )(place, u, *near(*arrays))
+    )(place, *near(*arrays))
 
 
 def pack_body(source, to_right, to_left):
@@ -401,38 +407,47 @@
 
 
 def finish_body(place, start, coarse, halves_0, halves_1, halves_2, out, mixed, rows):
-    for field, halves in enumerate((halves_0, halves_1, halves_2)):
-        def each(c, carry):
+    gy = place[1]
+
+    def one_field(field, halves):
+        for c in range(3):
             for half in range(2):
-                part = pl.ds(half * 64, 64)
                 for odd in range(2):
-                    tile = pl.multiple_of(c * 256 + odd * 128, 128)
-                    w = coarse[part, pl.ds(field * 768 + tile, 128)]
-                    e = halves[part, pl.ds(tile, 128)]
-                    at = half * 2 + odd
+                    tile = pl.ds(field * 768 + c * 256 + odd * 128, 128)
+                    w = jnp.concatenate(
+                        [coarse[device_of(half * 8 + i, gy), :, tile] for i in range(8)], axis=0
+                    )
+                    e = halves[pl.ds(half * 64, 64), pl.ds(c * 256 + odd * 128, 128)]
+                    at = (c * 2 + half) * 2 + odd
                     mixed[at, pl.ds(0, 64, stride=2), :] = w + e
                     mixed[at, pl.ds(1, 64, stride=2), :] = w - e
-                    rows[half, pl.ds(odd, 128, stride=2), :] = mixed[at].T
-                out[pl.ds((field * 3 + c) * 32, 32), half] = rows[half].reshape(32, 8, 128)
-            return carry
-
-        lax.fori_loop(0, 3, each, 0)
-
-    @pl.when(place[2] == 0)
+                    rows[c * 2 + half, pl.ds(odd, 128, stride=2), :] = mixed[at].T
+                out[pl.ds(c * 32, 32), half] = rows[c * 2 + half].reshape(32, 8, 128)
+
+    for field, halves in enumerate((halves_0, halves_1, halves_2)):
+        if field:
+            chosen = pl.program_id(0) == field
+        else:
+            chosen = (pl.program_id(0) == 0) & (place[2] > 0)
+        pl.when(chosen)(functools.partial(one_field, field, halves))
+
+    @pl.when((pl.program_id(0) == 0) & (place[2] == 0))
     def _():
-        pltpu.sync_copy(start.at[pl.ds(0, 96)], out.at[pl.ds(0, 96)])
+        pltpu.sync_copy(start.at[pl.ds(0, 96)], out)
 
 
 def finish(place, start, coarse, *halves):
     vmem = pl.BlockSpec(memory_space=pltpu.VMEM)
     return pl.pallas_call(
         finish_body,
+        grid=(3,),
         out_shape=jax.ShapeDtypeStruct((288, 2, 8, 128), f32),
         in_specs=[pl.BlockSpec(memory_space=pltpu.SMEM), pl.BlockSpec(memory_space=pl.ANY)] + [vmem] * 4,
-        scratch_shapes=[pltpu.VMEM((4, 128, 128), f32), pltpu.VMEM((2, 256, 128), f32)],
+        out_specs=pl.BlockSpec((96, 2, 8, 128), lambda f: (f, 0, 0, 0)),
+        scratch_shapes=[pltpu.VMEM((12, 128, 128), f32), pltpu.VMEM((6, 256, 128), f32)],
         compiler_params=pltpu.CompilerParams(vmem_limit_bytes=16 * 2**20),
         name="finish",
-    )(place, start, *near(coarse, *halves))
+    )(place, start, *near(coarse), *halves)
 
 
 def sent(block, axes, sizes, moves):
@@ -461,28 +476,28 @@
     pieces = ("ty", "gx", "gy")
 
     def beside(block, by):
-        name = lambda piece: (piece % 16) * 4 + piece // 16
+        def name(piece):
+            gy, at = divmod(piece, 16)
+            return snake(15 - at if gy % 2 else at) * 4 + gy
+
         pairs = [(name(i), name(i + by)) for i in range(64) if 0 <= i + by < 64]
         return lax.ppermute(block, pieces, pairs)
 
     def per_device(provisional):
         tz, ty, gx, gy = (lax.axis_index(a) for a in sizes)
-        place = jnp.stack([gx, gy, tz * 4 + ty, gy * 16 + ty * 4 + gx]).astype(jnp.int32)
+        piece = ty * 4 + jnp.where(ty % 2 == 0, gx, 3 - gx)
+        piece = gy * 16 + jnp.where(gy % 2 == 0, piece, 15 - piece)
+        place = jnp.stack([gx, gy, tz * 4 + ty, piece]).astype(jnp.int32)
         tiles = provisional.reshape(288, 8, 2, 128).transpose(0, 2, 1, 3)
-        u = tiles.reshape(4608, 128)
-        low_rows, high_rows, low_columns, high_columns = edges(u)
+        field, low_rows, high_rows = edges(tiles.reshape(4608, 128))
         after = sent(low_rows, ("gx",), sizes, {"gx": -1})
         before = sent(high_rows, ("gx",), sizes, {"gx": 1})
+        low_columns, high_columns = columns(field, before, after)
         south = sent(high_columns, ("gy",), sizes, {"gy": 1})
         north = sent(low_columns, ("gy",), sizes, {"gy": -1})
-        up, down = corners(south, north)
-        corner_before = sent(up, ("gx",), sizes, {"gx": 1})
-        corner_after = sent(down, ("gx",), sizes, {"gx": -1})
-        sources, halves_1, halves_2 = fine_part(
-            place, u, before, after, south, north, corner_before, corner_after
-        )
+        sources, halves_1, halves_2 = fine_part(place, field, before, after, south, north)
         halves_0 = lax.ppermute(halves_2, ("tz", "ty"), [(i, i + 1) for i in range(15)])
-        source = lax.all_to_all(sources.reshape(16, 8, 1536), group_axes, 0, 0)
+        source = lax.all_to_all(sources, group_axes, 0, 0)
         to_right, to_left = pack(source)
         source_left = beside(to_right, 1)
         source_right = beside(to_left, -1)
@@ -492,7 +507,9 @@
             if turn < 3:
                 own = sent(own, ("tz",), sizes, {"tz": 1})
                 starts = (own, beside(own, 1), beside(own, -1))
-        coarse = lax.all_to_all(own, group_axes, 0, 0).reshape(128, 2304)
+            if turn == 2:
+                starts, halves_0 = lax.optimization_barrier((starts, halves_0))
+        coarse = lax.all_to_all(own, group_axes, 0, 0)
         out = finish(place, tiles, coarse, halves_0, halves_1, halves_2)
         return out.transpose(0, 2, 1, 3).reshape(1, 3, 3, 16, 16, 256)
 

time: 201 us -> 173 us (0.86)
  the two profiles are of different devices: /device:TPU:130 before, /device:TPU:1 now
where the time goes in v4:
time: 173 us; the launch traced here: 172 us
  starting transfers between devices  56.6 us (33%)
  blocking collectives  52.5 us (30%)
  Pallas kernels  35.8 us (21%)
  waiting for transfers between devices  26.8 us (15%)
    all_to_all x1, blocking collectives, per_device(): coarse = lax.all_to_all(own, group_axes, 0, 0)  34.2 us
    ppermute x7, starting transfers between devices, sent(): return lax.ppermute(block, axes if len(axes) > 1 else axes[0], pairs)  27.7 us
    ppermute x8, starting transfers between devices, beside(): return lax.ppermute(block, pieces, pairs)  23.3 us
    all_to_all x1, blocking collectives, per_device(): source = lax.all_to_all(sources, group_axes, 0, 0)  18.3 us
    pallas_call x1, Pallas kernels, fine_part(): pl.pallas_call(fine_body, out_shape=(pltpu.VMEM((16, 8, 1536), f32), jax....  15.3 us
    ppermute x7, waiting for transfers between devices, sent(): return lax.ppermute(block, axes if len(axes) > 1 else axes[0], pairs)  14.8 us
    pallas_call x4, Pallas kernels, stage(): pl.pallas_call(functools.partial(stage_body, begins=not starts, ends=ends...  12.8 us
    ppermute x8, waiting for transfers between devices, beside(): return lax.ppermute(block, pieces, pairs)  12 us
  transfers between devices with their start and end apart: 16, of which 13 were waited for; matrix products, arithmetic and copies ran while one was open for 0% of the time, Pallas kernels for 2%

profile of v4, /device:TPU:1, one launch (start us, length us, event | category | flops | bytes accessed | tf_op | source)
XLA Modules:
  0.0 172.1 jit_solution(11948669719472187927)
XLA Ops:
  0.0 3.3 %edges.1 = (f32[9,16,16,256]{3,2,1,0:T(8,128)S(1)}, f32[9,3,16,256]{3,2,1,0:T(8,128)}, f32[9,3,16,256]{3,2,1,0:T(8,128)}) custom-call(f32[4608,128]{1,0:T(8,128)} %bitcast.12), custom_call_target="tpu_custom_call" | custom-call | tf_op jit(solution)/shard_map/edges/pallas_call | solution.py:63
  3.4 4.9 %collective-permute-start = (f32[9,3,16,256]{3,2,1,0:T(8,128)}, f32[9,3,16,256]{3,2,1,0:T(8,128)S(1)}, u32[]{:S(2)}, u32[]{:S(2)}) collective-permute-start(f32[9,3,16,256]{3,2,1,0:T(8,128)} %get-tuple-element.20), channel_id=1, source_target_pairs={{0,4},{4,8},{8,12},{1,5},{5,9},{9,13},{2,6},{6,10},{10,14},{3,7},{... | collective-permute-start | bytes 1327112 | tf_op jit(solution)/shard_map/ppermute | solution.py:470
  8.3 1.9 %collective-permute-start.1 = (f32[9,3,16,256]{3,2,1,0:T(8,128)}, f32[9,3,16,256]{3,2,1,0:T(8,128)S(1)}, u32[]{:S(2)}, u32[]{:S(2)}) collective-permute-start(f32[9,3,16,256]{3,2,1,0:T(8,128)} %get-tuple-element.21), channel_id=1, source_target_pairs={{4,0},{8,4},{12,8},{5,1},{9,5},{13,9},{6,2},{10,6},{14,10},{7,3},{... | collective-permute-start | bytes 1327112 | tf_op jit(solution)/shard_map/ppermute | solution.py:470
  10.2 3.6 %collective-permute-done.before = f32[9,3,16,256]{3,2,1,0:T(8,128)S(1)} collective-permute-done((f32[9,3,16,256]{3,2,1,0:T(8,128)}, f32[9,3,16,256]{3,2,1,0:T(8,128)S(1)}, u32[]{:S(2)}, u32[]{:S(2)}) %collective-permute-start) | collective-permute-done | bytes 442400 | tf_op jit(solution)/shard_map/ppermute | solution.py:470
  13.8 4.3 %collective-permute-done.1.after = f32[9,3,16,256]{3,2,1,0:T(8,128)S(1)} collective-permute-done((f32[9,3,16,256]{3,2,1,0:T(8,128)}, f32[9,3,16,256]{3,2,1,0:T(8,128)S(1)}, u32[]{:S(2)}, u32[]{:S(2)}) %collective-permute-start.1) | collective-permute-done | bytes 442400 | tf_op jit(solution)/shard_map/ppermute | solution.py:470
  18.1 1.4 columns.1
  19.6 3.1 %collective-permute-start.2 = (f32[9,16,128]{2,1,0:T(8,128)S(1)}, f32[9,16,128]{2,1,0:T(8,128)S(1)}, u32[]{:S(2)}, u32[]{:S(2)}) collective-permute-start(f32[9,16,128]{2,1,0:T(8,128)S(1)} %get-tuple-element.22), channel_id=1, source_target_pairs={{0,1},{1,2},{2,3},{4,5},{5,6},{6,7},{8,9},{9,10},{10,11},{12,13},{... | collective-permute-start | bytes 221192 | tf_op jit(solution)/shard_map/ppermute | solution.py:470
  24.1 3.7 %collective-permute-done.3.north = f32[9,16,128]{2,1,0:T(8,128)S(1)} collective-permute-done((f32[9,16,128]{2,1,0:T(8,128)S(1)}, f32[9,16,128]{2,1,0:T(8,128)S(1)}, u32[]{:S(2)}, u32[]{:S(2)}) %collective-permute-start.3) | collective-permute-done | bytes 73760 | tf_op jit(solution)/shard_map/ppermute | solution.py:470
  27.8 15.3 %fine.1 = (f32[16,8,1536]{2,1,0:T(8,128)S(1)}, f32[128,768]{1,0:T(8,128)S(1)}, f32[128,768]{1,0:T(8,128)S(1)}) custom-call(s32[4]{0:T(128)S(1)} %pad_add_fusion.place, f32[9,16,16,256]{3,2,1,0:T(8,128)S(1)} %get-tuple-element.19.field, f32[9,3,16,256]{3,2,1,0:T(8,128)S(1)} %collective-permute-done.before, ...), custom_call_target="tpu_custom_call" | custom-call | tf_op jit(solution)/shard_map/fine/pallas_call | solution.py:245
  43.1 18.3 %all_to_all.10.source.rest_0_.rest_3_ = f32[16,8,1536]{2,1,0:T(8,128)S(1)} all-to-all(f32[16,8,1536]{2,1,0:T(8,128)S(1)} %get-tuple-element.24), channel_id=1, replica_groups=mesh['tz'=4,'ty'=4,'gx'=4,'gy'=4] {'ty','gx'}, dimensions={0} | all-to-all | bytes 1572864 | tf_op jit(solution)/shard_map/all_to_all | solution.py:500
  61.5 3.2 %collective-permute-start.4 = (f32[8,8,1536]{2,1,0:T(8,128)S(1)}, f32[8,8,1536]{2,1,0:T(8,128)S(1)}, u32[]{:S(2)}, u32[]{:S(2)}) collective-permute-start(f32[8,8,1536]{2,1,0:T(8,128)S(1)} %get-tuple-element.25), channel_id=1, source_target_pairs={{0,4},{4,8},{8,12},{12,28},{28,24},{24,20},{20,16},{16,32},{32,36}... | collective-permute-start | bytes 1179656 | tf_op jit(solution)/shard_map/ppermute | solution.py:484
  64.7 1.9 %collective-permute-start.5 = (f32[8,8,1536]{2,1,0:T(8,128)S(1)}, f32[8,8,1536]{2,1,0:T(8,128)S(1)}, u32[]{:S(2)}, u32[]{:S(2)}) collective-permute-start(f32[8,8,1536]{2,1,0:T(8,128)S(1)} %get-tuple-element.26), channel_id=1, source_target_pairs={{4,0},{8,4},{12,8},{28,12},{24,28},{20,24},{16,20},{32,16},{36,32}... | collective-permute-start | bytes 1179656 | tf_op jit(solution)/shard_map/ppermute | solution.py:484
  66.7 2.8 %collective-permute-done.4.rest_1_.rest_4_ = f32[8,8,1536]{2,1,0:T(8,128)S(1)} collective-permute-done((f32[8,8,1536]{2,1,0:T(8,128)S(1)}, f32[8,8,1536]{2,1,0:T(8,128)S(1)}, u32[]{:S(2)}, u32[]{:S(2)}) %collective-permute-start.4) | collective-permute-done | bytes 393248 | tf_op jit(solution)/shard_map/ppermute | solution.py:484
  69.4 4.4 %collective-permute-done.5.rest_2_.rest_5_ = f32[8,8,1536]{2,1,0:T(8,128)S(1)} collective-permute-done((f32[8,8,1536]{2,1,0:T(8,128)S(1)}, f32[8,8,1536]{2,1,0:T(8,128)S(1)}, u32[]{:S(2)}, u32[]{:S(2)}) %collective-permute-start.5) | collective-permute-done | bytes 393248 | tf_op jit(solution)/shard_map/ppermute | solution.py:484
  73.8 3.2 %stage.4 = f32[3,8,8,128]{3,2,1,0:T(8,128)S(1)} custom-call(s32[4]{0:T(128)S(1)} %pad_add_fusion.place, f32[16,8,1536]{2,1,0:T(8,128)S(1)} %all_to_all.10.source.rest_0_.rest_3_, f32[8,8,1536]{2,1,0:T(8,128)S(1)} %collective-permute-done.4.rest_1_.rest_4_, f32[8,8,1536]{2,1,0:T(8,128)S(1)} %collective-permute-done.5.rest_2_.rest_5_), custom_call_target="tpu_custom_call" | custom-call | tf_op jit(solution)/shard_map/stage/pallas_call | solution.py:398
  77.0 4.9 %collective-permute-start.6 = (f32[3,8,8,128]{3,2,1,0:T(8,128)S(1)}, f32[3,8,8,128]{3,2,1,0:T(8,128)S(1)}, u32[]{:S(2)}, u32[]{:S(2)}) collective-permute-start(f32[3,8,8,128]{3,2,1,0:T(8,128)S(1)} %stage.4), channel_id=1, source_target_pairs={{0,64},{64,128},{128,192},{1,65},{65,129},{129,193},{2,66},{66,130... | collective-permute-start | bytes 294920 | tf_op jit(solution)/shard_map/ppermute | solution.py:470
  81.9 1.6 collective-permute-done.6.rest_0_
  83.6 1.9 %collective-permute-start.8 = (f32[3,8,8,128]{3,2,1,0:T(8,128)S(1)}, f32[3,8,8,128]{3,2,1,0:T(8,128)S(1)}, u32[]{:S(2)}, u32[]{:S(2)}) collective-permute-start(f32[3,8,8,128]{3,2,1,0:T(8,128)S(1)} %collective-permute-done.6.rest_0_), channel_id=1, source_target_pairs={{4,0},{8,4},{12,8},{28,12},{24,28},{20,24},{16,20},{32,16},{36,32}... | collective-permute-start | bytes 294920 | tf_op jit(solution)/shard_map/ppermute | solution.py:484
  85.5 3.6 %collective-permute-start.7 = (f32[3,8,8,128]{3,2,1,0:T(8,128)S(1)}, f32[3,8,8,128]{3,2,1,0:T(8,128)S(1)}, u32[]{:S(2)}, u32[]{:S(2)}) collective-permute-start(f32[3,8,8,128]{3,2,1,0:T(8,128)S(1)} %collective-permute-done.6.rest_0_), channel_id=1, source_target_pairs={{0,4},{4,8},{8,12},{12,28},{28,24},{24,20},{20,16},{16,32},{32,36}... | collective-permute-start | bytes 294920 | tf_op jit(solution)/shard_map/ppermute | solution.py:484
  90.7 3.2 %stage.5 = f32[3,8,8,128]{3,2,1,0:T(8,128)S(1)} custom-call(s32[4]{0:T(128)S(1)} %pad_add_fusion.place, f32[3,8,8,128]{3,2,1,0:T(8,128)S(1)} %collective-permute-done.6.rest_0_, f32[3,8,8,128]{3,2,1,0:T(8,128)S(1)} %collective-permute-done.7.rest_1_, f32[3,8,8,128]{3,2,1,0:T(8,128)S(1)} %collective-permute-done.8.rest_2_, ...), custom_call_target="tpu_custom_call" | custom-call | tf_op jit(solution)/shard_map/stage/pallas_call | solution.py:398
  94.0 5.2 %collective-permute-start.9 = (f32[3,8,8,128]{3,2,1,0:T(8,128)S(1)}, f32[3,8,8,128]{3,2,1,0:T(8,128)S(1)}, u32[]{:S(2)}, u32[]{:S(2)}) collective-permute-start(f32[3,8,8,128]{3,2,1,0:T(8,128)S(1)} %stage.5), channel_id=1, source_target_pairs={{0,64},{64,128},{128,192},{1,65},{65,129},{129,193},{2,66},{66,130... | collective-permute-start | bytes 294920 | tf_op jit(solution)/shard_map/ppermute | solution.py:470
  99.2 5.5 %collective-permute-start.15 = (f32[128,768]{1,0:T(8,128)S(1)}, f32[128,768]{1,0:T(8,128)S(1)}, u32[]{:S(2)}, u32[]{:S(2)}) collective-permute-start(f32[128,768]{1,0:T(8,128)S(1)} %get-tuple-element.27.halves_2), channel_id=1, source_target_pairs={{0,16},{16,32},{32,48},{48,64},{64,80},{80,96},{96,112},{112,128},... | collective-permute-start | bytes 1179656 | tf_op jit(solution)/shard_map/ppermute | solution.py:499
  104.8 1.9 %collective-permute-start.11 = (f32[3,8,8,128]{3,2,1,0:T(8,128)S(1)}, f32[3,8,8,128]{3,2,1,0:T(8,128)S(1)}, u32[]{:S(2)}, u32[]{:S(2)}) collective-permute-start(f32[3,8,8,128]{3,2,1,0:T(8,128)S(1)} %collective-permute-done.9.rest_0_), channel_id=1, source_target_pairs={{4,0},{8,4},{12,8},{28,12},{24,28},{20,24},{16,20},{32,16},{36,32}... | collective-permute-start | bytes 294920 | tf_op jit(solution)/shard_map/ppermute | solution.py:484
  106.7 3.6 %collective-permute-start.10 = (f32[3,8,8,128]{3,2,1,0:T(8,128)S(1)}, f32[3,8,8,128]{3,2,1,0:T(8,128)S(1)}, u32[]{:S(2)}, u32[]{:S(2)}) collective-permute-start(f32[3,8,8,128]{3,2,1,0:T(8,128)S(1)} %collective-permute-done.9.rest_0_), channel_id=1, source_target_pairs={{0,4},{4,8},{8,12},{12,28},{28,24},{24,20},{20,16},{16,32},{32,36}... | collective-permute-start | bytes 294920 | tf_op jit(solution)/shard_map/ppermute | solution.py:484
  112.0 3.2 %stage.6 = f32[3,8,8,128]{3,2,1,0:T(8,128)S(1)} custom-call(s32[4]{0:T(128)S(1)} %pad_add_fusion.place, f32[3,8,8,128]{3,2,1,0:T(8,128)S(1)} %collective-permute-done.9.rest_0_, f32[3,8,8,128]{3,2,1,0:T(8,128)S(1)} %collective-permute-done.10.rest_1_, f32[3,8,8,128]{3,2,1,0:T(8,128)S(1)} %collective-permute-done.11.rest_2_, ...), custom_call_target="tpu_custom_call" | custom-call | tf_op jit(solution)/shard_map/stage/pallas_call | solution.py:398
  115.2 6.3 %collective-permute-start.12 = (f32[3,8,8,128]{3,2,1,0:T(8,128)S(1)}, f32[3,8,8,128]{3,2,1,0:T(8,128)S(1)}, u32[]{:S(2)}, u32[]{:S(2)}) collective-permute-start(f32[3,8,8,128]{3,2,1,0:T(8,128)S(1)} %stage.6), channel_id=1, source_target_pairs={{0,64},{64,128},{128,192},{1,65},{65,129},{129,193},{2,66},{66,130... | collective-permute-start | bytes 294920 | tf_op jit(solution)/shard_map/ppermute | solution.py:470
  121.5 1.6 collective-permute-done.12.rest_0_
  123.1 1.9 %collective-permute-start.14 = (f32[3,8,8,128]{3,2,1,0:T(8,128)S(1)}, f32[3,8,8,128]{3,2,1,0:T(8,128)S(1)}, u32[]{:S(2)}, u32[]{:S(2)}) collective-permute-start(f32[3,8,8,128]{3,2,1,0:T(8,128)S(1)} %collective-permute-done.12.rest_0_), channel_id=1, source_target_pairs={{4,0},{8,4},{12,8},{28,12},{24,28},{20,24},{16,20},{32,16},{36,32}... | collective-permute-start | bytes 294920 | tf_op jit(solution)/shard_map/ppermute | solution.py:484
  125.0 5.2 %collective-permute-start.13 = (f32[3,8,8,128]{3,2,1,0:T(8,128)S(1)}, f32[3,8,8,128]{3,2,1,0:T(8,128)S(1)}, u32[]{:S(2)}, u32[]{:S(2)}) collective-permute-start(f32[3,8,8,128]{3,2,1,0:T(8,128)S(1)} %collective-permute-done.12.rest_0_), channel_id=1, source_target_pairs={{0,4},{4,8},{8,12},{12,28},{28,24},{24,20},{20,16},{16,32},{32,36}... | collective-permute-start | bytes 294920 | tf_op jit(solution)/shard_map/ppermute | solution.py:484
  131.8 3.2 %stage.7 = f32[16,8,2304]{2,1,0:T(8,128)S(1)} custom-call(s32[4]{0:T(128)S(1)} %pad_add_fusion.place, f32[3,8,8,128]{3,2,1,0:T(8,128)S(1)} %collective-permute-done.12.rest_0_, f32[3,8,8,128]{3,2,1,0:T(8,128)S(1)} %collective-permute-done.13.rest_1_, f32[3,8,8,128]{3,2,1,0:T(8,128)S(1)} %collective-permute-done.14.rest_2_, ...), custom_call_target="tpu_custom_call" | custom-call | tf_op jit(solution)/shard_map/stage/pallas_call | solution.py:398
  135.0 34.2 %all_to_all.11.coarse = f32[16,8,2304]{2,1,0:T(8,128)S(1)} all-to-all(f32[16,8,2304]{2,1,0:T(8,128)S(1)} %stage.7), channel_id=1, replica_groups=mesh['tz'=4,'ty'=4,'gx'=4,'gy'=4] {'ty','gx'}, dimensions={0} | all-to-all | bytes 2359296 | tf_op jit(solution)/shard_map/all_to_all | solution.py:512
  169.3 2.8 %finish.1 = f32[288,2,8,128]{3,2,1,0:T(8,128)} custom-call(s32[4]{0:T(128)S(1)} %pad_add_fusion.place, f32[288,2,8,128]{3,2,1,0:T(8,128)S(1)} %bitcast.13, f32[16,8,2304]{2,1,0:T(8,128)S(1)} %all_to_all.11.coarse, f32[128,768]{1,0:T(8,128)S(1)} %collective-permute-done.15.halves_0, f32[128,768]{1,0:T(8,128)S(1)} %get-tuple-element.32.halves_1, ...), custom_call_target="tpu_custom_call" | custom-call | tf_op jit(solution)/shard_map/finish/pallas_call | solution.py:441
  (14 shorter events, 6.3 us)
Async XLA Ops:
  3.4 10.5 %collective-permute-start = (f32[9,3,16,256]{3,2,1,0:T(8,128)}, f32[9,3,16,256]{3,2,1,0:T(8,128)S(1)}, u32[]{:S(2)}, u32[]{:S(2)}) collective-permute-start(f32[9,3,16,256]{3,2,1,0:T(8,128)} %get-tuple-element.20), channel_id=1, source_target_pairs={{0,4},{4,8},{8,12},{1,5},{5,9},{9,13},{2,6},{6,10},{10,14},{3,7},{... | collective-permute-start | bytes 1327112 | tf_op jit(solution)/shard_map/ppermute | solution.py:470
  8.3 9.8 %collective-permute-start.1 = (f32[9,3,16,256]{3,2,1,0:T(8,128)}, f32[9,3,16,256]{3,2,1,0:T(8,128)S(1)}, u32[]{:S(2)}, u32[]{:S(2)}) collective-permute-start(f32[9,3,16,256]{3,2,1,0:T(8,128)} %get-tuple-element.21), channel_id=1, source_target_pairs={{4,0},{8,4},{12,8},{5,1},{9,5},{13,9},{6,2},{10,6},{14,10},{7,3},{... | collective-permute-start | bytes 1327112 | tf_op jit(solution)/shard_map/ppermute | solution.py:470
  19.6 4.5 %collective-permute-start.2 = (f32[9,16,128]{2,1,0:T(8,128)S(1)}, f32[9,16,128]{2,1,0:T(8,128)S(1)}, u32[]{:S(2)}, u32[]{:S(2)}) collective-permute-start(f32[9,16,128]{2,1,0:T(8,128)S(1)} %get-tuple-element.22), channel_id=1, source_target_pairs={{0,1},{1,2},{2,3},{4,5},{5,6},{6,7},{8,9},{9,10},{10,11},{12,13},{... | collective-permute-start | bytes 221192 | tf_op jit(solution)/shard_map/ppermute | solution.py:470
  22.7 5.1 %collective-permute-start.3 = (f32[9,16,128]{2,1,0:T(8,128)S(1)}, f32[9,16,128]{2,1,0:T(8,128)S(1)}, u32[]{:S(2)}, u32[]{:S(2)}) collective-permute-start(f32[9,16,128]{2,1,0:T(8,128)S(1)} %get-tuple-element.23), channel_id=1, source_target_pairs={{1,0},{2,1},{3,2},{5,4},{6,5},{7,6},{9,8},{10,9},{11,10},{13,12},{... | collective-permute-start | bytes 221192 | tf_op jit(solution)/shard_map/ppermute | solution.py:470
  61.5 7.9 %collective-permute-start.4 = (f32[8,8,1536]{2,1,0:T(8,128)S(1)}, f32[8,8,1536]{2,1,0:T(8,128)S(1)}, u32[]{:S(2)}, u32[]{:S(2)}) collective-permute-start(f32[8,8,1536]{2,1,0:T(8,128)S(1)} %get-tuple-element.25), channel_id=1, source_target_pairs={{0,4},{4,8},{8,12},{12,28},{28,24},{24,20},{20,16},{16,32},{32,36}... | collective-permute-start | bytes 1179656 | tf_op jit(solution)/shard_map/ppermute | solution.py:484
  64.7 9.1 %collective-permute-start.5 = (f32[8,8,1536]{2,1,0:T(8,128)S(1)}, f32[8,8,1536]{2,1,0:T(8,128)S(1)}, u32[]{:S(2)}, u32[]{:S(2)}) collective-permute-start(f32[8,8,1536]{2,1,0:T(8,128)S(1)} %get-tuple-element.26), channel_id=1, source_target_pairs={{4,0},{8,4},{12,8},{28,12},{24,28},{20,24},{16,20},{32,16},{36,32}... | collective-permute-start | bytes 1179656 | tf_op jit(solution)/shard_map/ppermute | solution.py:484
  77.0 6.5 %collective-permute-start.6 = (f32[3,8,8,128]{3,2,1,0:T(8,128)S(1)}, f32[3,8,8,128]{3,2,1,0:T(8,128)S(1)}, u32[]{:S(2)}, u32[]{:S(2)}) collective-permute-start(f32[3,8,8,128]{3,2,1,0:T(8,128)S(1)} %stage.4), channel_id=1, source_target_pairs={{0,64},{64,128},{128,192},{1,65},{65,129},{129,193},{2,66},{66,130... | collective-permute-start | bytes 294920 | tf_op jit(solution)/shard_map/ppermute | solution.py:470
  83.6 5.9 %collective-permute-start.8 = (f32[3,8,8,128]{3,2,1,0:T(8,128)S(1)}, f32[3,8,8,128]{3,2,1,0:T(8,128)S(1)}, u32[]{:S(2)}, u32[]{:S(2)}) collective-permute-start(f32[3,8,8,128]{3,2,1,0:T(8,128)S(1)} %collective-permute-done.6.rest_0_), channel_id=1, source_target_pairs={{4,0},{8,4},{12,8},{28,12},{24,28},{20,24},{16,20},{32,16},{36,32}... | collective-permute-start | bytes 294920 | tf_op jit(solution)/shard_map/ppermute | solution.py:484
  85.5 5.3 %collective-permute-start.7 = (f32[3,8,8,128]{3,2,1,0:T(8,128)S(1)}, f32[3,8,8,128]{3,2,1,0:T(8,128)S(1)}, u32[]{:S(2)}, u32[]{:S(2)}) collective-permute-start(f32[3,8,8,128]{3,2,1,0:T(8,128)S(1)} %collective-permute-done.6.rest_0_), channel_id=1, source_target_pairs={{0,4},{4,8},{8,12},{12,28},{28,24},{24,20},{20,16},{16,32},{32,36}... | collective-permute-start | bytes 294920 | tf_op jit(solution)/shard_map/ppermute | solution.py:484
  94.0 10.8 %collective-permute-start.9 = (f32[3,8,8,128]{3,2,1,0:T(8,128)S(1)}, f32[3,8,8,128]{3,2,1,0:T(8,128)S(1)}, u32[]{:S(2)}, u32[]{:S(2)}) collective-permute-start(f32[3,8,8,128]{3,2,1,0:T(8,128)S(1)} %stage.5), channel_id=1, source_target_pairs={{0,64},{64,128},{128,192},{1,65},{65,129},{129,193},{2,66},{66,130... | collective-permute-start | bytes 294920 | tf_op jit(solution)/shard_map/ppermute | solution.py:470
  99.2 31.0 %collective-permute-start.15 = (f32[128,768]{1,0:T(8,128)S(1)}, f32[128,768]{1,0:T(8,128)S(1)}, u32[]{:S(2)}, u32[]{:S(2)}) collective-permute-start(f32[128,768]{1,0:T(8,128)S(1)} %get-tuple-element.27.halves_2), channel_id=1, source_target_pairs={{0,16},{16,32},{32,48},{48,64},{64,80},{80,96},{96,112},{112,128},... | collective-permute-start | bytes 1179656 | tf_op jit(solution)/shard_map/ppermute | solution.py:499
  104.8 5.9 %collective-permute-start.11 = (f32[3,8,8,128]{3,2,1,0:T(8,128)S(1)}, f32[3,8,8,128]{3,2,1,0:T(8,128)S(1)}, u32[]{:S(2)}, u32[]{:S(2)}) collective-permute-start(f32[3,8,8,128]{3,2,1,0:T(8,128)S(1)} %collective-permute-done.9.rest_0_), channel_id=1, source_target_pairs={{4,0},{8,4},{12,8},{28,12},{24,28},{20,24},{16,20},{32,16},{36,32}... | collective-permute-start | bytes 294920 | tf_op jit(solution)/shard_map/ppermute | solution.py:484
  106.7 5.3 %collective-permute-start.10 = (f32[3,8,8,128]{3,2,1,0:T(8,128)S(1)}, f32[3,8,8,128]{3,2,1,0:T(8,128)S(1)}, u32[]{:S(2)}, u32[]{:S(2)}) collective-permute-start(f32[3,8,8,128]{3,2,1,0:T(8,128)S(1)} %collective-permute-done.9.rest_0_), channel_id=1, source_target_pairs={{0,4},{4,8},{8,12},{12,28},{28,24},{24,20},{20,16},{16,32},{32,36}... | collective-permute-start | bytes 294920 | tf_op jit(solution)/shard_map/ppermute | solution.py:484
  115.2 54.1 %copy-start = (f32[1,3,3,16,16,256]{5,4,3,2,1,0:T(8,128)S(1)}, f32[1,3,3,16,16,256]{5,4,3,2,1,0:T(8,128)}, u32[]{:S(2)}) copy-start(f32[1,3,3,16,16,256]{5,4,3,2,1,0:T(8,128)} %param.1) | copy-start | bytes 7077892
  115.2 7.9 %collective-permute-start.12 = (f32[3,8,8,128]{3,2,1,0:T(8,128)S(1)}, f32[3,8,8,128]{3,2,1,0:T(8,128)S(1)}, u32[]{:S(2)}, u32[]{:S(2)}) collective-permute-start(f32[3,8,8,128]{3,2,1,0:T(8,128)S(1)} %stage.6), channel_id=1, source_target_pairs={{0,64},{64,128},{128,192},{1,65},{65,129},{129,193},{2,66},{66,130... | collective-permute-start | bytes 294920 | tf_op jit(solution)/shard_map/ppermute | solution.py:470
  123.1 7.4 %collective-permute-start.14 = (f32[3,8,8,128]{3,2,1,0:T(8,128)S(1)}, f32[3,8,8,128]{3,2,1,0:T(8,128)S(1)}, u32[]{:S(2)}, u32[]{:S(2)}) collective-permute-start(f32[3,8,8,128]{3,2,1,0:T(8,128)S(1)} %collective-permute-done.12.rest_0_), channel_id=1, source_target_pairs={{4,0},{8,4},{12,8},{28,12},{24,28},{20,24},{16,20},{32,16},{36,32}... | collective-permute-start | bytes 294920 | tf_op jit(solution)/shard_map/ppermute | solution.py:484
  125.0 6.8 %collective-permute-start.13 = (f32[3,8,8,128]{3,2,1,0:T(8,128)S(1)}, f32[3,8,8,128]{3,2,1,0:T(8,128)S(1)}, u32[]{:S(2)}, u32[]{:S(2)}) collective-permute-start(f32[3,8,8,128]{3,2,1,0:T(8,128)S(1)} %collective-permute-done.12.rest_0_), channel_id=1, source_target_pairs={{0,4},{4,8},{8,12},{12,28},{28,24},{24,20},{20,16},{16,32},{32,36}... | collective-permute-start | bytes 294920 | tf_op jit(solution)/shard_map/ppermute | solution.py:484

commit v5 on v4

--- a/solution.py
+++ b/solution.py
@@ -40,21 +40,19 @@
     return jnp.concatenate([u[pl.ds(at + 32 * odd, 8, stride=64), :] for odd in (0, 1)], axis=0)
 
 
-def edges_body(u, field, low_rows, high_rows, held, arrived):
-    copies = [pltpu.make_async_copy(u.at[pl.ds(512 * k, 512)], held.at[pl.ds(512 * k, 512)], arrived.at[k]) for k in range(9)]
+def edges_body(u, held, low_rows, high_rows, arrived):
+    copies = [
+        pltpu.make_async_copy(u.at[pl.ds(512 * k, 512)], held.at[pl.ds(512 * k, 512)], arrived.at[k])
+        for k in range(9)
+    ]
     for copy in copies:
         copy.start()
     for k in range(9):
         copies[k].wait()
-        for x in range(16):
+        for x in (0, 1, 2, 13, 14, 15):
+            to = low_rows.at[k, x] if x < 3 else high_rows.at[k, x - 13]
             for half in range(2):
-                at = pl.ds(half * 128, 128)
-                row = strided(held, k, x, half)
-                field[k, x, :, at] = row
-                if x < 3:
-                    low_rows[k, x, :, at] = row
-                if x > 12:
-                    high_rows[k, x - 13, :, at] = row
+                to[:, half * 128:(half + 1) * 128] = strided(held, k, x, half)
 
 
 def edges(u):
@@ -64,11 +62,33 @@
         edges_body,
         in_specs=[pl.BlockSpec(memory_space=pltpu.HBM)],
         out_specs=[vmem] * 3,
-        out_shape=(pltpu.VMEM((9, 16, 16, 256), f32), rows, rows),
-        scratch_shapes=[pltpu.VMEM((4608, 128), f32), pltpu.SemaphoreType.DMA((9,))],
+        out_shape=(pltpu.VMEM((4608, 128), f32), rows, rows),
+        scratch_shapes=[pltpu.SemaphoreType.DMA((9,))],
         compiler_params=pltpu.CompilerParams(vmem_limit_bytes=12 * 2**20),
         name="edges",
     )(pltpu.with_memory_space_constraint(u, pltpu.HBM))
+
+
+def turned_body(held, field):
+    def each(k, carry):
+        for x in range(16):
+            for half in range(2):
+                field[k, x, :, half * 128:(half + 1) * 128] = strided(held, k, x, half)
+        return carry
+
+    lax.fori_loop(0, 9, each, 0)
+
+
+def turned_field(held):
+    vmem = pl.BlockSpec(memory_space=pltpu.VMEM)
+    return pl.pallas_call(
+        turned_body,
+        in_specs=[vmem],
+        out_specs=vmem,
+        out_shape=pltpu.VMEM((9, 16, 16, 256), f32),
+        compiler_params=pltpu.CompilerParams(vmem_limit_bytes=8 * 2**20),
+        name="turned",
+    )(*near(held))
 
 
 def columns_body(field, before, after, low_columns, high_columns):
@@ -124,14 +144,27 @@
     return out
 
 
+quarter = 0.5 * slice_step
+one_0, one_1, one_2 = (quarter * w for w in first_row)
+two_0, two_1, two_2 = (quarter * w for w in second_row)
+
+
+def put(natives, base, x, value):
+    for odd in (0, 1):
+        at = pl.ds(base + x % 2 * 128 + x // 2 + odd * 8, 8, stride=16)
+        for half, native in enumerate(natives):
+            native[at, :] = value[odd * 8:odd * 8 + 8, half * 128:(half + 1) * 128]
+
+
+def split_pairs(native, start, scratch):
+    scratch[...] = native[pl.ds(start, 128), :].T
+    return scratch[pl.ds(0, 64, stride=2), :], scratch[pl.ds(1, 64, stride=2), :]
+
+
 def fine_body(place, field, before, after, south, north,
-              sources, halves_1, halves_2, ue, v1, v2, rest, f0, h1, pair_u, pair_v, native_0, native_1, turned):
+              halves_2, v1, v2, f0, h1, pair_u, pair_v, ue, rest, native_0, native_1, turned):
     gx = place[0]
     gy = place[1]
-    quarter = 0.5 * slice_step
-    one_0, one_1, one_2 = (quarter * w for w in first_row)
-    two_0, two_1, two_2 = (quarter * w for w in second_row)
-    leader = place[2] == 0
     lane = lanes((16, 128))
     wide = lanes((16, 384))
     even = wide % 2 == 0
@@ -189,74 +222,87 @@
 
     lax.fori_loop(2, 20, second, 0)
 
-    def put(field, c, x, value):
+    def moved(e, carry):
+        for c in range(3):
+            put((native_0, native_1), c * 256, e - 3, v2[c, e])
+        return carry
+
+    lax.fori_loop(3, 19, moved, 0)
+
+    for c in range(3):
         for odd in (0, 1):
-            at = pl.ds((field * 3 + c) * 256 + x % 2 * 128 + x // 2 + odd * 8, 8, stride=16)
-            native_0[at, :] = value[odd * 8:odd * 8 + 8, 0:128]
-            native_1[at, :] = value[odd * 8:odd * 8 + 8, 128:256]
+            for half, native in enumerate((native_0, native_1)):
+                one, two = split_pairs(native, c * 256 + odd * 128, turned.at[(c * 2 + odd) * 2 + half])
+                halves_2[half * 64:half * 64 + 64, c * 256 + odd * 128:c * 256 + odd * 128 + 128] = 0.5 * (one - two)
+
+
+def fine_part(place, *arrays):
+    vmem = pl.BlockSpec(memory_space=pltpu.VMEM)
+    kept = pltpu.VMEM((3, 22, 16, 384), f32)
+    return pl.pallas_call(
+        fine_body,
+        out_shape=[pltpu.VMEM((128, 768), f32)] + [kept] * 6,
+        in_specs=[pl.BlockSpec(memory_space=pltpu.SMEM)] + [vmem] * len(arrays),
+        out_specs=[vmem] * 7,
+        scratch_shapes=[pltpu.VMEM((9, 22, 16, 384), f32), kept]
+        + [pltpu.VMEM((768, 128), f32)] * 2
+        + [pltpu.VMEM((12, 128, 128), f32)],
+        compiler_params=pltpu.CompilerParams(vmem_limit_bytes=36 * 2**20),
+        name="fine",
+    )(place, *near(*arrays))
+
+
+def sources_body(place, field, v1, v2, f0, h1, pair_u, pair_v, sources, halves_1, native_0, native_1, turned):
+    gy = place[1]
+    leader = place[2] == 0
+    natives = (native_0, native_1)
 
     def third(e, carry):
-        rows = [[v2[c, e + d] for c in range(3)] for d in (-1, 0, 1)]
-        slope = tendency(*rows, 1, 1.0)
+        slope = tendency(*[[v2[c, e + d] for c in range(3)] for d in (-1, 0, 1)], 1, 1.0)
         base_u = tendency(*[[pair_u[c, e + d] for c in range(3)] for d in (-1, 0, 1)], 2, 2.0)
         base_v = tendency(*[[pair_v[c, e + d] for c in range(3)] for d in (-1, 0, 1)], 2, 2.0)
         for c in range(3):
-            a, b, d = f0[c, e], h1[c, e], slope[c]
+            a, b, d = f0[c, e, :, 0:256], h1[c, e, :, 0:256], slope[c][:, 0:256]
             one = one_0 * a + one_1 * b + one_2 * d
             two = two_0 * a + two_1 * b + two_2 * d
-            one = one + jnp.where(leader, ue[c, e], (-0.5 * half_step) * base_u[c])
-            two = two - (0.5 * half_step) * base_v[c]
-            put(0, c, e - 3, one)
-            put(1, c, e - 3, two)
-            put(2, c, e - 3, v1[c, e])
-            put(3, c, e - 3, rows[1][c])
+            one = one + jnp.where(leader, field[c, e - 3], (-0.5 * half_step) * base_u[c][:, 0:256])
+            two = two - (0.5 * half_step) * base_v[c][:, 0:256]
+            put(natives, c * 256, e - 3, one)
+            put(natives, (3 + c) * 256, e - 3, two)
+            put(natives, (6 + c) * 256, e - 3, v1[c, e, :, 0:256])
         return carry
 
     lax.fori_loop(3, 19, third, 0)
 
     def compact(c, carry):
-        for field in range(4):
+        for part in range(3):
             for odd in (0, 1):
-                start = pl.multiple_of((field * 3 + c) * 256 + odd * 128, 128)
-                for half, native in enumerate((native_0, native_1)):
-                    at = (field * 2 + odd) * 2 + half
-                    turned[at] = native[pl.ds(start, 128), :].T
-                    one = turned[at, pl.ds(0, 64, stride=2), :]
-                    two = turned[at, pl.ds(1, 64, stride=2), :]
-                    rows = pl.ds(half * 64, 64)
-                    tile = pl.ds(pl.multiple_of(c * 256 + odd * 128, 128), 128)
-                    if field < 2:
-                        tile = pl.ds(pl.multiple_of(field * 768 + c * 256 + odd * 128, 128), 128)
+                start = pl.multiple_of((part * 3 + c) * 256 + odd * 128, 128)
+                for half, native in enumerate(natives):
+                    one, two = split_pairs(native, start, turned.at[(part * 2 + odd) * 2 + half])
+                    tile = pl.multiple_of(c * 256 + odd * 128, 128)
+                    if part == 2:
+                        halves_1[pl.ds(half * 64, 64), pl.ds(tile, 128)] = 0.5 * (one - two)
+                    else:
                         mean = 0.5 * (one + two)
                         for i in range(8):
-                            sources[device_of(half * 8 + i, gy), :, tile] = mean[8 * i:8 * i + 8]
-                    elif field == 2:
-                        halves_1[rows, tile] = 0.5 * (one - two)
-                    else:
-                        halves_2[rows, tile] = 0.5 * (one - two)
+                            to = device_of(half * 8 + i, gy)
+                            sources[to, :, pl.ds(part * 768 + tile, 128)] = mean[8 * i:8 * i + 8]
         return carry
 
     lax.fori_loop(0, 3, compact, 0)
 
 
-def fine_part(place, *arrays):
-    vmem = pl.BlockSpec(memory_space=pltpu.VMEM)
-    field = pltpu.VMEM((3, 22, 16, 384), f32)
-    return pl.pallas_call(
-        fine_body,
-        out_shape=(
-            pltpu.VMEM((16, 8, 1536), f32),
-            jax.ShapeDtypeStruct((128, 768), f32),
-            pltpu.VMEM((128, 768), f32),
-        ),
+def sources_part(place, *arrays):
+    vmem = pl.BlockSpec(memory_space=pltpu.VMEM)
+    return pl.pallas_call(
+        sources_body,
+        out_shape=(pltpu.VMEM((16, 8, 1536), f32), jax.ShapeDtypeStruct((128, 768), f32)),
         in_specs=[pl.BlockSpec(memory_space=pltpu.SMEM)] + [vmem] * len(arrays),
-        out_specs=[vmem] * 3,
-        scratch_shapes=[pltpu.VMEM((9, 22, 16, 384), f32)]
-        + [field] * 7
-        + [pltpu.VMEM((3072, 128), f32)] * 2
-        + [pltpu.VMEM((16, 128, 128), f32)],
-        compiler_params=pltpu.CompilerParams(vmem_limit_bytes=36 * 2**20),
-        name="fine",
+        out_specs=[vmem] * 2,
+        scratch_shapes=[pltpu.VMEM((2304, 128), f32)] * 2 + [pltpu.VMEM((12, 128, 128), f32)],
+        compiler_params=pltpu.CompilerParams(vmem_limit_bytes=16 * 2**20),
+        name="sources",
     )(place, *near(*arrays))
 
 
@@ -489,14 +535,16 @@
         piece = gy * 16 + jnp.where(gy % 2 == 0, piece, 15 - piece)
         place = jnp.stack([gx, gy, tz * 4 + ty, piece]).astype(jnp.int32)
         tiles = provisional.reshape(288, 8, 2, 128).transpose(0, 2, 1, 3)
-        field, low_rows, high_rows = edges(tiles.reshape(4608, 128))
+        held, low_rows, high_rows = edges(tiles.reshape(4608, 128))
         after = sent(low_rows, ("gx",), sizes, {"gx": -1})
         before = sent(high_rows, ("gx",), sizes, {"gx": 1})
+        field = turned_field(held)
         low_columns, high_columns = columns(field, before, after)
         south = sent(high_columns, ("gy",), sizes, {"gy": 1})
         north = sent(low_columns, ("gy",), sizes, {"gy": -1})
-        sources, halves_1, halves_2 = fine_part(place, field, before, after, south, north)
+        halves_2, *kept = fine_part(place, field, before, after, south, north)
         halves_0 = lax.ppermute(halves_2, ("tz", "ty"), [(i, i + 1) for i in range(15)])
+        sources, halves_1 = sources_part(place, field, *kept)
         source = lax.all_to_all(sources, group_axes, 0, 0)
         to_right, to_left = pack(source)
         source_left = beside(to_right, 1)

time: 173 us -> 174 us (level)
  waiting for transfers between devices: 26.8 us -> 23.7 us
  local copies, waits for them, and re-layouts: 0.01 us -> 3.07 us
    ppermute x7, waiting for transfers between devices: 14.8 us -> 11.7 us  [sent(): return lax.ppermute(block, axes if len(axes) > 1 else axes[0], pairs)]
    unnamed x2 -> x6, local copies, waits for them, and re-layouts: 0.01 us -> 3.07 us
    pallas_call x1 -> x3, Pallas kernels: 15.3 us -> 17.7 us  [the longest x1 11.4 us: fine_part(): pl.pallas_call(fine_body, out_shape=[pltpu.VMEM((128, 768), f32)] + [kept...]
  transfers between devices with their start and end apart: 16 -> 16, of which waited for: 13 -> 13; matrix products, arithmetic and copies ran while one was open for 0% -> 0% of each run, Pallas kernels for 2% -> 3%
where the time goes in v5:
time: 174 us
  starting transfers between devices  56.4 us (32%)
  blocking collectives  52.7 us (30%)
  Pallas kernels  37.5 us (22%)
  waiting for transfers between devices  23.7 us (14%)
  local copies, waits for them, and re-layouts  3.07 us (2%)
    all_to_all x1, blocking collectives, per_device(): coarse = lax.all_to_all(own, group_axes, 0, 0)  34.4 us
    ppermute x7, starting transfers between devices, sent(): return lax.ppermute(block, axes if len(axes) > 1 else axes[0], pairs)  27.6 us
    ppermute x8, starting transfers between devices, beside(): return lax.ppermute(block, pieces, pairs)  23.3 us
    all_to_all x1, blocking collectives, per_device(): source = lax.all_to_all(sources, group_axes, 0, 0)  18.3 us
    pallas_call x4, Pallas kernels, stage(): pl.pallas_call(functools.partial(stage_body, begins=not starts, ends=ends...  12.8 us
    ppermute x8, waiting for transfers between devices, beside(): return lax.ppermute(block, pieces, pairs)  12 us
    ppermute x7, waiting for transfers between devices, sent(): return lax.ppermute(block, axes if len(axes) > 1 else axes[0], pairs)  11.7 us
    pallas_call x1, Pallas kernels, fine_part(): pl.pallas_call(fine_body, out_shape=[pltpu.VMEM((128, 768), f32)] + [kept...  11.4 us
  transfers between devices with their start and end apart: 16, of which 13 were waited for; matrix products, arithmetic and copies ran while one was open for 0% of the time, Pallas kernels for 3%

profile of v5, /device:TPU:1, one launch (start us, length us, event | category | flops | bytes accessed | tf_op | source)
XLA Modules:
  0.0 173.7 jit_solution(4806385361631377336)
XLA Ops:
  0.0 2.6 %edges.1 = (f32[4608,128]{1,0:T(8,128)S(1)}, f32[9,3,16,256]{3,2,1,0:T(8,128)}, f32[9,3,16,256]{3,2,1,0:T(8,128)}) custom-call(f32[4608,128]{1,0:T(8,128)} %bitcast.12), custom_call_target="tpu_custom_call" | custom-call | tf_op jit(solution)/shard_map/edges/pallas_call | solution.py:61
  4.1 4.9 %collective-permute-start = (f32[9,3,16,256]{3,2,1,0:T(8,128)}, f32[9,3,16,256]{3,2,1,0:T(8,128)S(1)}, u32[]{:S(2)}, u32[]{:S(2)}) collective-permute-start(f32[9,3,16,256]{3,2,1,0:T(8,128)} %get-tuple-element.26), channel_id=1, source_target_pairs={{0,4},{4,8},{8,12},{1,5},{5,9},{9,13},{2,6},{6,10},{10,14},{3,7},{... | collective-permute-start | bytes 1327112 | tf_op jit(solution)/shard_map/ppermute | solution.py:516
  9.0 1.9 %collective-permute-start.1 = (f32[9,3,16,256]{3,2,1,0:T(8,128)}, f32[9,3,16,256]{3,2,1,0:T(8,128)S(1)}, u32[]{:S(2)}, u32[]{:S(2)}) collective-permute-start(f32[9,3,16,256]{3,2,1,0:T(8,128)} %get-tuple-element.27), channel_id=1, source_target_pairs={{4,0},{8,4},{12,8},{5,1},{9,5},{13,9},{6,2},{10,6},{14,10},{7,3},{... | collective-permute-start | bytes 1327112 | tf_op jit(solution)/shard_map/ppermute | solution.py:516
  10.9 1.7 copy-done.2
  14.5 4.3 %collective-permute-done.1.after = f32[9,3,16,256]{3,2,1,0:T(8,128)S(1)} collective-permute-done((f32[9,3,16,256]{3,2,1,0:T(8,128)}, f32[9,3,16,256]{3,2,1,0:T(8,128)S(1)}, u32[]{:S(2)}, u32[]{:S(2)}) %collective-permute-start.1) | collective-permute-done | bytes 442400 | tf_op jit(solution)/shard_map/ppermute | solution.py:516
  20.2 3.1 %collective-permute-start.2 = (f32[9,16,128]{2,1,0:T(8,128)S(1)}, f32[9,16,128]{2,1,0:T(8,128)S(1)}, u32[]{:S(2)}, u32[]{:S(2)}) collective-permute-start(f32[9,16,128]{2,1,0:T(8,128)S(1)} %get-tuple-element.28), channel_id=1, source_target_pairs={{0,1},{1,2},{2,3},{4,5},{5,6},{6,7},{8,9},{9,10},{10,11},{12,13},{... | collective-permute-start | bytes 221192 | tf_op jit(solution)/shard_map/ppermute | solution.py:516
  24.8 3.7 %collective-permute-done.3.north = f32[9,16,128]{2,1,0:T(8,128)S(1)} collective-permute-done((f32[9,16,128]{2,1,0:T(8,128)S(1)}, f32[9,16,128]{2,1,0:T(8,128)S(1)}, u32[]{:S(2)}, u32[]{:S(2)}) %collective-permute-start.3) | collective-permute-done | bytes 73760 | tf_op jit(solution)/shard_map/ppermute | solution.py:516
  28.5 11.4 %fine.1 = (f32[128,768]{1,0:T(8,128)S(1)}, f32[3,22,16,384]{3,2,1,0:T(8,128)S(1)}, f32[3,22,16,384]{3,2,1,0:T(8,128)S(1)}, f32[3,22,16,384]{3,2,1,0:T(8,128)S(1)...) custom-call(s32[4]{0:T(128)S(1)} %pad_add_fusion.place, ...), custom_call_target="tpu_custom_call" | custom-call | tf_op jit(solution)/shard_map/fine/pallas_call | solution.py:242
  39.9 4.9 %sources.1 = (f32[16,8,1536]{2,1,0:T(8,128)S(1)}, f32[128,768]{1,0:T(8,128)S(1)}) custom-call(s32[4]{0:T(128)S(1)} %pad_add_fusion.place, f32[9,16,16,256]{3,2,1,0:T(8,128)S(1)} %turned.1.field, f32[3,22,16,384]{3,2,1,0:T(8,128)S(1)} %get-tuple-element.30.v1, f32[3,22,16,384]{3,2,1,0:T(8,128)S(1)} %get-tuple-element.31.v2, ...), custom_call_target="tpu_custom_call" | custom-call | tf_op jit(solution)/shard_map/sources/pallas_call | solution.py:298
  44.8 18.3 %all_to_all.10.source.rest_0_.rest_3_ = f32[16,8,1536]{2,1,0:T(8,128)S(1)} all-to-all(f32[16,8,1536]{2,1,0:T(8,128)S(1)} %get-tuple-element.36), channel_id=1, replica_groups=mesh['tz'=4,'ty'=4,'gx'=4,'gy'=4] {'ty','gx'}, dimensions={0} | all-to-all | bytes 1572864 | tf_op jit(solution)/shard_map/all_to_all | solution.py:548
  63.1 3.2 %collective-permute-start.4 = (f32[8,8,1536]{2,1,0:T(8,128)S(1)}, f32[8,8,1536]{2,1,0:T(8,128)S(1)}, u32[]{:S(2)}, u32[]{:S(2)}) collective-permute-start(f32[8,8,1536]{2,1,0:T(8,128)S(1)} %get-tuple-element.37), channel_id=1, source_target_pairs={{0,4},{4,8},{8,12},{12,28},{28,24},{24,20},{20,16},{16,32},{32,36}... | collective-permute-start | bytes 1179656 | tf_op jit(solution)/shard_map/ppermute | solution.py:530
  66.4 1.9 %collective-permute-start.5 = (f32[8,8,1536]{2,1,0:T(8,128)S(1)}, f32[8,8,1536]{2,1,0:T(8,128)S(1)}, u32[]{:S(2)}, u32[]{:S(2)}) collective-permute-start(f32[8,8,1536]{2,1,0:T(8,128)S(1)} %get-tuple-element.38), channel_id=1, source_target_pairs={{4,0},{8,4},{12,8},{28,12},{24,28},{20,24},{16,20},{32,16},{36,32}... | collective-permute-start | bytes 1179656 | tf_op jit(solution)/shard_map/ppermute | solution.py:530
  68.3 2.8 %collective-permute-done.4.rest_1_.rest_4_ = f32[8,8,1536]{2,1,0:T(8,128)S(1)} collective-permute-done((f32[8,8,1536]{2,1,0:T(8,128)S(1)}, f32[8,8,1536]{2,1,0:T(8,128)S(1)}, u32[]{:S(2)}, u32[]{:S(2)}) %collective-permute-start.4) | collective-permute-done | bytes 393248 | tf_op jit(solution)/shard_map/ppermute | solution.py:530
  71.1 4.4 %collective-permute-done.5.rest_2_.rest_5_ = f32[8,8,1536]{2,1,0:T(8,128)S(1)} collective-permute-done((f32[8,8,1536]{2,1,0:T(8,128)S(1)}, f32[8,8,1536]{2,1,0:T(8,128)S(1)}, u32[]{:S(2)}, u32[]{:S(2)}) %collective-permute-start.5) | collective-permute-done | bytes 393248 | tf_op jit(solution)/shard_map/ppermute | solution.py:530
  75.5 3.2 %stage.4 = f32[3,8,8,128]{3,2,1,0:T(8,128)S(1)} custom-call(s32[4]{0:T(128)S(1)} %pad_add_fusion.place, f32[16,8,1536]{2,1,0:T(8,128)S(1)} %all_to_all.10.source.rest_0_.rest_3_, f32[8,8,1536]{2,1,0:T(8,128)S(1)} %collective-permute-done.4.rest_1_.rest_4_, f32[8,8,1536]{2,1,0:T(8,128)S(1)} %collective-permute-done.5.rest_2_.rest_5_), custom_call_target="tpu_custom_call" | custom-call | tf_op jit(solution)/shard_map/stage/pallas_call | solution.py:444
  78.7 4.9 %collective-permute-start.6 = (f32[3,8,8,128]{3,2,1,0:T(8,128)S(1)}, f32[3,8,8,128]{3,2,1,0:T(8,128)S(1)}, u32[]{:S(2)}, u32[]{:S(2)}) collective-permute-start(f32[3,8,8,128]{3,2,1,0:T(8,128)S(1)} %stage.4), channel_id=1, source_target_pairs={{0,64},{64,128},{128,192},{1,65},{65,129},{129,193},{2,66},{66,130... | collective-permute-start | bytes 294920 | tf_op jit(solution)/shard_map/ppermute | solution.py:516
  83.6 1.6 collective-permute-done.6.rest_0_
  85.2 1.9 %collective-permute-start.8 = (f32[3,8,8,128]{3,2,1,0:T(8,128)S(1)}, f32[3,8,8,128]{3,2,1,0:T(8,128)S(1)}, u32[]{:S(2)}, u32[]{:S(2)}) collective-permute-start(f32[3,8,8,128]{3,2,1,0:T(8,128)S(1)} %collective-permute-done.6.rest_0_), channel_id=1, source_target_pairs={{4,0},{8,4},{12,8},{28,12},{24,28},{20,24},{16,20},{32,16},{36,32}... | collective-permute-start | bytes 294920 | tf_op jit(solution)/shard_map/ppermute | solution.py:530
  87.1 3.6 %collective-permute-start.7 = (f32[3,8,8,128]{3,2,1,0:T(8,128)S(1)}, f32[3,8,8,128]{3,2,1,0:T(8,128)S(1)}, u32[]{:S(2)}, u32[]{:S(2)}) collective-permute-start(f32[3,8,8,128]{3,2,1,0:T(8,128)S(1)} %collective-permute-done.6.rest_0_), channel_id=1, source_target_pairs={{0,4},{4,8},{8,12},{12,28},{28,24},{24,20},{20,16},{16,32},{32,36}... | collective-permute-start | bytes 294920 | tf_op jit(solution)/shard_map/ppermute | solution.py:530
  92.4 3.2 %stage.5 = f32[3,8,8,128]{3,2,1,0:T(8,128)S(1)} custom-call(s32[4]{0:T(128)S(1)} %pad_add_fusion.place, f32[3,8,8,128]{3,2,1,0:T(8,128)S(1)} %collective-permute-done.6.rest_0_, f32[3,8,8,128]{3,2,1,0:T(8,128)S(1)} %collective-permute-done.7.rest_1_, f32[3,8,8,128]{3,2,1,0:T(8,128)S(1)} %collective-permute-done.8.rest_2_, ...), custom_call_target="tpu_custom_call" | custom-call | tf_op jit(solution)/shard_map/stage/pallas_call | solution.py:444
  95.6 5.2 %collective-permute-start.9 = (f32[3,8,8,128]{3,2,1,0:T(8,128)S(1)}, f32[3,8,8,128]{3,2,1,0:T(8,128)S(1)}, u32[]{:S(2)}, u32[]{:S(2)}) collective-permute-start(f32[3,8,8,128]{3,2,1,0:T(8,128)S(1)} %stage.5), channel_id=1, source_target_pairs={{0,64},{64,128},{128,192},{1,65},{65,129},{129,193},{2,66},{66,130... | collective-permute-start | bytes 294920 | tf_op jit(solution)/shard_map/ppermute | solution.py:516
  100.9 5.5 %collective-permute-start.15 = (f32[128,768]{1,0:T(8,128)S(1)}, f32[128,768]{1,0:T(8,128)S(1)}, u32[]{:S(2)}, u32[]{:S(2)}) collective-permute-start(f32[128,768]{1,0:T(8,128)S(1)} %get-tuple-element.39.halves_2), channel_id=1, source_target_pairs={{0,16},{16,32},{32,48},{48,64},{64,80},{80,96},{96,112},{112,128},... | collective-permute-start | bytes 1179656 | tf_op jit(solution)/shard_map/ppermute | solution.py:546
  106.4 1.9 %collective-permute-start.11 = (f32[3,8,8,128]{3,2,1,0:T(8,128)S(1)}, f32[3,8,8,128]{3,2,1,0:T(8,128)S(1)}, u32[]{:S(2)}, u32[]{:S(2)}) collective-permute-start(f32[3,8,8,128]{3,2,1,0:T(8,128)S(1)} %collective-permute-done.9.rest_0_), channel_id=1, source_target_pairs={{4,0},{8,4},{12,8},{28,12},{24,28},{20,24},{16,20},{32,16},{36,32}... | collective-permute-start | bytes 294920 | tf_op jit(solution)/shard_map/ppermute | solution.py:530
  108.4 3.6 %collective-permute-start.10 = (f32[3,8,8,128]{3,2,1,0:T(8,128)S(1)}, f32[3,8,8,128]{3,2,1,0:T(8,128)S(1)}, u32[]{:S(2)}, u32[]{:S(2)}) collective-permute-start(f32[3,8,8,128]{3,2,1,0:T(8,128)S(1)} %collective-permute-done.9.rest_0_), channel_id=1, source_target_pairs={{0,4},{4,8},{8,12},{12,28},{28,24},{24,20},{20,16},{16,32},{32,36}... | collective-permute-start | bytes 294920 | tf_op jit(solution)/shard_map/ppermute | solution.py:530
  113.6 3.2 %stage.6 = f32[3,8,8,128]{3,2,1,0:T(8,128)S(1)} custom-call(s32[4]{0:T(128)S(1)} %pad_add_fusion.place, f32[3,8,8,128]{3,2,1,0:T(8,128)S(1)} %collective-permute-done.9.rest_0_, f32[3,8,8,128]{3,2,1,0:T(8,128)S(1)} %collective-permute-done.10.rest_1_, f32[3,8,8,128]{3,2,1,0:T(8,128)S(1)} %collective-permute-done.11.rest_2_, ...), custom_call_target="tpu_custom_call" | custom-call | tf_op jit(solution)/shard_map/stage/pallas_call | solution.py:444
  116.8 6.2 %collective-permute-start.12 = (f32[3,8,8,128]{3,2,1,0:T(8,128)S(1)}, f32[3,8,8,128]{3,2,1,0:T(8,128)S(1)}, u32[]{:S(2)}, u32[]{:S(2)}) collective-permute-start(f32[3,8,8,128]{3,2,1,0:T(8,128)S(1)} %stage.6), channel_id=1, source_target_pairs={{0,64},{64,128},{128,192},{1,65},{65,129},{129,193},{2,66},{66,130... | collective-permute-start | bytes 294920 | tf_op jit(solution)/shard_map/ppermute | solution.py:516
  123.0 1.6 collective-permute-done.12.rest_0_
  124.6 1.9 %collective-permute-start.14 = (f32[3,8,8,128]{3,2,1,0:T(8,128)S(1)}, f32[3,8,8,128]{3,2,1,0:T(8,128)S(1)}, u32[]{:S(2)}, u32[]{:S(2)}) collective-permute-start(f32[3,8,8,128]{3,2,1,0:T(8,128)S(1)} %collective-permute-done.12.rest_0_), channel_id=1, source_target_pairs={{4,0},{8,4},{12,8},{28,12},{24,28},{20,24},{16,20},{32,16},{36,32}... | collective-permute-start | bytes 294920 | tf_op jit(solution)/shard_map/ppermute | solution.py:530
  126.6 5.2 %collective-permute-start.13 = (f32[3,8,8,128]{3,2,1,0:T(8,128)S(1)}, f32[3,8,8,128]{3,2,1,0:T(8,128)S(1)}, u32[]{:S(2)}, u32[]{:S(2)}) collective-permute-start(f32[3,8,8,128]{3,2,1,0:T(8,128)S(1)} %collective-permute-done.12.rest_0_), channel_id=1, source_target_pairs={{0,4},{4,8},{8,12},{12,28},{28,24},{24,20},{20,16},{16,32},{32,36}... | collective-permute-start | bytes 294920 | tf_op jit(solution)/shard_map/ppermute | solution.py:530
  133.3 3.2 %stage.7 = f32[16,8,2304]{2,1,0:T(8,128)S(1)} custom-call(s32[4]{0:T(128)S(1)} %pad_add_fusion.place, f32[3,8,8,128]{3,2,1,0:T(8,128)S(1)} %collective-permute-done.12.rest_0_, f32[3,8,8,128]{3,2,1,0:T(8,128)S(1)} %collective-permute-done.13.rest_1_, f32[3,8,8,128]{3,2,1,0:T(8,128)S(1)} %collective-permute-done.14.rest_2_, ...), custom_call_target="tpu_custom_call" | custom-call | tf_op jit(solution)/shard_map/stage/pallas_call | solution.py:444
  136.6 34.4 %all_to_all.11.coarse = f32[16,8,2304]{2,1,0:T(8,128)S(1)} all-to-all(f32[16,8,2304]{2,1,0:T(8,128)S(1)} %stage.7), channel_id=1, replica_groups=mesh['tz'=4,'ty'=4,'gx'=4,'gy'=4] {'ty','gx'}, dimensions={0} | all-to-all | bytes 2359296 | tf_op jit(solution)/shard_map/all_to_all | solution.py:560
  170.9 2.8 %finish.1 = f32[288,2,8,128]{3,2,1,0:T(8,128)} custom-call(s32[4]{0:T(128)S(1)} %pad_add_fusion.place, f32[288,2,8,128]{3,2,1,0:T(8,128)S(1)} %bitcast.13, f32[16,8,2304]{2,1,0:T(8,128)S(1)} %all_to_all.11.coarse, f32[128,768]{1,0:T(8,128)S(1)} %collective-permute-done.15.halves_0, f32[128,768]{1,0:T(8,128)S(1)} %get-tuple-element.44.halves_1, ...), custom_call_target="tpu_custom_call" | custom-call | tf_op jit(solution)/shard_map/finish/pallas_call | solution.py:487
  (20 shorter events, 11.0 us)
Async XLA Ops:
  2.6 1.4 copy-start.1
  4.1 10.5 %collective-permute-start = (f32[9,3,16,256]{3,2,1,0:T(8,128)}, f32[9,3,16,256]{3,2,1,0:T(8,128)S(1)}, u32[]{:S(2)}, u32[]{:S(2)}) collective-permute-start(f32[9,3,16,256]{3,2,1,0:T(8,128)} %get-tuple-element.26), channel_id=1, source_target_pairs={{0,4},{4,8},{8,12},{1,5},{5,9},{9,13},{2,6},{6,10},{10,14},{3,7},{... | collective-permute-start | bytes 1327112 | tf_op jit(solution)/shard_map/ppermute | solution.py:516
  9.0 9.8 %collective-permute-start.1 = (f32[9,3,16,256]{3,2,1,0:T(8,128)}, f32[9,3,16,256]{3,2,1,0:T(8,128)S(1)}, u32[]{:S(2)}, u32[]{:S(2)}) collective-permute-start(f32[9,3,16,256]{3,2,1,0:T(8,128)} %get-tuple-element.27), channel_id=1, source_target_pairs={{4,0},{8,4},{12,8},{5,1},{9,5},{13,9},{6,2},{10,6},{14,10},{7,3},{... | collective-permute-start | bytes 1327112 | tf_op jit(solution)/shard_map/ppermute | solution.py:516
  10.9 1.7 copy-start.2
  20.2 4.5 %collective-permute-start.2 = (f32[9,16,128]{2,1,0:T(8,128)S(1)}, f32[9,16,128]{2,1,0:T(8,128)S(1)}, u32[]{:S(2)}, u32[]{:S(2)}) collective-permute-start(f32[9,16,128]{2,1,0:T(8,128)S(1)} %get-tuple-element.28), channel_id=1, source_target_pairs={{0,1},{1,2},{2,3},{4,5},{5,6},{6,7},{8,9},{9,10},{10,11},{12,13},{... | collective-permute-start | bytes 221192 | tf_op jit(solution)/shard_map/ppermute | solution.py:516
  23.4 5.1 %collective-permute-start.3 = (f32[9,16,128]{2,1,0:T(8,128)S(1)}, f32[9,16,128]{2,1,0:T(8,128)S(1)}, u32[]{:S(2)}, u32[]{:S(2)}) collective-permute-start(f32[9,16,128]{2,1,0:T(8,128)S(1)} %get-tuple-element.29), channel_id=1, source_target_pairs={{1,0},{2,1},{3,2},{5,4},{6,5},{7,6},{9,8},{10,9},{11,10},{13,12},{... | collective-permute-start | bytes 221192 | tf_op jit(solution)/shard_map/ppermute | solution.py:516
  63.1 7.9 %collective-permute-start.4 = (f32[8,8,1536]{2,1,0:T(8,128)S(1)}, f32[8,8,1536]{2,1,0:T(8,128)S(1)}, u32[]{:S(2)}, u32[]{:S(2)}) collective-permute-start(f32[8,8,1536]{2,1,0:T(8,128)S(1)} %get-tuple-element.37), channel_id=1, source_target_pairs={{0,4},{4,8},{8,12},{12,28},{28,24},{24,20},{20,16},{16,32},{32,36}... | collective-permute-start | bytes 1179656 | tf_op jit(solution)/shard_map/ppermute | solution.py:530
  66.4 9.1 %collective-permute-start.5 = (f32[8,8,1536]{2,1,0:T(8,128)S(1)}, f32[8,8,1536]{2,1,0:T(8,128)S(1)}, u32[]{:S(2)}, u32[]{:S(2)}) collective-permute-start(f32[8,8,1536]{2,1,0:T(8,128)S(1)} %get-tuple-element.38), channel_id=1, source_target_pairs={{4,0},{8,4},{12,8},{28,12},{24,28},{20,24},{16,20},{32,16},{36,32}... | collective-permute-start | bytes 1179656 | tf_op jit(solution)/shard_map/ppermute | solution.py:530
  78.7 6.5 %collective-permute-start.6 = (f32[3,8,8,128]{3,2,1,0:T(8,128)S(1)}, f32[3,8,8,128]{3,2,1,0:T(8,128)S(1)}, u32[]{:S(2)}, u32[]{:S(2)}) collective-permute-start(f32[3,8,8,128]{3,2,1,0:T(8,128)S(1)} %stage.4), channel_id=1, source_target_pairs={{0,64},{64,128},{128,192},{1,65},{65,129},{129,193},{2,66},{66,130... | collective-permute-start | bytes 294920 | tf_op jit(solution)/shard_map/ppermute | solution.py:516
  85.2 5.9 %collective-permute-start.8 = (f32[3,8,8,128]{3,2,1,0:T(8,128)S(1)}, f32[3,8,8,128]{3,2,1,0:T(8,128)S(1)}, u32[]{:S(2)}, u32[]{:S(2)}) collective-permute-start(f32[3,8,8,128]{3,2,1,0:T(8,128)S(1)} %collective-permute-done.6.rest_0_), channel_id=1, source_target_pairs={{4,0},{8,4},{12,8},{28,12},{24,28},{20,24},{16,20},{32,16},{36,32}... | collective-permute-start | bytes 294920 | tf_op jit(solution)/shard_map/ppermute | solution.py:530
  87.1 5.3 %collective-permute-start.7 = (f32[3,8,8,128]{3,2,1,0:T(8,128)S(1)}, f32[3,8,8,128]{3,2,1,0:T(8,128)S(1)}, u32[]{:S(2)}, u32[]{:S(2)}) collective-permute-start(f32[3,8,8,128]{3,2,1,0:T(8,128)S(1)} %collective-permute-done.6.rest_0_), channel_id=1, source_target_pairs={{0,4},{4,8},{8,12},{12,28},{28,24},{24,20},{20,16},{16,32},{32,36}... | collective-permute-start | bytes 294920 | tf_op jit(solution)/shard_map/ppermute | solution.py:530
  95.6 10.8 %collective-permute-start.9 = (f32[3,8,8,128]{3,2,1,0:T(8,128)S(1)}, f32[3,8,8,128]{3,2,1,0:T(8,128)S(1)}, u32[]{:S(2)}, u32[]{:S(2)}) collective-permute-start(f32[3,8,8,128]{3,2,1,0:T(8,128)S(1)} %stage.5), channel_id=1, source_target_pairs={{0,64},{64,128},{128,192},{1,65},{65,129},{129,193},{2,66},{66,130... | collective-permute-start | bytes 294920 | tf_op jit(solution)/shard_map/ppermute | solution.py:516
  100.9 30.9 %collective-permute-start.15 = (f32[128,768]{1,0:T(8,128)S(1)}, f32[128,768]{1,0:T(8,128)S(1)}, u32[]{:S(2)}, u32[]{:S(2)}) collective-permute-start(f32[128,768]{1,0:T(8,128)S(1)} %get-tuple-element.39.halves_2), channel_id=1, source_target_pairs={{0,16},{16,32},{32,48},{48,64},{64,80},{80,96},{96,112},{112,128},... | collective-permute-start | bytes 1179656 | tf_op jit(solution)/shard_map/ppermute | solution.py:546
  106.4 5.9 %collective-permute-start.11 = (f32[3,8,8,128]{3,2,1,0:T(8,128)S(1)}, f32[3,8,8,128]{3,2,1,0:T(8,128)S(1)}, u32[]{:S(2)}, u32[]{:S(2)}) collective-permute-start(f32[3,8,8,128]{3,2,1,0:T(8,128)S(1)} %collective-permute-done.9.rest_0_), channel_id=1, source_target_pairs={{4,0},{8,4},{12,8},{28,12},{24,28},{20,24},{16,20},{32,16},{36,32}... | collective-permute-start | bytes 294920 | tf_op jit(solution)/shard_map/ppermute | solution.py:530
  108.4 5.3 %collective-permute-start.10 = (f32[3,8,8,128]{3,2,1,0:T(8,128)S(1)}, f32[3,8,8,128]{3,2,1,0:T(8,128)S(1)}, u32[]{:S(2)}, u32[]{:S(2)}) collective-permute-start(f32[3,8,8,128]{3,2,1,0:T(8,128)S(1)} %collective-permute-done.9.rest_0_), channel_id=1, source_target_pairs={{0,4},{4,8},{8,12},{12,28},{28,24},{24,20},{20,16},{16,32},{32,36}... | collective-permute-start | bytes 294920 | tf_op jit(solution)/shard_map/ppermute | solution.py:530
  116.8 7.8 %collective-permute-start.12 = (f32[3,8,8,128]{3,2,1,0:T(8,128)S(1)}, f32[3,8,8,128]{3,2,1,0:T(8,128)S(1)}, u32[]{:S(2)}, u32[]{:S(2)}) collective-permute-start(f32[3,8,8,128]{3,2,1,0:T(8,128)S(1)} %stage.6), channel_id=1, source_target_pairs={{0,64},{64,128},{128,192},{1,65},{65,129},{129,193},{2,66},{66,130... | collective-permute-start | bytes 294920 | tf_op jit(solution)/shard_map/ppermute | solution.py:516
  124.6 7.4 %collective-permute-start.14 = (f32[3,8,8,128]{3,2,1,0:T(8,128)S(1)}, f32[3,8,8,128]{3,2,1,0:T(8,128)S(1)}, u32[]{:S(2)}, u32[]{:S(2)}) collective-permute-start(f32[3,8,8,128]{3,2,1,0:T(8,128)S(1)} %collective-permute-done.12.rest_0_), channel_id=1, source_target_pairs={{4,0},{8,4},{12,8},{28,12},{24,28},{20,24},{16,20},{32,16},{36,32}... | collective-permute-start | bytes 294920 | tf_op jit(solution)/shard_map/ppermute | solution.py:530
  126.6 6.8 %collective-permute-start.13 = (f32[3,8,8,128]{3,2,1,0:T(8,128)S(1)}, f32[3,8,8,128]{3,2,1,0:T(8,128)S(1)}, u32[]{:S(2)}, u32[]{:S(2)}) collective-permute-start(f32[3,8,8,128]{3,2,1,0:T(8,128)S(1)} %collective-permute-done.12.rest_0_), channel_id=1, source_target_pairs={{0,4},{4,8},{8,12},{12,28},{28,24},{24,20},{20,16},{16,32},{32,36}... | collective-permute-start | bytes 294920 | tf_op jit(solution)/shard_map/ppermute | solution.py:530
  136.6 34.4 %copy-start = (f32[1,3,3,16,16,256]{5,4,3,2,1,0:T(8,128)S(1)}, f32[1,3,3,16,16,256]{5,4,3,2,1,0:T(8,128)}, u32[]{:S(2)}) copy-start(f32[1,3,3,16,16,256]{5,4,3,2,1,0:T(8,128)} %param.1) | copy-start | bytes 7077892

commit v6 on v5

--- a/solution.py
+++ b/solution.py
@@ -91,20 +91,22 @@
     )(*near(held))
 
 
-def columns_body(field, before, after, low_columns, high_columns):
-    slot = lanes((16, 128)) // 4
+def columns_body(field, before, after, low, high):
+    lane = lanes((16, 128))
 
     def each(k, carry):
-        left = jnp.zeros((16, 128), f32)
-        right = jnp.zeros((16, 128), f32)
-        for e in range(22):
-            ref, x = (before, e) if e < 3 else (field, e - 3) if e < 19 else (after, e - 19)
-            a = ref[k, x, :, 0:128]
-            b = ref[k, x, :, 128:256]
-            left = jnp.where(slot == e, pltpu.roll(a, 4 * e, 1) if e else a, left)
-            right = jnp.where(slot == e, pltpu.roll(b, 4 * e + 4, 1), right)
-        low_columns[k] = left
-        high_columns[k] = right
+        for t in range(3):
+            one = jnp.zeros((16, 128), f32)
+            two = jnp.zeros((16, 128), f32)
+            for e in range(8 * t, min(8 * t + 8, 22)):
+                ref, x = (before, e) if e < 3 else (field, e - 3) if e < 19 else (after, e - 19)
+                at = e % 8 * 16
+                turned_one = pltpu.roll(ref[k, x, :, 0:128], at + 4, 1)
+                turned_two = pltpu.roll(ref[k, x, :, 128:256], (at + 12) % 128, 1)
+                one = jnp.where((lane >= at + 4) & (lane < at + 16), turned_one, one)
+                two = jnp.where((lane >= at) & (lane < at + 12), turned_two, two)
+            low[k, :, t * 128:(t + 1) * 128] = one
+            high[k, :, t * 128:(t + 1) * 128] = two
         return carry
 
     lax.fori_loop(0, 9, each, 0)
@@ -112,7 +114,7 @@
 
 def columns(field, before, after):
     vmem = pl.BlockSpec(memory_space=pltpu.VMEM)
-    shape = pltpu.VMEM((9, 16, 128), f32)
+    shape = pltpu.VMEM((9, 16, 384), f32)
     return pl.pallas_call(
         columns_body,
         in_specs=[vmem] * 3,
@@ -161,27 +163,39 @@
     return scratch[pl.ds(0, 64, stride=2), :], scratch[pl.ds(1, 64, stride=2), :]
 
 
-def fine_body(place, field, before, after, south, north,
-              halves_2, v1, v2, f0, h1, pair_u, pair_v, ue, rest, native_0, native_1, turned):
-    gx = place[0]
-    gy = place[1]
-    lane = lanes((16, 128))
-    wide = lanes((16, 384))
-    even = wide % 2 == 0
-    low_ok = jnp.where(gx > 0, 1.0, 0.0).astype(f32)
-    high_ok = jnp.where(gx < 3, 1.0, 0.0).astype(f32)
-    north_ok = jnp.where(gy < 3, 1.0, 0.0).astype(f32)
-    south_ok = jnp.where(gy > 0, 1.0, 0.0).astype(f32)
-    columns_ok = jnp.where(wide < 256, 1.0, jnp.where(wide < 320, north_ok, south_ok))
+def edge_factor(place, axis, low):
+    return jnp.where(place[axis] > 0 if low else place[axis] < 3, 1.0, 0.0).astype(f32)
+
+
+def paired(field):
+    width = field.shape[-1]
+    even = lanes(field.shape) % 2 == 0
+    return 0.5 * (field + jnp.where(even, pltpu.roll(field, width - 1, 1), pltpu.roll(field, 1, 1)))
+
+
+def swept(rows_of):
+    flux = [tendency(*rows_of(node), 1, 1.0) for node in range(3)]
+    start = rows_of(0)[1]
+    new = [start[c] + (one_0 * flux[0][c] + one_1 * flux[1][c] + one_2 * flux[2][c]) for c in range(3)]
+    rest = [two_0 * flux[0][c] + (two_1 - 0.5 * half_step) * flux[1][c] + two_2 * flux[2][c] for c in range(3)]
+    return new, rest, flux[0]
+
+
+def source_pair(leader, start, a, b, d, base_u, base_v):
+    one = one_0 * a + one_1 * b + one_2 * d
+    two = two_0 * a + two_1 * b + two_2 * d
+    one = one + jnp.where(leader, start, (-0.5 * half_step) * base_u)
+    return one, two - (0.5 * half_step) * base_v
+
+
+def fine_body(place, field, before, after, v1, v2, f0, h1, pair_u, pair_v, ue, rest):
+    low_ok = edge_factor(place, 0, True)
+    high_ok = edge_factor(place, 0, False)
 
     def gather(k, carry):
-        a = north[k]
-        b = south[k]
         for e in range(22):
             ref, x = (before, e) if e < 3 else (field, e - 3) if e < 19 else (after, e - 19)
-            ue[k, e, :, 0:256] = ref[k, x]
-            right = pltpu.roll(a, 128 - 4 * e, 1) if e else a
-            ue[k, e, :, 256:384] = jnp.where(lane < 64, right, pltpu.roll(b, 124 - 4 * e, 1))
+            ue[k, e] = ref[k, x]
         return carry
 
     lax.fori_loop(0, 9, gather, 0)
@@ -189,24 +203,15 @@
     def row_ok(e):
         return jnp.where(e < 3, low_ok, jnp.where(e > 18, high_ok, 1.0))
 
-    def paired(field):
-        return 0.5 * (field + jnp.where(even, pltpu.roll(field, 383, 1), pltpu.roll(field, 1, 1)))
-
     def first(e, carry):
-        flux = []
-        for node in range(3):
-            rows = [[ue[3 * node + c, e + d] for c in range(3)] for d in (-1, 0, 1)]
-            flux.append(tendency(*rows, 1, 1.0))
-        ok = columns_ok * row_ok(e)
+        new, more, flux = swept(lambda node: [[ue[3 * node + c, e + d] for c in range(3)] for d in (-1, 0, 1)])
         for c in range(3):
-            a, b, d = flux[0][c], flux[1][c], flux[2][c]
-            start = ue[c, e]
-            new = (start + (one_0 * a + one_1 * b + one_2 * d)) * ok
-            v1[c, e] = new
-            rest[c, e] = two_0 * a + (two_1 - 0.5 * half_step) * b + two_2 * d
-            f0[c, e] = a
-            pair_u[c, e] = paired(start)
-            pair_v[c, e] = paired(new)
+            value = new[c] * row_ok(e)
+            v1[c, e] = value
+            rest[c, e] = more[c]
+            f0[c, e] = flux[c]
+            pair_u[c, e] = paired(ue[c, e])
+            pair_v[c, e] = paired(value)
         return carry
 
     lax.fori_loop(1, 21, first, 0)
@@ -214,45 +219,114 @@
     def second(e, carry):
         rows = [[v1[c, e + d] for c in range(3)] for d in (-1, 0, 1)]
         slope = tendency(*rows, 1, 1.0)
-        ok = columns_ok * row_ok(e)
         for c in range(3):
-            v2[c, e] = (rows[1][c] + (0.5 * half_step) * slope[c] + rest[c, e]) * ok
+            v2[c, e] = (rows[1][c] + (0.5 * half_step) * slope[c] + rest[c, e]) * row_ok(e)
             h1[c, e] = slope[c]
         return carry
 
     lax.fori_loop(2, 20, second, 0)
 
+
+def fine_part(place, *arrays):
+    vmem = pl.BlockSpec(memory_space=pltpu.VMEM)
+    kept = pltpu.VMEM((3, 22, 16, 256), f32)
+    return pl.pallas_call(
+        fine_body,
+        out_shape=[kept] * 6,
+        in_specs=[pl.BlockSpec(memory_space=pltpu.SMEM)] + [vmem] * len(arrays),
+        out_specs=[vmem] * 6,
+        scratch_shapes=[pltpu.VMEM((9, 22, 16, 256), f32), kept],
+        compiler_params=pltpu.CompilerParams(vmem_limit_bytes=28 * 2**20),
+        name="fine",
+    )(place, *near(*arrays))
+
+
+def strip_body(place, low, high, south, north, strips):
+    lane = lanes((16, 768))
+    row = lane % 384 // 16
+    south_side = (lane < 384) & (lane % 16 < 4)
+    north_side = (lane >= 384) & (lane % 16 > 11)
+    column_ok = jnp.where(south_side, edge_factor(place, 1, True), jnp.where(north_side, edge_factor(place, 1, False), 1.0))
+    rows_ok = jnp.where(row < 3, edge_factor(place, 0, True), jnp.where(row > 18, edge_factor(place, 0, False), 1.0))
+    ok = column_ok * rows_ok
+    slot = lanes((16, 384)) % 16
+
+    def whole(k):
+        left = jnp.where(slot < 4, pltpu.roll(south[k], 376, 1), low[k])
+        right = jnp.where(slot > 11, pltpu.roll(north[k], 8, 1), high[k])
+        return jnp.concatenate([left, right], axis=1)
+
+    def around(rows):
+        return [pltpu.roll(r, 16, 1) for r in rows], rows, [pltpu.roll(r, 752, 1) for r in rows]
+
+    u = [[whole(3 * node + c) for c in range(3)] for node in range(3)]
+    nodes = [around(u[node]) for node in range(3)]
+    new, more, flux = swept(lambda node: nodes[node])
+    v1 = [value * ok for value in new]
+    h1 = tendency(*around(v1), 1, 1.0)
+    v2 = [(v1[c] + (0.5 * half_step) * h1[c] + more[c]) * ok for c in range(3)]
+    h2 = tendency(*around(v2), 1, 1.0)
+    base_u = tendency(*around([paired(x) for x in u[0]]), 2, 2.0)
+    base_v = tendency(*around([paired(x) for x in v1]), 2, 2.0)
+    for c in range(3):
+        one, two = source_pair(place[2] == 0, u[0][c], flux[c], h1[c], h2[c], base_u[c], base_v[c])
+        for part, value in enumerate((one, two, v1[c], v2[c])):
+            for t in range(6):
+                strips[part * 3 + c, t] = value[:, t * 128:(t + 1) * 128]
+
+
+def strip_part(place, *arrays):
+    vmem = pl.BlockSpec(memory_space=pltpu.VMEM)
+    return pl.pallas_call(
+        strip_body,
+        out_shape=pltpu.VMEM((12, 6, 16, 128), f32),
+        in_specs=[pl.BlockSpec(memory_space=pltpu.SMEM)] + [vmem] * 4,
+        out_specs=vmem,
+        compiler_params=pltpu.CompilerParams(vmem_limit_bytes=8 * 2**20),
+        name="strip",
+    )(place, *near(*arrays))
+
+
+def joined(value, strips, at, e):
+    lane = lanes((16, 128))
+    shift = e % 8 * 16
+    left = pltpu.roll(strips[at, e // 8], 124 - shift, 1)
+    right = pltpu.roll(strips[at, 3 + e // 8], 116 - shift, 1)
+    low = jnp.where(lane < 4, left, value[:, 0:128])
+    high = jnp.where(lane >= 124, right, value[:, 128:256])
+    return jnp.concatenate([low, high], axis=1)
+
+
+def halves_body(values, strips, halves, native_0, native_1, turned, part):
     def moved(e, carry):
         for c in range(3):
-            put((native_0, native_1), c * 256, e - 3, v2[c, e])
+            put((native_0, native_1), c * 256, e - 3, joined(values[c, e], strips, part * 3 + c, e))
         return carry
 
     lax.fori_loop(3, 19, moved, 0)
 
     for c in range(3):
         for odd in (0, 1):
+            tile = c * 256 + odd * 128
             for half, native in enumerate((native_0, native_1)):
-                one, two = split_pairs(native, c * 256 + odd * 128, turned.at[(c * 2 + odd) * 2 + half])
-                halves_2[half * 64:half * 64 + 64, c * 256 + odd * 128:c * 256 + odd * 128 + 128] = 0.5 * (one - two)
-
-
-def fine_part(place, *arrays):
-    vmem = pl.BlockSpec(memory_space=pltpu.VMEM)
-    kept = pltpu.VMEM((3, 22, 16, 384), f32)
-    return pl.pallas_call(
-        fine_body,
-        out_shape=[pltpu.VMEM((128, 768), f32)] + [kept] * 6,
-        in_specs=[pl.BlockSpec(memory_space=pltpu.SMEM)] + [vmem] * len(arrays),
-        out_specs=[vmem] * 7,
-        scratch_shapes=[pltpu.VMEM((9, 22, 16, 384), f32), kept]
-        + [pltpu.VMEM((768, 128), f32)] * 2
-        + [pltpu.VMEM((12, 128, 128), f32)],
-        compiler_params=pltpu.CompilerParams(vmem_limit_bytes=36 * 2**20),
-        name="fine",
-    )(place, *near(*arrays))
-
-
-def sources_body(place, field, v1, v2, f0, h1, pair_u, pair_v, sources, halves_1, native_0, native_1, turned):
+                one, two = split_pairs(native, tile, turned.at[(c * 2 + odd) * 2 + half])
+                halves[half * 64:half * 64 + 64, tile:tile + 128] = 0.5 * (one - two)
+
+
+def halves_part(values, strips, part):
+    vmem = pl.BlockSpec(memory_space=pltpu.VMEM)
+    return pl.pallas_call(
+        functools.partial(halves_body, part=part),
+        out_shape=pltpu.VMEM((128, 768), f32),
+        in_specs=[vmem] * 2,
+        out_specs=vmem,
+        scratch_shapes=[pltpu.VMEM((768, 128), f32)] * 2 + [pltpu.VMEM((12, 128, 128), f32)],
+        compiler_params=pltpu.CompilerParams(vmem_limit_bytes=8 * 2**20),
+        name="halves",
+    )(*near(values, strips))
+
+
+def sources_body(place, field, strips, v2, f0, h1, pair_u, pair_v, sources, native_0, native_1, turned):
     gy = place[1]
     leader = place[2] == 0
     natives = (native_0, native_1)
@@ -262,32 +336,23 @@
         base_u = tendency(*[[pair_u[c, e + d] for c in range(3)] for d in (-1, 0, 1)], 2, 2.0)
         base_v = tendency(*[[pair_v[c, e + d] for c in range(3)] for d in (-1, 0, 1)], 2, 2.0)
         for c in range(3):
-            a, b, d = f0[c, e, :, 0:256], h1[c, e, :, 0:256], slope[c][:, 0:256]
-            one = one_0 * a + one_1 * b + one_2 * d
-            two = two_0 * a + two_1 * b + two_2 * d
-            one = one + jnp.where(leader, field[c, e - 3], (-0.5 * half_step) * base_u[c][:, 0:256])
-            two = two - (0.5 * half_step) * base_v[c][:, 0:256]
-            put(natives, c * 256, e - 3, one)
-            put(natives, (3 + c) * 256, e - 3, two)
-            put(natives, (6 + c) * 256, e - 3, v1[c, e, :, 0:256])
+            both = source_pair(leader, field[c, e - 3], f0[c, e], h1[c, e], slope[c], base_u[c], base_v[c])
+            for part, value in enumerate(both):
+                put(natives, (3 * part + c) * 256, e - 3, joined(value, strips, 3 * part + c, e))
         return carry
 
     lax.fori_loop(3, 19, third, 0)
 
     def compact(c, carry):
-        for part in range(3):
+        for part in range(2):
             for odd in (0, 1):
                 start = pl.multiple_of((part * 3 + c) * 256 + odd * 128, 128)
                 for half, native in enumerate(natives):
                     one, two = split_pairs(native, start, turned.at[(part * 2 + odd) * 2 + half])
-                    tile = pl.multiple_of(c * 256 + odd * 128, 128)
-                    if part == 2:
-                        halves_1[pl.ds(half * 64, 64), pl.ds(tile, 128)] = 0.5 * (one - two)
-                    else:
-                        mean = 0.5 * (one + two)
-                        for i in range(8):
-                            to = device_of(half * 8 + i, gy)
-                            sources[to, :, pl.ds(part * 768 + tile, 128)] = mean[8 * i:8 * i + 8]
+                    mean = 0.5 * (one + two)
+                    tile = pl.multiple_of(part * 768 + c * 256 + odd * 128, 128)
+                    for i in range(8):
+                        sources[device_of(half * 8 + i, gy), :, pl.ds(tile, 128)] = mean[8 * i:8 * i + 8]
         return carry
 
     lax.fori_loop(0, 3, compact, 0)
@@ -297,10 +362,10 @@
     vmem = pl.BlockSpec(memory_space=pltpu.VMEM)
     return pl.pallas_call(
         sources_body,
-        out_shape=(pltpu.VMEM((16, 8, 1536), f32), jax.ShapeDtypeStruct((128, 768), f32)),
+        out_shape=pltpu.VMEM((16, 8, 1536), f32),
         in_specs=[pl.BlockSpec(memory_space=pltpu.SMEM)] + [vmem] * len(arrays),
-        out_specs=[vmem] * 2,
-        scratch_shapes=[pltpu.VMEM((2304, 128), f32)] * 2 + [pltpu.VMEM((12, 128, 128), f32)],
+        out_specs=vmem,
+        scratch_shapes=[pltpu.VMEM((1536, 128), f32)] * 2 + [pltpu.VMEM((8, 128, 128), f32)],
         compiler_params=pltpu.CompilerParams(vmem_limit_bytes=16 * 2**20),
         name="sources",
     )(place, *near(*arrays))
@@ -539,16 +604,19 @@
         after = sent(low_rows, ("gx",), sizes, {"gx": -1})
         before = sent(high_rows, ("gx",), sizes, {"gx": 1})
         field = turned_field(held)
-        low_columns, high_columns = columns(field, before, after)
-        south = sent(high_columns, ("gy",), sizes, {"gy": 1})
-        north = sent(low_columns, ("gy",), sizes, {"gy": -1})
-        halves_2, *kept = fine_part(place, field, before, after, south, north)
+        low, high = columns(field, before, after)
+        south = sent(high, ("gy",), sizes, {"gy": 1})
+        north = sent(low, ("gy",), sizes, {"gy": -1})
+        v1, v2, *kept = fine_part(place, field, before, after)
+        strips = strip_part(place, low, high, south, north)
+        halves_2 = halves_part(v2, strips, 3)
         halves_0 = lax.ppermute(halves_2, ("tz", "ty"), [(i, i + 1) for i in range(15)])
-        sources, halves_1 = sources_part(place, field, *kept)
+        sources = sources_part(place, field, strips, v2, *kept)
         source = lax.all_to_all(sources, group_axes, 0, 0)
         to_right, to_left = pack(source)
         source_left = beside(to_right, 1)
         source_right = beside(to_left, -1)
+        halves_1 = halves_part(v1, strips, 2)
         starts = ()
         for turn in range(4):
             own = stage(place, starts, (source, source_left, source_right), turn == 3)

time: 174 us -> 174 us (level)
  the two profiles are of different devices: /device:TPU:1 before, /device:TPU:66 now
where the time goes in v6:
time: 174 us; the launch traced here: 173 us
  starting transfers between devices  66.8 us (38%)
  Pallas kernels  40.6 us (23%)
  waiting for transfers between devices  35.7 us (21%)
  blocking collectives  23.6 us (14%)
  local copies, waits for them, and re-layouts  5.73 us (3%)
    ppermute x7, starting transfers between devices, sent(): return lax.ppermute(block, axes if len(axes) > 1 else axes[0], pairs)  25.7 us
    ppermute x8, starting transfers between devices, beside(): return lax.ppermute(block, pieces, pairs)  23.9 us
    all_to_all x1, blocking collectives, per_device(): source = lax.all_to_all(sources, group_axes, 0, 0)  23.6 us
    all_to_all x1, starting transfers between devices, per_device(): coarse = lax.all_to_all(own, group_axes, 0, 0)  15.3 us
    all_to_all x1, waiting for transfers between devices, per_device(): coarse = lax.all_to_all(own, group_axes, 0, 0)  14.3 us
    ppermute x8, waiting for transfers between devices, beside(): return lax.ppermute(block, pieces, pairs)  13.5 us
    pallas_call x4, Pallas kernels, stage(): pl.pallas_call(functools.partial(stage_body, begins=not starts, ends=ends...  12.7 us
    ppermute x7, waiting for transfers between devices, sent(): return lax.ppermute(block, axes if len(axes) > 1 else axes[0], pairs)  7.88 us
  transfers between devices with their start and end apart: 17, of which 11 were waited for; matrix products, arithmetic and copies ran while one was open for 0% of the time, Pallas kernels for 9%

profile of v6, /device:TPU:66, one launch (start us, length us, event | category | flops | bytes accessed | tf_op | source)
XLA Modules:
  0.0 172.8 jit_solution(1512706276492117547)
XLA Ops:
  1.7 1.8 %collective-permute-start = (f32[9,3,16,256]{3,2,1,0:T(8,128)S(1)}, f32[9,3,16,256]{3,2,1,0:T(8,128)S(1)}, u32[]{:S(2)}, u32[]{:S(2)}) collective-permute-start(f32[9,3,16,256]{3,2,1,0:T(8,128)S(1)} %get-tuple-element.23), channel_id=1, source_target_pairs={{0,4},{4,8},{8,12},{1,5},{5,9},{9,13},{2,6},{6,10},{10,14},{3,7},{... | collective-permute-start | bytes 1327112 | tf_op jit(solution)/shard_map/ppermute | solution.py:581
  6.2 2.6 %collective-permute-done.1.after = f32[9,3,16,256]{3,2,1,0:T(8,128)S(1)} collective-permute-done((f32[9,3,16,256]{3,2,1,0:T(8,128)S(1)}, f32[9,3,16,256]{3,2,1,0:T(8,128)S(1)}, u32[]{:S(2)}, u32[]{:S(2)}) %collective-permute-start.1) | collective-permute-done | bytes 442400 | tf_op jit(solution)/shard_map/ppermute | solution.py:581
  8.9 2.1 %columns.1 = (f32[9,16,384]{2,1,0:T(8,128)S(1)}, f32[9,16,384]{2,1,0:T(8,128)}) custom-call(f32[9,16,16,256]{3,2,1,0:T(8,128)S(1)} %turned.1.field, f32[9,3,16,256]{3,2,1,0:T(8,128)S(1)} %collective-permute-done.before, f32[9,3,16,256]{3,2,1,0:T(8,128)S(1)} %collective-permute-done.1.after), custom_call_target="tpu_custom_call" | custom-call | tf_op jit(solution)/shard_map/columns/pallas_call | solution.py:118
  11.0 2.4 %collective-permute-start.3 = (f32[9,16,384]{2,1,0:T(8,128)S(1)}, f32[9,16,384]{2,1,0:T(8,128)}, u32[]{:S(2)}, u32[]{:S(2)}) collective-permute-start(f32[9,16,384]{2,1,0:T(8,128)S(1)} %get-tuple-element.25.low), channel_id=1, source_target_pairs={{1,0},{2,1},{3,2},{5,4},{6,5},{7,6},{9,8},{10,9},{11,10},{13,12},{... | collective-permute-start | bytes 663560 | tf_op jit(solution)/shard_map/ppermute | solution.py:581
  13.4 3.4 %collective-permute-start.2 = (f32[9,16,384]{2,1,0:T(8,128)}, f32[9,16,384]{2,1,0:T(8,128)}, u32[]{:S(2)}, u32[]{:S(2)}) collective-permute-start(f32[9,16,384]{2,1,0:T(8,128)} %get-tuple-element.26.high), channel_id=1, source_target_pairs={{0,1},{1,2},{2,3},{4,5},{5,6},{6,7},{8,9},{9,10},{10,11},{12,13},{... | collective-permute-start | bytes 663560 | tf_op jit(solution)/shard_map/ppermute | solution.py:581
  17.0 7.8 %fine.1 = (f32[3,22,16,256]{3,2,1,0:T(8,128)S(1)}, f32[3,22,16,256]{3,2,1,0:T(8,128)S(1)}, f32[3,22,16,256]{3,2,1,0:T(8,128)S(1)}, f32[3,22,16,256]{3,2,1,0:T(8,...) custom-call(s32[4]{0:T(128)S(1)} %pad_add_fusion.place, f32[9,16,16,256]{3,2,1,0:T(8,128)S(1)} %turned.1.field, ...), custom_call_target="tpu_custom_call" | custom-call | tf_op jit(solution)/shard_map/fine/pallas_call | solution.py:233
  24.8 3.2 %strip.1.strips = f32[12,6,16,128]{3,2,1,0:T(8,128)S(1)} custom-call(s32[4]{0:T(128)S(1)} %pad_add_fusion.place, f32[9,16,384]{2,1,0:T(8,128)S(1)} %get-tuple-element.25.low, f32[9,16,384]{2,1,0:T(8,128)} %get-tuple-element.26.high, f32[9,16,384]{2,1,0:T(8,128)} %collective-permute-done.2.south, f32[9,16,384]{2,1,0:T(8,128)} %collective-permute-done.3.north), custom_call_target="tpu_custom_call" | custom-call | tf_op jit(solution)/shard_map/strip/pallas_call | solution.py:280
  28.0 4.3 %sources.1 = f32[16,8,1536]{2,1,0:T(8,128)S(1)} custom-call(s32[4]{0:T(128)S(1)} %pad_add_fusion.place, f32[9,16,16,256]{3,2,1,0:T(8,128)S(1)} %turned.1.field, f32[12,6,16,128]{3,2,1,0:T(8,128)S(1)} %strip.1.strips, f32[3,22,16,256]{3,2,1,0:T(8,128)S(1)} %get-tuple-element.27.v2.values, f32[3,22,16,256]{3,2,1,0:T(8,128)S(1)} %get-tuple-element.28.f0, ...), custom_call_target="tpu_custom_call" | custom-call | tf_op jit(solution)/shard_map/sources/pallas_call | solution.py:363
  32.2 23.6 %all_to_all.10.source.rest_0_.rest_3_ = f32[16,8,1536]{2,1,0:T(8,128)S(1)} all-to-all(f32[16,8,1536]{2,1,0:T(8,128)S(1)} %sources.1), channel_id=1, replica_groups=mesh['tz'=4,'ty'=4,'gx'=4,'gy'=4] {'ty','gx'}, dimensions={0} | all-to-all | bytes 1572864 | tf_op jit(solution)/shard_map/all_to_all | solution.py:615
  55.9 4.1 %collective-permute-start.4 = (f32[8,8,1536]{2,1,0:T(8,128)S(1)}, f32[8,8,1536]{2,1,0:T(8,128)S(1)}, u32[]{:S(2)}, u32[]{:S(2)}) collective-permute-start(f32[8,8,1536]{2,1,0:T(8,128)S(1)} %get-tuple-element.32), channel_id=1, source_target_pairs={{0,4},{4,8},{8,12},{12,28},{28,24},{24,20},{20,16},{16,32},{32,36}... | collective-permute-start | bytes 1179656 | tf_op jit(solution)/shard_map/ppermute | solution.py:595
  60.0 1.9 %collective-permute-start.5 = (f32[8,8,1536]{2,1,0:T(8,128)S(1)}, f32[8,8,1536]{2,1,0:T(8,128)S(1)}, u32[]{:S(2)}, u32[]{:S(2)}) collective-permute-start(f32[8,8,1536]{2,1,0:T(8,128)S(1)} %get-tuple-element.33), channel_id=1, source_target_pairs={{4,0},{8,4},{12,8},{28,12},{24,28},{20,24},{16,20},{32,16},{36,32}... | collective-permute-start | bytes 1179656 | tf_op jit(solution)/shard_map/ppermute | solution.py:595
  61.9 3.3 %collective-permute-done.4.rest_1_.rest_4_ = f32[8,8,1536]{2,1,0:T(8,128)S(1)} collective-permute-done((f32[8,8,1536]{2,1,0:T(8,128)S(1)}, f32[8,8,1536]{2,1,0:T(8,128)S(1)}, u32[]{:S(2)}, u32[]{:S(2)}) %collective-permute-start.4) | collective-permute-done | bytes 393248 | tf_op jit(solution)/shard_map/ppermute | solution.py:595
  65.3 4.4 %collective-permute-done.5.rest_2_.rest_5_ = f32[8,8,1536]{2,1,0:T(8,128)S(1)} collective-permute-done((f32[8,8,1536]{2,1,0:T(8,128)S(1)}, f32[8,8,1536]{2,1,0:T(8,128)S(1)}, u32[]{:S(2)}, u32[]{:S(2)}) %collective-permute-start.5) | collective-permute-done | bytes 393248 | tf_op jit(solution)/shard_map/ppermute | solution.py:595
  69.6 3.2 %stage.4 = f32[3,8,8,128]{3,2,1,0:T(8,128)S(1)} custom-call(s32[4]{0:T(128)S(1)} %pad_add_fusion.place, f32[16,8,1536]{2,1,0:T(8,128)S(1)} %all_to_all.10.source.rest_0_.rest_3_, f32[8,8,1536]{2,1,0:T(8,128)S(1)} %collective-permute-done.4.rest_1_.rest_4_, f32[8,8,1536]{2,1,0:T(8,128)S(1)} %collective-permute-done.5.rest_2_.rest_5_), custom_call_target="tpu_custom_call" | custom-call | tf_op jit(solution)/shard_map/stage/pallas_call | solution.py:509
  72.8 5.5 %collective-permute-start.6 = (f32[3,8,8,128]{3,2,1,0:T(8,128)S(1)}, f32[3,8,8,128]{3,2,1,0:T(8,128)S(1)}, u32[]{:S(2)}, u32[]{:S(2)}) collective-permute-start(f32[3,8,8,128]{3,2,1,0:T(8,128)S(1)} %stage.4), channel_id=1, source_target_pairs={{0,64},{64,128},{128,192},{1,65},{65,129},{129,193},{2,66},{66,130... | collective-permute-start | bytes 294920 | tf_op jit(solution)/shard_map/ppermute | solution.py:581
  78.3 2.2 %collective-permute-done.6.rest_0_ = f32[3,8,8,128]{3,2,1,0:T(8,128)S(1)} collective-permute-done((f32[3,8,8,128]{3,2,1,0:T(8,128)S(1)}, f32[3,8,8,128]{3,2,1,0:T(8,128)S(1)}, u32[]{:S(2)}, u32[]{:S(2)}) %collective-permute-start.6) | collective-permute-done | bytes 98336 | tf_op jit(solution)/shard_map/ppermute | solution.py:581
  80.5 1.9 %collective-permute-start.8 = (f32[3,8,8,128]{3,2,1,0:T(8,128)S(1)}, f32[3,8,8,128]{3,2,1,0:T(8,128)S(1)}, u32[]{:S(2)}, u32[]{:S(2)}) collective-permute-start(f32[3,8,8,128]{3,2,1,0:T(8,128)S(1)} %collective-permute-done.6.rest_0_), channel_id=1, source_target_pairs={{4,0},{8,4},{12,8},{28,12},{24,28},{20,24},{16,20},{32,16},{36,32}... | collective-permute-start | bytes 294920 | tf_op jit(solution)/shard_map/ppermute | solution.py:595
  82.4 3.9 %collective-permute-start.7 = (f32[3,8,8,128]{3,2,1,0:T(8,128)S(1)}, f32[3,8,8,128]{3,2,1,0:T(8,128)S(1)}, u32[]{:S(2)}, u32[]{:S(2)}) collective-permute-start(f32[3,8,8,128]{3,2,1,0:T(8,128)S(1)} %collective-permute-done.6.rest_0_), channel_id=1, source_target_pairs={{0,4},{4,8},{8,12},{12,28},{28,24},{24,20},{20,16},{16,32},{32,36}... | collective-permute-start | bytes 294920 | tf_op jit(solution)/shard_map/ppermute | solution.py:595
  88.5 3.2 %stage.5 = f32[3,8,8,128]{3,2,1,0:T(8,128)S(1)} custom-call(s32[4]{0:T(128)S(1)} %pad_add_fusion.place, f32[3,8,8,128]{3,2,1,0:T(8,128)S(1)} %collective-permute-done.6.rest_0_, f32[3,8,8,128]{3,2,1,0:T(8,128)S(1)} %collective-permute-done.7.rest_1_, f32[3,8,8,128]{3,2,1,0:T(8,128)S(1)} %collective-permute-done.8.rest_2_, ...), custom_call_target="tpu_custom_call" | custom-call | tf_op jit(solution)/shard_map/stage/pallas_call | solution.py:509
  91.7 6.4 %collective-permute-start.9 = (f32[3,8,8,128]{3,2,1,0:T(8,128)S(1)}, f32[3,8,8,128]{3,2,1,0:T(8,128)S(1)}, u32[]{:S(2)}, u32[]{:S(2)}) collective-permute-start(f32[3,8,8,128]{3,2,1,0:T(8,128)S(1)} %stage.5), channel_id=1, source_target_pairs={{0,64},{64,128},{128,192},{1,65},{65,129},{129,193},{2,66},{66,130... | collective-permute-start | bytes 294920 | tf_op jit(solution)/shard_map/ppermute | solution.py:581
  99.9 1.9 %collective-permute-start.15 = (f32[128,768]{1,0:T(8,128)S(1)}, f32[128,768]{1,0:T(8,128)S(1)}, u32[]{:S(2)}, u32[]{:S(2)}) collective-permute-start(f32[128,768]{1,0:T(8,128)S(1)} %halves.2.halves_2), channel_id=1, source_target_pairs={{0,16},{16,32},{32,48},{48,64},{64,80},{80,96},{96,112},{112,128},... | collective-permute-start | bytes 1179656 | tf_op jit(solution)/shard_map/ppermute | solution.py:613
  101.9 1.9 %collective-permute-start.11 = (f32[3,8,8,128]{3,2,1,0:T(8,128)S(1)}, f32[3,8,8,128]{3,2,1,0:T(8,128)S(1)}, u32[]{:S(2)}, u32[]{:S(2)}) collective-permute-start(f32[3,8,8,128]{3,2,1,0:T(8,128)S(1)} %collective-permute-done.9.rest_0_), channel_id=1, source_target_pairs={{4,0},{8,4},{12,8},{28,12},{24,28},{20,24},{16,20},{32,16},{36,32}... | collective-permute-start | bytes 294920 | tf_op jit(solution)/shard_map/ppermute | solution.py:595
  103.8 4.3 %collective-permute-start.10 = (f32[3,8,8,128]{3,2,1,0:T(8,128)S(1)}, f32[3,8,8,128]{3,2,1,0:T(8,128)S(1)}, u32[]{:S(2)}, u32[]{:S(2)}) collective-permute-start(f32[3,8,8,128]{3,2,1,0:T(8,128)S(1)} %collective-permute-done.9.rest_0_), channel_id=1, source_target_pairs={{0,4},{4,8},{8,12},{12,28},{28,24},{24,20},{20,16},{16,32},{32,36}... | collective-permute-start | bytes 294920 | tf_op jit(solution)/shard_map/ppermute | solution.py:595
  110.3 3.2 %stage.6 = f32[3,8,8,128]{3,2,1,0:T(8,128)S(1)} custom-call(s32[4]{0:T(128)S(1)} %pad_add_fusion.place, f32[3,8,8,128]{3,2,1,0:T(8,128)S(1)} %collective-permute-done.9.rest_0_, f32[3,8,8,128]{3,2,1,0:T(8,128)S(1)} %collective-permute-done.10.rest_1_, f32[3,8,8,128]{3,2,1,0:T(8,128)S(1)} %collective-permute-done.11.rest_2_, ...), custom_call_target="tpu_custom_call" | custom-call | tf_op jit(solution)/shard_map/stage/pallas_call | solution.py:509
  113.5 4.9 %collective-permute-start.12 = (f32[3,8,8,128]{3,2,1,0:T(8,128)S(1)}, f32[3,8,8,128]{3,2,1,0:T(8,128)S(1)}, u32[]{:S(2)}, u32[]{:S(2)}) collective-permute-start(f32[3,8,8,128]{3,2,1,0:T(8,128)S(1)} %stage.6), channel_id=1, source_target_pairs={{0,64},{64,128},{128,192},{1,65},{65,129},{129,193},{2,66},{66,130... | collective-permute-start | bytes 294920 | tf_op jit(solution)/shard_map/ppermute | solution.py:581
  118.4 3.0 %collective-permute-done.12.rest_0_ = f32[3,8,8,128]{3,2,1,0:T(8,128)S(1)} collective-permute-done((f32[3,8,8,128]{3,2,1,0:T(8,128)S(1)}, f32[3,8,8,128]{3,2,1,0:T(8,128)S(1)}, u32[]{:S(2)}, u32[]{:S(2)}) %collective-permute-start.12) | collective-permute-done | bytes 98336 | tf_op jit(solution)/shard_map/ppermute | solution.py:581
  121.4 1.9 %collective-permute-start.14 = (f32[3,8,8,128]{3,2,1,0:T(8,128)S(1)}, f32[3,8,8,128]{3,2,1,0:T(8,128)S(1)}, u32[]{:S(2)}, u32[]{:S(2)}) collective-permute-start(f32[3,8,8,128]{3,2,1,0:T(8,128)S(1)} %collective-permute-done.12.rest_0_), channel_id=1, source_target_pairs={{4,0},{8,4},{12,8},{28,12},{24,28},{20,24},{16,20},{32,16},{36,32}... | collective-permute-start | bytes 294920 | tf_op jit(solution)/shard_map/ppermute | solution.py:595
  123.3 3.9 %collective-permute-start.13 = (f32[3,8,8,128]{3,2,1,0:T(8,128)S(1)}, f32[3,8,8,128]{3,2,1,0:T(8,128)S(1)}, u32[]{:S(2)}, u32[]{:S(2)}) collective-permute-start(f32[3,8,8,128]{3,2,1,0:T(8,128)S(1)} %collective-permute-done.12.rest_0_), channel_id=1, source_target_pairs={{0,4},{4,8},{8,12},{12,28},{28,24},{24,20},{20,16},{16,32},{32,36}... | collective-permute-start | bytes 294920 | tf_op jit(solution)/shard_map/ppermute | solution.py:595
  129.4 3.2 %stage.7 = f32[16,8,2304]{2,1,0:T(8,128)S(1)} custom-call(s32[4]{0:T(128)S(1)} %pad_add_fusion.place, f32[3,8,8,128]{3,2,1,0:T(8,128)S(1)} %collective-permute-done.12.rest_0_, f32[3,8,8,128]{3,2,1,0:T(8,128)S(1)} %collective-permute-done.13.rest_1_, f32[3,8,8,128]{3,2,1,0:T(8,128)S(1)} %collective-permute-done.14.rest_2_, ...), custom_call_target="tpu_custom_call" | custom-call | tf_op jit(solution)/shard_map/stage/pallas_call | solution.py:509
  133.6 15.3 %all-to-all-start.1 = ((f32[16,8,2304]{2,1,0:T(8,128)}), f32[16,8,2304]{2,1,0:T(8,128)}, u32[]{:S(2)}, u32[]{:S(2)}) async-start(f32[16,8,2304]{2,1,0:T(8,128)} %copy-done.1), calls=%async_computation.1 | async-start | bytes 2359296 | tf_op jit(solution)/shard_map/all_to_all | solution.py:628
  152.7 14.3 %all-to-all-done.1.coarse = f32[16,8,2304]{2,1,0:T(8,128)} async-done(((f32[16,8,2304]{2,1,0:T(8,128)}), f32[16,8,2304]{2,1,0:T(8,128)}, u32[]{:S(2)}, u32[]{:S(2)}) %all-to-all-start.1) | async-done | bytes 1179680 | tf_op jit(solution)/shard_map/all_to_all | solution.py:628
  169.0 3.8 %finish.1 = f32[288,2,8,128]{3,2,1,0:T(8,128)} custom-call(s32[4]{0:T(128)S(1)} %pad_add_fusion.place, f32[288,2,8,128]{3,2,1,0:T(8,128)S(1)} %bitcast.13, f32[16,8,2304]{2,1,0:T(8,128)} %all-to-all-done.1.coarse, f32[128,768]{1,0:T(8,128)S(1)} %copy-done.7, f32[128,768]{1,0:T(8,128)S(1)} %copy-done.3, f32[128,768]{1,0:T(8,128)S(1)} %halves.2.halves_2), custom_call_target="tpu_custom_call" | custom-call | tf_op jit(solution)/shard_map/finish/pallas_call | solution.py:552
  (34 shorter events, 19.6 us)
Async XLA Ops:
  1.7 4.5 %collective-permute-start = (f32[9,3,16,256]{3,2,1,0:T(8,128)S(1)}, f32[9,3,16,256]{3,2,1,0:T(8,128)S(1)}, u32[]{:S(2)}, u32[]{:S(2)}) collective-permute-start(f32[9,3,16,256]{3,2,1,0:T(8,128)S(1)} %get-tuple-element.23), channel_id=1, source_target_pairs={{0,4},{4,8},{8,12},{1,5},{5,9},{9,13},{2,6},{6,10},{10,14},{3,7},{... | collective-permute-start | bytes 1327112 | tf_op jit(solution)/shard_map/ppermute | solution.py:581
  3.5 5.4 %collective-permute-start.1 = (f32[9,3,16,256]{3,2,1,0:T(8,128)S(1)}, f32[9,3,16,256]{3,2,1,0:T(8,128)S(1)}, u32[]{:S(2)}, u32[]{:S(2)}) collective-permute-start(f32[9,3,16,256]{3,2,1,0:T(8,128)S(1)} %get-tuple-element.24), channel_id=1, source_target_pairs={{4,0},{8,4},{12,8},{5,1},{9,5},{13,9},{6,2},{10,6},{14,10},{7,3},{... | collective-permute-start | bytes 1327112 | tf_op jit(solution)/shard_map/ppermute | solution.py:581
  11.0 13.8 %collective-permute-start.3 = (f32[9,16,384]{2,1,0:T(8,128)S(1)}, f32[9,16,384]{2,1,0:T(8,128)}, u32[]{:S(2)}, u32[]{:S(2)}) collective-permute-start(f32[9,16,384]{2,1,0:T(8,128)S(1)} %get-tuple-element.25.low), channel_id=1, source_target_pairs={{1,0},{2,1},{3,2},{5,4},{6,5},{7,6},{9,8},{10,9},{11,10},{13,12},{... | collective-permute-start | bytes 663560 | tf_op jit(solution)/shard_map/ppermute | solution.py:581
  13.4 11.3 %collective-permute-start.2 = (f32[9,16,384]{2,1,0:T(8,128)}, f32[9,16,384]{2,1,0:T(8,128)}, u32[]{:S(2)}, u32[]{:S(2)}) collective-permute-start(f32[9,16,384]{2,1,0:T(8,128)} %get-tuple-element.26.high), channel_id=1, source_target_pairs={{0,1},{1,2},{2,3},{4,5},{5,6},{6,7},{8,9},{9,10},{10,11},{12,13},{... | collective-permute-start | bytes 663560 | tf_op jit(solution)/shard_map/ppermute | solution.py:581
  24.8 7.5 %copy-start.4 = (f32[3,22,16,256]{3,2,1,0:T(8,128)}, f32[3,22,16,256]{3,2,1,0:T(8,128)S(1)}, u32[]{:S(2)}) copy-start(f32[3,22,16,256]{3,2,1,0:T(8,128)S(1)} %get-tuple-element.38.values) | copy-start | bytes 3244036
  55.9 9.4 %collective-permute-start.4 = (f32[8,8,1536]{2,1,0:T(8,128)S(1)}, f32[8,8,1536]{2,1,0:T(8,128)S(1)}, u32[]{:S(2)}, u32[]{:S(2)}) collective-permute-start(f32[8,8,1536]{2,1,0:T(8,128)S(1)} %get-tuple-element.32), channel_id=1, source_target_pairs={{0,4},{4,8},{8,12},{12,28},{28,24},{24,20},{20,16},{16,32},{32,36}... | collective-permute-start | bytes 1179656 | tf_op jit(solution)/shard_map/ppermute | solution.py:595
  60.0 9.7 %collective-permute-start.5 = (f32[8,8,1536]{2,1,0:T(8,128)S(1)}, f32[8,8,1536]{2,1,0:T(8,128)S(1)}, u32[]{:S(2)}, u32[]{:S(2)}) collective-permute-start(f32[8,8,1536]{2,1,0:T(8,128)S(1)} %get-tuple-element.33), channel_id=1, source_target_pairs={{4,0},{8,4},{12,8},{28,12},{24,28},{20,24},{16,20},{32,16},{36,32}... | collective-permute-start | bytes 1179656 | tf_op jit(solution)/shard_map/ppermute | solution.py:595
  72.8 7.7 %collective-permute-start.6 = (f32[3,8,8,128]{3,2,1,0:T(8,128)S(1)}, f32[3,8,8,128]{3,2,1,0:T(8,128)S(1)}, u32[]{:S(2)}, u32[]{:S(2)}) collective-permute-start(f32[3,8,8,128]{3,2,1,0:T(8,128)S(1)} %stage.4), channel_id=1, source_target_pairs={{0,64},{64,128},{128,192},{1,65},{65,129},{129,193},{2,66},{66,130... | collective-permute-start | bytes 294920 | tf_op jit(solution)/shard_map/ppermute | solution.py:581
  80.5 6.5 %collective-permute-start.8 = (f32[3,8,8,128]{3,2,1,0:T(8,128)S(1)}, f32[3,8,8,128]{3,2,1,0:T(8,128)S(1)}, u32[]{:S(2)}, u32[]{:S(2)}) collective-permute-start(f32[3,8,8,128]{3,2,1,0:T(8,128)S(1)} %collective-permute-done.6.rest_0_), channel_id=1, source_target_pairs={{4,0},{8,4},{12,8},{28,12},{24,28},{20,24},{16,20},{32,16},{36,32}... | collective-permute-start | bytes 294920 | tf_op jit(solution)/shard_map/ppermute | solution.py:595
  82.4 6.1 %collective-permute-start.7 = (f32[3,8,8,128]{3,2,1,0:T(8,128)S(1)}, f32[3,8,8,128]{3,2,1,0:T(8,128)S(1)}, u32[]{:S(2)}, u32[]{:S(2)}) collective-permute-start(f32[3,8,8,128]{3,2,1,0:T(8,128)S(1)} %collective-permute-done.6.rest_0_), channel_id=1, source_target_pairs={{0,4},{4,8},{8,12},{12,28},{28,24},{24,20},{20,16},{16,32},{32,36}... | collective-permute-start | bytes 294920 | tf_op jit(solution)/shard_map/ppermute | solution.py:595
  91.7 10.1 %collective-permute-start.9 = (f32[3,8,8,128]{3,2,1,0:T(8,128)S(1)}, f32[3,8,8,128]{3,2,1,0:T(8,128)S(1)}, u32[]{:S(2)}, u32[]{:S(2)}) collective-permute-start(f32[3,8,8,128]{3,2,1,0:T(8,128)S(1)} %stage.5), channel_id=1, source_target_pairs={{0,64},{64,128},{128,192},{1,65},{65,129},{129,193},{2,66},{66,130... | collective-permute-start | bytes 294920 | tf_op jit(solution)/shard_map/ppermute | solution.py:581
  99.9 27.3 %collective-permute-start.15 = (f32[128,768]{1,0:T(8,128)S(1)}, f32[128,768]{1,0:T(8,128)S(1)}, u32[]{:S(2)}, u32[]{:S(2)}) collective-permute-start(f32[128,768]{1,0:T(8,128)S(1)} %halves.2.halves_2), channel_id=1, source_target_pairs={{0,16},{16,32},{32,48},{48,64},{64,80},{80,96},{96,112},{112,128},... | collective-permute-start | bytes 1179656 | tf_op jit(solution)/shard_map/ppermute | solution.py:613
  101.9 6.9 %collective-permute-start.11 = (f32[3,8,8,128]{3,2,1,0:T(8,128)S(1)}, f32[3,8,8,128]{3,2,1,0:T(8,128)S(1)}, u32[]{:S(2)}, u32[]{:S(2)}) collective-permute-start(f32[3,8,8,128]{3,2,1,0:T(8,128)S(1)} %collective-permute-done.9.rest_0_), channel_id=1, source_target_pairs={{4,0},{8,4},{12,8},{28,12},{24,28},{20,24},{16,20},{32,16},{36,32}... | collective-permute-start | bytes 294920 | tf_op jit(solution)/shard_map/ppermute | solution.py:595
  103.8 6.5 %collective-permute-start.10 = (f32[3,8,8,128]{3,2,1,0:T(8,128)S(1)}, f32[3,8,8,128]{3,2,1,0:T(8,128)S(1)}, u32[]{:S(2)}, u32[]{:S(2)}) collective-permute-start(f32[3,8,8,128]{3,2,1,0:T(8,128)S(1)} %collective-permute-done.9.rest_0_), channel_id=1, source_target_pairs={{0,4},{4,8},{8,12},{12,28},{28,24},{24,20},{20,16},{16,32},{32,36}... | collective-permute-start | bytes 294920 | tf_op jit(solution)/shard_map/ppermute | solution.py:595
  113.5 7.9 %collective-permute-start.12 = (f32[3,8,8,128]{3,2,1,0:T(8,128)S(1)}, f32[3,8,8,128]{3,2,1,0:T(8,128)S(1)}, u32[]{:S(2)}, u32[]{:S(2)}) collective-permute-start(f32[3,8,8,128]{3,2,1,0:T(8,128)S(1)} %stage.6), channel_id=1, source_target_pairs={{0,64},{64,128},{128,192},{1,65},{65,129},{129,193},{2,66},{66,130... | collective-permute-start | bytes 294920 | tf_op jit(solution)/shard_map/ppermute | solution.py:581
  121.4 6.6 %collective-permute-start.14 = (f32[3,8,8,128]{3,2,1,0:T(8,128)S(1)}, f32[3,8,8,128]{3,2,1,0:T(8,128)S(1)}, u32[]{:S(2)}, u32[]{:S(2)}) collective-permute-start(f32[3,8,8,128]{3,2,1,0:T(8,128)S(1)} %collective-permute-done.12.rest_0_), channel_id=1, source_target_pairs={{4,0},{8,4},{12,8},{28,12},{24,28},{20,24},{16,20},{32,16},{36,32}... | collective-permute-start | bytes 294920 | tf_op jit(solution)/shard_map/ppermute | solution.py:595
  123.3 6.1 %collective-permute-start.13 = (f32[3,8,8,128]{3,2,1,0:T(8,128)S(1)}, f32[3,8,8,128]{3,2,1,0:T(8,128)S(1)}, u32[]{:S(2)}, u32[]{:S(2)}) collective-permute-start(f32[3,8,8,128]{3,2,1,0:T(8,128)S(1)} %collective-permute-done.12.rest_0_), channel_id=1, source_target_pairs={{0,4},{4,8},{8,12},{12,28},{28,24},{24,20},{20,16},{16,32},{32,36}... | collective-permute-start | bytes 294920 | tf_op jit(solution)/shard_map/ppermute | solution.py:595
  127.3 0.8 copy-start.6
  132.6 1.0 copy-start.1
  133.6 33.3 %copy-start = (f32[1,3,3,16,16,256]{5,4,3,2,1,0:T(8,128)S(1)}, f32[1,3,3,16,16,256]{5,4,3,2,1,0:T(8,128)}, u32[]{:S(2)}) copy-start(f32[1,3,3,16,16,256]{5,4,3,2,1,0:T(8,128)} %param.1) | copy-start | bytes 7077892
  133.6 33.3 %all-to-all-start.1 = ((f32[16,8,2304]{2,1,0:T(8,128)}), f32[16,8,2304]{2,1,0:T(8,128)}, u32[]{:S(2)}, u32[]{:S(2)}) async-start(f32[16,8,2304]{2,1,0:T(8,128)} %copy-done.1), calls=%async_computation.1 | async-start | bytes 2359296 | tf_op jit(solution)/shard_map/all_to_all | solution.py:628
  148.9 1.2 copy-start.5
  151.9 0.8 copy-start.2
  167.0 1.0 copy-start.3
  168.0 1.0 copy-start.7

commit v7 on v6

--- a/solution.py
+++ b/solution.py
@@ -120,7 +120,7 @@
         in_specs=[vmem] * 3,
         out_specs=[vmem] * 2,
         out_shape=(shape, shape),
-        compiler_params=pltpu.CompilerParams(vmem_limit_bytes=8 * 2**20),
+        compiler_params=pltpu.CompilerParams(vmem_limit_bytes=3 * 2**20),
         name="columns",
     )(*near(field, before, after))
 
@@ -188,33 +188,83 @@
     return one, two - (0.5 * half_step) * base_v
 
 
-def fine_body(place, field, before, after, v1, v2, f0, h1, pair_u, pair_v, ue, rest):
+def first_sweep(rows_of, factor, at, v1, rest, f0):
+    new, more, flux = swept(rows_of)
+    for c in range(3):
+        value = new[c] if factor is None else new[c] * factor
+        v1[c, at] = value
+        rest[c, at] = more[c]
+        f0[c, at] = flux[c]
+
+
+def inner_body(field, *outs):
+    def first(e, carry):
+        first_sweep(
+            lambda node: [[field[3 * node + c, e - 3 + d] for c in range(3)] for d in (-1, 0, 1)], None, e - 4, *outs
+        )
+        return carry
+
+    lax.fori_loop(4, 18, first, 0)
+
+
+def inner_part(field):
+    vmem = pl.BlockSpec(memory_space=pltpu.VMEM)
+    return pl.pallas_call(
+        inner_body,
+        out_shape=[pltpu.VMEM((3, 14, 16, 256), f32)] * 3,
+        in_specs=[vmem],
+        out_specs=[vmem] * 3,
+        compiler_params=pltpu.CompilerParams(vmem_limit_bytes=3 * 2**20),
+        name="inner",
+    )(*near(field))
+
+
+def fine_body(place, field, before, after, *rest_of):
+    inner = rest_of[:3]
+    v1, f0, pair_u, pair_v, v2, h1, rest, ue, arrived = rest_of[3:]
     low_ok = edge_factor(place, 0, True)
     high_ok = edge_factor(place, 0, False)
 
+    copies = [
+        pltpu.make_async_copy(source, to.at[:, pl.ds(4, 14)], arrived.at[i])
+        for i, (source, to) in enumerate(zip(inner, (v1, rest, f0)))
+    ]
+    for copy in copies:
+        copy.start()
+
     def gather(k, carry):
-        for e in range(22):
+        for e in (0, 1, 2, 3, 4, 17, 18, 19, 20, 21):
             ref, x = (before, e) if e < 3 else (field, e - 3) if e < 19 else (after, e - 19)
             ue[k, e] = ref[k, x]
         return carry
 
     lax.fori_loop(0, 9, gather, 0)
+    for copy in copies:
+        copy.wait()
 
     def row_ok(e):
         return jnp.where(e < 3, low_ok, jnp.where(e > 18, high_ok, 1.0))
 
-    def first(e, carry):
-        new, more, flux = swept(lambda node: [[ue[3 * node + c, e + d] for c in range(3)] for d in (-1, 0, 1)])
+    def first(i, carry):
+        e = jnp.where(i < 3, i + 1, i + 15)
+        first_sweep(
+            lambda node: [[ue[3 * node + c, e + d] for c in range(3)] for d in (-1, 0, 1)],
+            row_ok(e), e, v1, rest, f0,
+        )
+        return carry
+
+    lax.fori_loop(0, 6, first, 0)
+
+    def pairs_of(e, carry):
         for c in range(3):
-            value = new[c] * row_ok(e)
-            v1[c, e] = value
-            rest[c, e] = more[c]
-            f0[c, e] = flux[c]
-            pair_u[c, e] = paired(ue[c, e])
-            pair_v[c, e] = paired(value)
-        return carry
-
-    lax.fori_loop(1, 21, first, 0)
+            pair_v[c, e] = paired(v1[c, e])
+        return carry
+
+    lax.fori_loop(2, 20, pairs_of, 0)
+    for e in range(2, 20):
+        for c in range(3):
+            ref, x = (before, e) if e < 3 else (field, e - 3) if e < 19 else (after, e - 19)
+            pair_u[c, e] = paired(ref[c, x])
 
     def second(e, carry):
         rows = [[v1[c, e + d] for c in range(3)] for d in (-1, 0, 1)]
@@ -227,18 +277,21 @@
     lax.fori_loop(2, 20, second, 0)
 
 
-def fine_part(place, *arrays):
-    vmem = pl.BlockSpec(memory_space=pltpu.VMEM)
-    kept = pltpu.VMEM((3, 22, 16, 256), f32)
+def fine_part(place, field, before, after, inner):
+    vmem = pl.BlockSpec(memory_space=pltpu.VMEM)
     return pl.pallas_call(
         fine_body,
-        out_shape=[kept] * 6,
-        in_specs=[pl.BlockSpec(memory_space=pltpu.SMEM)] + [vmem] * len(arrays),
+        out_shape=[pltpu.VMEM((3, 22, 16, 256), f32)] * 6,
+        in_specs=[pl.BlockSpec(memory_space=pltpu.SMEM)] + [vmem] * 3 + [pl.BlockSpec(memory_space=pltpu.HBM)] * 3,
         out_specs=[vmem] * 6,
-        scratch_shapes=[pltpu.VMEM((9, 22, 16, 256), f32), kept],
-        compiler_params=pltpu.CompilerParams(vmem_limit_bytes=28 * 2**20),
+        scratch_shapes=[
+            pltpu.VMEM((3, 22, 16, 256), f32),
+            pltpu.VMEM((9, 22, 16, 256), f32),
+            pltpu.SemaphoreType.DMA((3,)),
+        ],
+        compiler_params=pltpu.CompilerParams(vmem_limit_bytes=8 * 2**20),
         name="fine",
-    )(place, *near(*arrays))
+    )(place, *near(field, before, after), *(pltpu.with_memory_space_constraint(a, pltpu.HBM) for a in inner))
 
 
 def strip_body(place, low, high, south, north, strips):
@@ -604,14 +657,15 @@
         after = sent(low_rows, ("gx",), sizes, {"gx": -1})
         before = sent(high_rows, ("gx",), sizes, {"gx": 1})
         field = turned_field(held)
+        inner = inner_part(field)
         low, high = columns(field, before, after)
         south = sent(high, ("gy",), sizes, {"gy": 1})
         north = sent(low, ("gy",), sizes, {"gy": -1})
-        v1, v2, *kept = fine_part(place, field, before, after)
+        v1, f0, pair_u, pair_v, v2, h1 = fine_part(place, field, before, after, inner)
         strips = strip_part(place, low, high, south, north)
         halves_2 = halves_part(v2, strips, 3)
         halves_0 = lax.ppermute(halves_2, ("tz", "ty"), [(i, i + 1) for i in range(15)])
-        sources = sources_part(place, field, strips, v2, *kept)
+        sources = sources_part(place, field, strips, v2, f0, h1, pair_u, pair_v)
         source = lax.all_to_all(sources, group_axes, 0, 0)
         to_right, to_left = pack(source)
         source_left = beside(to_right, 1)

time: 174 us -> 179 us (1.029)
  the two profiles are of different devices: /device:TPU:66 before, /device:TPU:70 now
where the time goes in v7:
time: 179 us; the launch traced here: 178 us
  starting transfers between devices  74.3 us (42%)
  Pallas kernels  41.8 us (23%)
  waiting for transfers between devices  28.7 us (16%)
  blocking collectives  23.6 us (13%)
  local copies, waits for them, and re-layouts  9.28 us (5%)
    all_to_all x1, blocking collectives, per_device(): source = lax.all_to_all(sources, group_axes, 0, 0)  23.6 us
    ppermute x7, starting transfers between devices, sent(): return lax.ppermute(block, axes if len(axes) > 1 else axes[0], pairs)  23.2 us
    all_to_all x1, starting transfers between devices, per_device(): coarse = lax.all_to_all(own, group_axes, 0, 0)  21.7 us
    ppermute x8, starting transfers between devices, beside(): return lax.ppermute(block, pieces, pairs)  21.6 us
    all_to_all x1, waiting for transfers between devices, per_device(): coarse = lax.all_to_all(own, group_axes, 0, 0)  14.3 us
    pallas_call x4, Pallas kernels, stage(): pl.pallas_call(functools.partial(stage_body, begins=not starts, ends=ends...  12.7 us
    ppermute x7, waiting for transfers between devices, sent(): return lax.ppermute(block, axes if len(axes) > 1 else axes[0], pairs)  11.1 us
    unnamed x22, local copies, waits for them, and re-layouts  9.28 us
  transfers between devices with their start and end apart: 17, of which 8 were waited for; matrix products, arithmetic and copies ran while one was open for 0% of the time, Pallas kernels for 10%

profile of v7, /device:TPU:70, one launch (start us, length us, event | category | flops | bytes accessed | tf_op | source)
XLA Modules:
  0.0 178.1 jit_solution(3925875297092246879)
XLA Ops:
  0.0 1.7 edges.1
  1.7 1.8 collective-permute-start
  4.8 1.4 turned.1.field
  6.2 2.6 %collective-permute-done.1.after = f32[9,3,16,256]{3,2,1,0:T(8,128)S(1)} collective-permute-done((f32[9,3,16,256]{3,2,1,0:T(8,128)S(1)}, f32[9,3,16,256]{3,2,1,0:T(8,128)S(1)}, u32[]{:S(2)}, u32[]{:S(2)}) %collective-permute-start.1) | collective-permute-done | bytes 442400 | tf_op jit(solution)/shard_map/ppermute | solution.py:634
  8.9 2.1 %columns.1 = (f32[9,16,384]{2,1,0:T(8,128)S(1)}, f32[9,16,384]{2,1,0:T(8,128)}) custom-call(f32[9,16,16,256]{3,2,1,0:T(8,128)S(1)} %turned.1.field, f32[9,3,16,256]{3,2,1,0:T(8,128)S(1)} %collective-permute-done.before, f32[9,3,16,256]{3,2,1,0:T(8,128)S(1)} %collective-permute-done.1.after), custom_call_target="tpu_custom_call" | custom-call | tf_op jit(solution)/shard_map/columns/pallas_call | solution.py:118
  12.3 5.2 %collective-permute-start.3 = (f32[9,16,384]{2,1,0:T(8,128)S(1)}, f32[9,16,384]{2,1,0:T(8,128)}, u32[]{:S(2)}, u32[]{:S(2)}) collective-permute-start(f32[9,16,384]{2,1,0:T(8,128)S(1)} %get-tuple-element.28.low), channel_id=1, source_target_pairs={{1,0},{2,1},{3,2},{5,4},{6,5},{7,6},{9,8},{10,9},{11,10},{13,12},{... | collective-permute-start | bytes 663560 | tf_op jit(solution)/shard_map/ppermute | solution.py:634
  17.5 2.2 %inner.1 = (f32[3,14,16,256]{3,2,1,0:T(8,128)S(1)}, f32[3,14,16,256]{3,2,1,0:T(8,128)S(1)}, f32[3,14,16,256]{3,2,1,0:T(8,128)S(1)}) custom-call(f32[9,16,16,256]{3,2,1,0:T(8,128)S(1)} %turned.1.field), custom_call_target="tpu_custom_call" | custom-call | tf_op jit(solution)/shard_map/inner/pallas_call | solution.py:212
  22.4 7.2 %fine.1 = (f32[3,22,16,256]{3,2,1,0:T(8,128)S(1)}, f32[3,22,16,256]{3,2,1,0:T(8,128)S(1)}, f32[3,22,16,256]{3,2,1,0:T(8,128)S(1)}, f32[3,22,16,256]{3,2,1,0:T(8,...) custom-call(s32[4]{0:T(128)S(1)} %pad_add_fusion.place, f32[9,16,16,256]{3,2,1,0:T(8,128)S(1)} %turned.1.field, ...), custom_call_target="tpu_custom_call" | custom-call | tf_op jit(solution)/shard_map/fine/pallas_call | solution.py:282
  30.6 2.8 %strip.1.strips = f32[12,6,16,128]{3,2,1,0:T(8,128)S(1)} custom-call(s32[4]{0:T(128)S(1)} %pad_add_fusion.place, f32[9,16,384]{2,1,0:T(8,128)S(1)} %get-tuple-element.28.low, f32[9,16,384]{2,1,0:T(8,128)} %get-tuple-element.29.high, f32[9,16,384]{2,1,0:T(8,128)} %collective-permute-done.2.south, f32[9,16,384]{2,1,0:T(8,128)} %collective-permute-done.3.north), custom_call_target="tpu_custom_call" | custom-call | tf_op jit(solution)/shard_map/strip/pallas_call | solution.py:333
  33.4 4.3 %sources.1 = f32[16,8,1536]{2,1,0:T(8,128)S(1)} custom-call(s32[4]{0:T(128)S(1)} %pad_add_fusion.place, f32[9,16,16,256]{3,2,1,0:T(8,128)S(1)} %turned.1.field, f32[12,6,16,128]{3,2,1,0:T(8,128)S(1)} %strip.1.strips, f32[3,22,16,256]{3,2,1,0:T(8,128)S(1)} %get-tuple-element.33.v2.values, f32[3,22,16,256]{3,2,1,0:T(8,128)S(1)} %get-tuple-element.34.f0, ...), custom_call_target="tpu_custom_call" | custom-call | tf_op jit(solution)/shard_map/sources/pallas_call | solution.py:416
  37.7 23.6 %all_to_all.10.source.rest_0_.rest_3_ = f32[16,8,1536]{2,1,0:T(8,128)S(1)} all-to-all(f32[16,8,1536]{2,1,0:T(8,128)S(1)} %sources.1), channel_id=1, replica_groups=mesh['tz'=4,'ty'=4,'gx'=4,'gy'=4] {'ty','gx'}, dimensions={0} | all-to-all | bytes 1572864 | tf_op jit(solution)/shard_map/all_to_all | solution.py:669
  61.4 1.3 collective-permute-start.4
  62.7 3.1 %collective-permute-start.5 = (f32[8,8,1536]{2,1,0:T(8,128)S(1)}, f32[8,8,1536]{2,1,0:T(8,128)S(1)}, u32[]{:S(2)}, u32[]{:S(2)}) collective-permute-start(f32[8,8,1536]{2,1,0:T(8,128)S(1)} %get-tuple-element.39), channel_id=1, source_target_pairs={{4,0},{8,4},{12,8},{28,12},{24,28},{20,24},{16,20},{32,16},{36,32}... | collective-permute-start | bytes 1179656 | tf_op jit(solution)/shard_map/ppermute | solution.py:648
  65.7 1.3 collective-permute-done.5.rest_2_.rest_5_
  67.0 3.2 %stage.4 = f32[3,8,8,128]{3,2,1,0:T(8,128)S(1)} custom-call(s32[4]{0:T(128)S(1)} %pad_add_fusion.place, f32[16,8,1536]{2,1,0:T(8,128)S(1)} %all_to_all.10.source.rest_0_.rest_3_, f32[8,8,1536]{2,1,0:T(8,128)S(1)} %collective-permute-done.4.rest_1_.rest_4_, f32[8,8,1536]{2,1,0:T(8,128)S(1)} %collective-permute-done.5.rest_2_.rest_5_), custom_call_target="tpu_custom_call" | custom-call | tf_op jit(solution)/shard_map/stage/pallas_call | solution.py:562
  70.2 5.5 %collective-permute-start.6 = (f32[3,8,8,128]{3,2,1,0:T(8,128)S(1)}, f32[3,8,8,128]{3,2,1,0:T(8,128)S(1)}, u32[]{:S(2)}, u32[]{:S(2)}) collective-permute-start(f32[3,8,8,128]{3,2,1,0:T(8,128)S(1)} %stage.4), channel_id=1, source_target_pairs={{0,64},{64,128},{128,192},{1,65},{65,129},{129,193},{2,66},{66,130... | collective-permute-start | bytes 294920 | tf_op jit(solution)/shard_map/ppermute | solution.py:634
  75.7 2.2 %collective-permute-done.6.rest_0_ = f32[3,8,8,128]{3,2,1,0:T(8,128)S(1)} collective-permute-done((f32[3,8,8,128]{3,2,1,0:T(8,128)S(1)}, f32[3,8,8,128]{3,2,1,0:T(8,128)S(1)}, u32[]{:S(2)}, u32[]{:S(2)}) %collective-permute-start.6) | collective-permute-done | bytes 98336 | tf_op jit(solution)/shard_map/ppermute | solution.py:634
  79.2 7.3 %collective-permute-start.8 = (f32[3,8,8,128]{3,2,1,0:T(8,128)S(1)}, f32[3,8,8,128]{3,2,1,0:T(8,128)S(1)}, u32[]{:S(2)}, u32[]{:S(2)}) collective-permute-start(f32[3,8,8,128]{3,2,1,0:T(8,128)S(1)} %collective-permute-done.6.rest_0_), channel_id=1, source_target_pairs={{4,0},{8,4},{12,8},{28,12},{24,28},{20,24},{16,20},{32,16},{36,32}... | collective-permute-start | bytes 294920 | tf_op jit(solution)/shard_map/ppermute | solution.py:648
  87.4 3.2 %stage.5 = f32[3,8,8,128]{3,2,1,0:T(8,128)S(1)} custom-call(s32[4]{0:T(128)S(1)} %pad_add_fusion.place, f32[3,8,8,128]{3,2,1,0:T(8,128)S(1)} %collective-permute-done.6.rest_0_, f32[3,8,8,128]{3,2,1,0:T(8,128)S(1)} %collective-permute-done.7.rest_1_, f32[3,8,8,128]{3,2,1,0:T(8,128)S(1)} %collective-permute-done.8.rest_2_, ...), custom_call_target="tpu_custom_call" | custom-call | tf_op jit(solution)/shard_map/stage/pallas_call | solution.py:562
  90.6 6.2 %collective-permute-start.9 = (f32[3,8,8,128]{3,2,1,0:T(8,128)S(1)}, f32[3,8,8,128]{3,2,1,0:T(8,128)S(1)}, u32[]{:S(2)}, u32[]{:S(2)}) collective-permute-start(f32[3,8,8,128]{3,2,1,0:T(8,128)S(1)} %stage.5), channel_id=1, source_target_pairs={{0,64},{64,128},{128,192},{1,65},{65,129},{129,193},{2,66},{66,130... | collective-permute-start | bytes 294920 | tf_op jit(solution)/shard_map/ppermute | solution.py:634
  96.8 1.8 halves.2.halves_2
  98.6 7.8 %collective-permute-start.15 = (f32[128,768]{1,0:T(8,128)S(1)}, f32[128,768]{1,0:T(8,128)S(1)}, u32[]{:S(2)}, u32[]{:S(2)}) collective-permute-start(f32[128,768]{1,0:T(8,128)S(1)} %halves.2.halves_2), channel_id=1, source_target_pairs={{0,16},{16,32},{32,48},{48,64},{64,80},{80,96},{96,112},{112,128},... | collective-permute-start | bytes 1179656 | tf_op jit(solution)/shard_map/ppermute | solution.py:667
  107.7 3.0 %collective-permute-start.11 = (f32[3,8,8,128]{3,2,1,0:T(8,128)S(1)}, f32[3,8,8,128]{3,2,1,0:T(8,128)S(1)}, u32[]{:S(2)}, u32[]{:S(2)}) collective-permute-start(f32[3,8,8,128]{3,2,1,0:T(8,128)S(1)} %collective-permute-done.9.rest_0_), channel_id=1, source_target_pairs={{4,0},{8,4},{12,8},{28,12},{24,28},{20,24},{16,20},{32,16},{36,32}... | collective-permute-start | bytes 294920 | tf_op jit(solution)/shard_map/ppermute | solution.py:648
  111.7 3.2 %stage.6 = f32[3,8,8,128]{3,2,1,0:T(8,128)S(1)} custom-call(s32[4]{0:T(128)S(1)} %pad_add_fusion.place, f32[3,8,8,128]{3,2,1,0:T(8,128)S(1)} %collective-permute-done.9.rest_0_, f32[3,8,8,128]{3,2,1,0:T(8,128)S(1)} %collective-permute-done.10.rest_1_, f32[3,8,8,128]{3,2,1,0:T(8,128)S(1)} %collective-permute-done.11.rest_2_, ...), custom_call_target="tpu_custom_call" | custom-call | tf_op jit(solution)/shard_map/stage/pallas_call | solution.py:562
  114.8 1.9 %collective-permute-start.12 = (f32[3,8,8,128]{3,2,1,0:T(8,128)S(1)}, f32[3,8,8,128]{3,2,1,0:T(8,128)S(1)}, u32[]{:S(2)}, u32[]{:S(2)}) collective-permute-start(f32[3,8,8,128]{3,2,1,0:T(8,128)S(1)} %stage.6), channel_id=1, source_target_pairs={{0,64},{64,128},{128,192},{1,65},{65,129},{129,193},{2,66},{66,130... | collective-permute-start | bytes 294920 | tf_op jit(solution)/shard_map/ppermute | solution.py:634
  116.8 6.3 %collective-permute-done.12.rest_0_ = f32[3,8,8,128]{3,2,1,0:T(8,128)S(1)} collective-permute-done((f32[3,8,8,128]{3,2,1,0:T(8,128)S(1)}, f32[3,8,8,128]{3,2,1,0:T(8,128)S(1)}, u32[]{:S(2)}, u32[]{:S(2)}) %collective-permute-start.12) | collective-permute-done | bytes 98336 | tf_op jit(solution)/shard_map/ppermute | solution.py:634
  124.3 3.0 %collective-permute-start.14 = (f32[3,8,8,128]{3,2,1,0:T(8,128)S(1)}, f32[3,8,8,128]{3,2,1,0:T(8,128)S(1)}, u32[]{:S(2)}, u32[]{:S(2)}) collective-permute-start(f32[3,8,8,128]{3,2,1,0:T(8,128)S(1)} %collective-permute-done.12.rest_0_), channel_id=1, source_target_pairs={{4,0},{8,4},{12,8},{28,12},{24,28},{20,24},{16,20},{32,16},{36,32}... | collective-permute-start | bytes 294920 | tf_op jit(solution)/shard_map/ppermute | solution.py:648
  128.3 3.2 %stage.7 = f32[16,8,2304]{2,1,0:T(8,128)S(1)} custom-call(s32[4]{0:T(128)S(1)} %pad_add_fusion.place, f32[3,8,8,128]{3,2,1,0:T(8,128)S(1)} %collective-permute-done.12.rest_0_, f32[3,8,8,128]{3,2,1,0:T(8,128)S(1)} %collective-permute-done.13.rest_1_, f32[3,8,8,128]{3,2,1,0:T(8,128)S(1)} %collective-permute-done.14.rest_2_, ...), custom_call_target="tpu_custom_call" | custom-call | tf_op jit(solution)/shard_map/stage/pallas_call | solution.py:562
  132.5 21.7 %all-to-all-start.1 = ((f32[16,8,2304]{2,1,0:T(8,128)}), f32[16,8,2304]{2,1,0:T(8,128)}, u32[]{:S(2)}, u32[]{:S(2)}) async-start(f32[16,8,2304]{2,1,0:T(8,128)} %copy-done.1), calls=%async_computation.1 | async-start | bytes 2359296 | tf_op jit(solution)/shard_map/all_to_all | solution.py:682
  155.5 1.8 halves.3.halves_1
  158.0 14.3 %all-to-all-done.1.coarse = f32[16,8,2304]{2,1,0:T(8,128)} async-done(((f32[16,8,2304]{2,1,0:T(8,128)}), f32[16,8,2304]{2,1,0:T(8,128)}, u32[]{:S(2)}, u32[]{:S(2)}) %all-to-all-start.1) | async-done | bytes 1179680 | tf_op jit(solution)/shard_map/all_to_all | solution.py:682
  174.3 3.8 %finish.1 = f32[288,2,8,128]{3,2,1,0:T(8,128)} custom-call(s32[4]{0:T(128)S(1)} %pad_add_fusion.place, f32[288,2,8,128]{3,2,1,0:T(8,128)S(1)} %bitcast.13, f32[16,8,2304]{2,1,0:T(8,128)} %all-to-all-done.1.coarse, f32[128,768]{1,0:T(8,128)S(1)} %copy-done.10, f32[128,768]{1,0:T(8,128)S(1)} %copy-done.3, f32[128,768]{1,0:T(8,128)S(1)} %halves.2.halves_2), custom_call_target="tpu_custom_call" | custom-call | tf_op jit(solution)/shard_map/finish/pallas_call | solution.py:605
  (41 shorter events, 17.8 us)
Async XLA Ops:
  1.7 4.5 %collective-permute-start = (f32[9,3,16,256]{3,2,1,0:T(8,128)S(1)}, f32[9,3,16,256]{3,2,1,0:T(8,128)S(1)}, u32[]{:S(2)}, u32[]{:S(2)}) collective-permute-start(f32[9,3,16,256]{3,2,1,0:T(8,128)S(1)} %get-tuple-element.26), channel_id=1, source_target_pairs={{0,4},{4,8},{8,12},{1,5},{5,9},{9,13},{2,6},{6,10},{10,14},{3,7},{... | collective-permute-start | bytes 1327112 | tf_op jit(solution)/shard_map/ppermute | solution.py:634
  3.5 5.4 %collective-permute-start.1 = (f32[9,3,16,256]{3,2,1,0:T(8,128)S(1)}, f32[9,3,16,256]{3,2,1,0:T(8,128)S(1)}, u32[]{:S(2)}, u32[]{:S(2)}) collective-permute-start(f32[9,3,16,256]{3,2,1,0:T(8,128)S(1)} %get-tuple-element.27), channel_id=1, source_target_pairs={{4,0},{8,4},{12,8},{5,1},{9,5},{13,9},{6,2},{10,6},{14,10},{7,3},{... | collective-permute-start | bytes 1327112 | tf_op jit(solution)/shard_map/ppermute | solution.py:634
  11.0 19.6 %collective-permute-start.2 = (f32[9,16,384]{2,1,0:T(8,128)}, f32[9,16,384]{2,1,0:T(8,128)}, u32[]{:S(2)}, u32[]{:S(2)}) collective-permute-start(f32[9,16,384]{2,1,0:T(8,128)} %get-tuple-element.29.high), channel_id=1, source_target_pairs={{0,1},{1,2},{2,3},{4,5},{5,6},{6,7},{8,9},{9,10},{10,11},{12,13},{... | collective-permute-start | bytes 663560 | tf_op jit(solution)/shard_map/ppermute | solution.py:634
  12.3 18.3 %collective-permute-start.3 = (f32[9,16,384]{2,1,0:T(8,128)S(1)}, f32[9,16,384]{2,1,0:T(8,128)}, u32[]{:S(2)}, u32[]{:S(2)}) collective-permute-start(f32[9,16,384]{2,1,0:T(8,128)S(1)} %get-tuple-element.28.low), channel_id=1, source_target_pairs={{1,0},{2,1},{3,2},{5,4},{6,5},{7,6},{9,8},{10,9},{11,10},{13,12},{... | collective-permute-start | bytes 663560 | tf_op jit(solution)/shard_map/ppermute | solution.py:634
  19.7 0.8 copy-start.6
  20.6 0.9 copy-start.7
  21.4 0.9 copy-start.8
  29.6 1.0 copy-start.4
  61.4 4.4 %collective-permute-start.4 = (f32[8,8,1536]{2,1,0:T(8,128)S(1)}, f32[8,8,1536]{2,1,0:T(8,128)S(1)}, u32[]{:S(2)}, u32[]{:S(2)}) collective-permute-start(f32[8,8,1536]{2,1,0:T(8,128)S(1)} %get-tuple-element.38), channel_id=1, source_target_pairs={{0,4},{4,8},{8,12},{12,28},{28,24},{24,20},{20,16},{16,32},{32,36}... | collective-permute-start | bytes 1179656 | tf_op jit(solution)/shard_map/ppermute | solution.py:648
  62.7 4.4 %collective-permute-start.5 = (f32[8,8,1536]{2,1,0:T(8,128)S(1)}, f32[8,8,1536]{2,1,0:T(8,128)S(1)}, u32[]{:S(2)}, u32[]{:S(2)}) collective-permute-start(f32[8,8,1536]{2,1,0:T(8,128)S(1)} %get-tuple-element.39), channel_id=1, source_target_pairs={{4,0},{8,4},{12,8},{28,12},{24,28},{20,24},{16,20},{32,16},{36,32}... | collective-permute-start | bytes 1179656 | tf_op jit(solution)/shard_map/ppermute | solution.py:648
  70.2 7.7 %collective-permute-start.6 = (f32[3,8,8,128]{3,2,1,0:T(8,128)S(1)}, f32[3,8,8,128]{3,2,1,0:T(8,128)S(1)}, u32[]{:S(2)}, u32[]{:S(2)}) collective-permute-start(f32[3,8,8,128]{3,2,1,0:T(8,128)S(1)} %stage.4), channel_id=1, source_target_pairs={{0,64},{64,128},{128,192},{1,65},{65,129},{129,193},{2,66},{66,130... | collective-permute-start | bytes 294920 | tf_op jit(solution)/shard_map/ppermute | solution.py:634
  77.9 8.6 %collective-permute-start.7 = (f32[3,8,8,128]{3,2,1,0:T(8,128)S(1)}, f32[3,8,8,128]{3,2,1,0:T(8,128)S(1)}, u32[]{:S(2)}, u32[]{:S(2)}) collective-permute-start(f32[3,8,8,128]{3,2,1,0:T(8,128)S(1)} %collective-permute-done.6.rest_0_), channel_id=1, source_target_pairs={{0,4},{4,8},{8,12},{12,28},{28,24},{24,20},{20,16},{16,32},{32,36}... | collective-permute-start | bytes 294920 | tf_op jit(solution)/shard_map/ppermute | solution.py:648
  79.2 8.3 %collective-permute-start.8 = (f32[3,8,8,128]{3,2,1,0:T(8,128)S(1)}, f32[3,8,8,128]{3,2,1,0:T(8,128)S(1)}, u32[]{:S(2)}, u32[]{:S(2)}) collective-permute-start(f32[3,8,8,128]{3,2,1,0:T(8,128)S(1)} %collective-permute-done.6.rest_0_), channel_id=1, source_target_pairs={{4,0},{8,4},{12,8},{28,12},{24,28},{20,24},{16,20},{32,16},{36,32}... | collective-permute-start | bytes 294920 | tf_op jit(solution)/shard_map/ppermute | solution.py:648
  90.6 15.8 %collective-permute-start.9 = (f32[3,8,8,128]{3,2,1,0:T(8,128)S(1)}, f32[3,8,8,128]{3,2,1,0:T(8,128)S(1)}, u32[]{:S(2)}, u32[]{:S(2)}) collective-permute-start(f32[3,8,8,128]{3,2,1,0:T(8,128)S(1)} %stage.5), channel_id=1, source_target_pairs={{0,64},{64,128},{128,192},{1,65},{65,129},{129,193},{2,66},{66,130... | collective-permute-start | bytes 294920 | tf_op jit(solution)/shard_map/ppermute | solution.py:634
  98.6 28.8 %collective-permute-start.15 = (f32[128,768]{1,0:T(8,128)S(1)}, f32[128,768]{1,0:T(8,128)S(1)}, u32[]{:S(2)}, u32[]{:S(2)}) collective-permute-start(f32[128,768]{1,0:T(8,128)S(1)} %halves.2.halves_2), channel_id=1, source_target_pairs={{0,16},{16,32},{32,48},{48,64},{64,80},{80,96},{96,112},{112,128},... | collective-permute-start | bytes 1179656 | tf_op jit(solution)/shard_map/ppermute | solution.py:667
  106.4 4.3 %collective-permute-start.10 = (f32[3,8,8,128]{3,2,1,0:T(8,128)S(1)}, f32[3,8,8,128]{3,2,1,0:T(8,128)S(1)}, u32[]{:S(2)}, u32[]{:S(2)}) collective-permute-start(f32[3,8,8,128]{3,2,1,0:T(8,128)S(1)} %collective-permute-done.9.rest_0_), channel_id=1, source_target_pairs={{0,4},{4,8},{8,12},{12,28},{28,24},{24,20},{20,16},{16,32},{32,36}... | collective-permute-start | bytes 294920 | tf_op jit(solution)/shard_map/ppermute | solution.py:648
  107.7 4.0 %collective-permute-start.11 = (f32[3,8,8,128]{3,2,1,0:T(8,128)S(1)}, f32[3,8,8,128]{3,2,1,0:T(8,128)S(1)}, u32[]{:S(2)}, u32[]{:S(2)}) collective-permute-start(f32[3,8,8,128]{3,2,1,0:T(8,128)S(1)} %collective-permute-done.9.rest_0_), channel_id=1, source_target_pairs={{4,0},{8,4},{12,8},{28,12},{24,28},{20,24},{16,20},{32,16},{36,32}... | collective-permute-start | bytes 294920 | tf_op jit(solution)/shard_map/ppermute | solution.py:648
  114.8 8.2 %collective-permute-start.12 = (f32[3,8,8,128]{3,2,1,0:T(8,128)S(1)}, f32[3,8,8,128]{3,2,1,0:T(8,128)S(1)}, u32[]{:S(2)}, u32[]{:S(2)}) collective-permute-start(f32[3,8,8,128]{3,2,1,0:T(8,128)S(1)} %stage.6), channel_id=1, source_target_pairs={{0,64},{64,128},{128,192},{1,65},{65,129},{129,193},{2,66},{66,130... | collective-permute-start | bytes 294920 | tf_op jit(solution)/shard_map/ppermute | solution.py:634
  123.1 5.1 %collective-permute-start.13 = (f32[3,8,8,128]{3,2,1,0:T(8,128)S(1)}, f32[3,8,8,128]{3,2,1,0:T(8,128)S(1)}, u32[]{:S(2)}, u32[]{:S(2)}) collective-permute-start(f32[3,8,8,128]{3,2,1,0:T(8,128)S(1)} %collective-permute-done.12.rest_0_), channel_id=1, source_target_pairs={{0,4},{4,8},{8,12},{12,28},{28,24},{24,20},{20,16},{16,32},{32,36}... | collective-permute-start | bytes 294920 | tf_op jit(solution)/shard_map/ppermute | solution.py:648
  124.3 4.0 %collective-permute-start.14 = (f32[3,8,8,128]{3,2,1,0:T(8,128)S(1)}, f32[3,8,8,128]{3,2,1,0:T(8,128)S(1)}, u32[]{:S(2)}, u32[]{:S(2)}) collective-permute-start(f32[3,8,8,128]{3,2,1,0:T(8,128)S(1)} %collective-permute-done.12.rest_0_), channel_id=1, source_target_pairs={{4,0},{8,4},{12,8},{28,12},{24,28},{20,24},{16,20},{32,16},{36,32}... | collective-permute-start | bytes 294920 | tf_op jit(solution)/shard_map/ppermute | solution.py:648
  127.4 0.8 copy-start.9
  131.5 1.0 copy-start.1
  132.5 39.8 %copy-start = (f32[1,3,3,16,16,256]{5,4,3,2,1,0:T(8,128)S(1)}, f32[1,3,3,16,16,256]{5,4,3,2,1,0:T(8,128)}, u32[]{:S(2)}) copy-start(f32[1,3,3,16,16,256]{5,4,3,2,1,0:T(8,128)} %param.1) | copy-start | bytes 7077892
  132.5 39.8 %all-to-all-start.1 = ((f32[16,8,2304]{2,1,0:T(8,128)}), f32[16,8,2304]{2,1,0:T(8,128)}, u32[]{:S(2)}, u32[]{:S(2)}) async-start(f32[16,8,2304]{2,1,0:T(8,128)} %copy-done.1), calls=%async_computation.1 | async-start | bytes 2359296 | tf_op jit(solution)/shard_map/all_to_all | solution.py:682
  154.2 1.2 copy-start.5
  157.2 0.7 copy-start.2
  172.3 1.0 copy-start.3
  173.3 1.0 copy-start.10
